TPU v7x, 256 devices: a whole 4x4x8 slice. The times are simulated.
256 devices in a mesh: tmpl: 32 (over x, z_lo, core), tm: 8 (over y, z_hi).
Axes of the slice: x: 4, y: 4, z: 8 (z_hi: 2, z_lo: 4; z = z_hi * 4 + z_lo), core: 2. Of those that a mesh axis runs over, the one named last changes fastest.
Arguments:
- records: bfloat16 [1536, 4096], P('tmpl', 'tm'), may hold values from -6 to 6
- templates: bfloat16 [2, 1024, 48, 200], P(None, 'tmpl'), may hold values from -0.0625 to 0.0625
- channels: int32 [2, 1024, 48], P(None, 'tmpl'), may hold values from 0 to 1535
- moveouts: int32 [2, 1024, 48], P(None, 'tmpl'), may hold values from 0 to 55
Outputs:
- detections: float32 [2, 1024, 4096], P(None, 'tmpl', 'tm')
All inputs are finite; a program needn't handle non-finite values.
Results may differ from a plain program's by a relative error of at most 0.0043.
Values may be sent and summed in bfloat16 or wider, within the bound.
No kernel may reach another device: no remote copies, remote signals or barrier semaphores. Data moves between devices by JAX's collectives and lax.ppermute only.
A program may use at most 64 MiB of HBM per device.

v0:
```python
import math

import jax
import jax.numpy as jnp
from jax import lax
from jax.sharding import PartitionSpec as P

L = 200
LAGS = 56


def from_behind(block, axis, distance):
    devices = range(lax.axis_size(axis))
    route = [(i - distance, i) for i in devices if i - distance in devices]
    return lax.ppermute(block, axis, route)


def tables(count, freqs, width):
    sample = jnp.arange(count, dtype=jnp.int32)[:, None]
    freq = jnp.arange(freqs, dtype=jnp.int32)[None, :]
    angle = 2.0 * math.pi / width * (sample * freq % width).astype(jnp.float32)
    return jnp.concatenate([jnp.cos(angle), jnp.sin(angle)], axis=1)


def detect(waves, chans, lags, spectra, forward, inverse, weight, freq, width, freqs):
    count = waves.shape[0]
    hspec = jnp.dot(
        waves.reshape(-1, waves.shape[2]),
        forward[: waves.shape[2]],
        preferred_element_type=jnp.float32,
    )
    h_cos, h_sin = (hspec[:, :freqs], hspec[:, freqs:])
    angle = (
        2.0
        * math.pi
        / width
        * (lags.reshape(-1)[:, None] * freq[None, :] % width).astype(jnp.float32)
    )
    c_theta, s_theta = (jnp.cos(angle), jnp.sin(angle))
    picked = spectra[chans.reshape(-1)].astype(jnp.float32)
    x_cos, x_sin = (picked[:, :freqs], picked[:, freqs:])
    prod_a = h_cos * x_cos + h_sin * x_sin
    prod_b = h_sin * x_cos - h_cos * x_sin
    real_part = (prod_a * c_theta - prod_b * s_theta).reshape(count, -1, freqs).sum(axis=1)
    imag_part = (prod_a * s_theta + prod_b * c_theta).reshape(count, -1, freqs).sum(axis=1)
    joint = jnp.concatenate([real_part * weight, -imag_part * weight], axis=1)
    return lax.dot_general(
        joint, inverse, (((1,), (1,)), ((), ())), precision=lax.Precision.HIGHEST
    )


def per_device(records, templates, channels, moveouts):
    time_dev = records.shape[1]
    extra = L + LAGS - 2
    width = time_dev + extra
    freqs = width // 2 + 1
    forward = tables(width, freqs, width).astype(jnp.bfloat16)
    inverse = tables(time_dev, freqs, width)
    freq = jnp.arange(freqs, dtype=jnp.int32)
    weight = jnp.where((freq == 0) | (freq == freqs - 1), 1.0, 2.0).astype(jnp.float32) / width
    rim = from_behind(records[:, :extra], "tm", -1)
    window = jnp.concatenate([records, rim], axis=1)
    spectra = jnp.dot(
        lax.all_gather(window, "tmpl", axis=0, tiled=True),
        forward,
        preferred_element_type=jnp.float32,
    ).astype(jnp.bfloat16)
    results = []
    for batch in range(templates.shape[0]):
        results.append(
            detect(
                templates[batch],
                channels[batch],
                moveouts[batch],
                spectra,
                forward,
                inverse,
                weight,
                freq,
                width,
                freqs,
            )
        )
    return jnp.stack(results)


def solution(mesh):
    placed = (
        P("tmpl", "tm"),
        P(None, "tmpl", None, None),
        P(None, "tmpl", None),
        P(None, "tmpl", None),
    )
    return jax.shard_map(
        per_device, mesh=mesh, in_specs=placed, out_specs=P(None, "tmpl", "tm"), check_vma=False
    )
```

profile of v0, /device:TPU:1, one launch (start us, length us, event | category | flops | bytes accessed | tf_op | source)
XLA Modules:
  0.0 185.4 jit_solution(2177436032640914762)
XLA Ops:
  6.5 0.7 slice.52
  7.3 1.4 collective-permute-start
  8.7 9.6 %collective-permute-done = bf16[48,254]{1,0:T(8,128)(2,1)S(1)} collective-permute-done((bf16[48,254]{1,0:T(8,128)(2,1)S(1)}, bf16[48,254]{1,0:T(8,128)(2,1)S(1)}, u32[]{:S(2)}, u32[]{:S(2)}) %collective-permute-start) | collective-permute-done | bytes 24416 | tf_op jit(solution)/shard_map/ppermute | solution.py:15
  18.3 1.4 pad_maximum_fusion.9
  19.7 0.7 fusion.46
  20.5 0.7 fusion.47
  21.6 5.0 %sine_convert_fusion = (bf16[766,384]{1,0:T(8,128)(2,1)S(1)}, bf16[766,384]{1,0:T(8,128)(2,1)S(1)}) fusion(), kind=kLoop, calls=%fused_computation.41 | loop fusion | flops 3235584 | bytes 1176576 | tf_op jit(solution)/shard_map/convert.1
  26.7 0.8 copy-done.3
  27.7 4.2 %fusion.30 = (f32[512,384]{1,0:T(8,128)S(1)}, f32[512,384]{1,0:T(8,128)}) fusion(), kind=kLoop, calls=%fused_computation.54 | loop fusion | flops 1769472 | bytes 1572864 | tf_op jit(solution)/shard_map/sin | solution.py:22
  32.1 3.0 %convolution_bitcast_fusion = f32[1536,768]{0,1:T(8,128)} fusion(bf16[200,768]{1,0:T(8,128)(2,1)S(1)} %pad_maximum_fusion.7, bf16[1536,200]{1,0:T(8,128)(2,1)S(1)} %bitcast.24), kind=kOutput, calls=%fused_computation.2 | convolution fusion | flops 471859200 | bytes 5640192 | tf_op jit(solution)/shard_map/dot_general | solution.py:27
  35.1 3.0 %convolution_bitcast_fusion.1 = f32[1536,768]{0,1:T(8,128)} fusion(bf16[200,768]{1,0:T(8,128)(2,1)S(1)} %pad_maximum_fusion.7, bf16[1536,200]{1,0:T(8,128)(2,1)S(1)} %bitcast.23), kind=kOutput, calls=%fused_computation.3 | convolution fusion | flops 471859200 | bytes 5640192 | tf_op jit(solution)/shard_map/dot_general | solution.py:27
  38.0 46.4 %all-gather.2.cloned.1.call-done = bf16[1536,766]{1,0:T(8,128)(2,1)} async-done(((bf16[48,766]{1,0:T(8,128)(2,1)}), bf16[1536,766]{1,0:T(8,128)(2,1)}) %all-gather.2.cloned.1.call-update) | async-done | bytes 2353168 | tf_op jit(solution)/shard_map/all_gather | solution.py:64
  84.4 4.0 %convolution_convert_fusion = bf16[1536,768]{1,0:T(8,128)(2,1)S(1)} fusion(bf16[1536,766]{1,0:T(8,128)(2,1)} %all-gather.2.cloned.1.call-done, bf16[766,384]{1,0:T(8,128)(2,1)} %copy-done.3, bf16[766,384]{1,0:T(8,128)(2,1)} %copy-done.4), kind=kOutput, calls=%fused_computation.6 | convolution fusion | flops 1810753536 | bytes 5889024 | tf_op jit(solution)/shard_map/dot_general | solution.py:63
  88.4 5.7 %gather_fusion.1 = bf16[1536,768]{1,0:T(8,128)(2,1)} fusion(bf16[1536,768]{1,0:T(8,128)(2,1)S(1)} %convolution_convert_fusion, s32[2048]{0:T(1024)S(1)} %pad_clamp_fusion), kind=kCustom, calls=%fused_computation.1 | custom fusion | bytes 4724736 | tf_op jit(solution)/shard_map/gather | solution.py:40
  94.1 4.3 %copy.10 = bf16[1536,768]{0,1:T(8,128)(2,1)} copy(bf16[1536,768]{1,0:T(8,128)(2,1)} %gather_fusion.1) | data formatting | bytes 4718592 | tf_op jit(solution)/shard_map/gather | solution.py:40
  98.3 2.3 %convert_element_type.31 = f32[1536,768]{0,1:T(8,128)S(1)} convert(bf16[1536,768]{0,1:T(8,128)(2,1)} %copy.10) | non-fusion elementwise | flops 1179648 | bytes 7077888 | tf_op jit(solution)/shard_map/convert_element_type | solution.py:40
  100.6 13.5 %multiply_subtract_fusion = (f32[1536,384]{0,1:T(8,128)}, f32[1536,384]{0,1:T(8,128)S(1)}, f32[1536,384]{0,1:T(8,128)S(1)}) fusion(s32[1536]{0:T(1024)S(1)} %mul.198, f32[1536,768]{0,1:T(8,128)S(1)} %convert_element_type.31, f32[1536,768]{0,1:T(8,128)} %convolution_bitcast_fusion), kind=kLoop, calls=%fused_computation.12 | loop fusion | flops 10616832 | bytes 16521216 | tf_op jit(solution)/shard_map/sub | solution.py:44
  114.1 10.8 %multiply_add_fusion = f32[1536,384]{0,1:T(8,128)} fusion(f32[1536,384]{0,1:T(8,128)S(1)} %get-tuple-element.10, f32[1536,384]{0,1:T(8,128)S(1)} %get-tuple-element.9, s32[1536]{0:T(1024)S(1)} %mul.198), kind=kLoop, calls=%fused_computation.11 | loop fusion | flops 7077888 | bytes 7084032 | tf_op jit(solution)/shard_map/add | solution.py:45
  124.9 3.1 %copy.12 = f32[1536,384]{1,0:T(8,128)} copy(f32[1536,384]{0,1:T(8,128)} %multiply_add_fusion) | data formatting | bytes 4718592 | tf_op jit(solution)/shard_map/add | solution.py:45
  128.1 5.7 %gather_fusion = bf16[1536,768]{1,0:T(8,128)(2,1)} fusion(bf16[1536,768]{1,0:T(8,128)(2,1)S(1)} %convolution_convert_fusion, s32[2048]{0:T(1024)S(1)} %pad_clamp_fusion.1), kind=kCustom, calls=%fused_computation | custom fusion | bytes 4724736 | tf_op jit(solution)/shard_map/gather | solution.py:40
  133.7 2.8 %copy.7 = bf16[1536,768]{0,1:T(8,128)(2,1)S(1)} copy(bf16[1536,768]{1,0:T(8,128)(2,1)} %gather_fusion) | data formatting | bytes 4718592 | tf_op jit(solution)/shard_map/gather | solution.py:40
  137.2 13.5 %multiply_subtract_fusion.2 = (f32[1536,384]{0,1:T(8,128)}, f32[1536,384]{0,1:T(8,128)S(1)}, f32[1536,384]{0,1:T(8,128)S(1)}) fusion(s32[1536]{0:T(1024)S(1)} %mul.177, f32[1536,768]{0,1:T(8,128)S(1)} %convert_element_type.28, f32[1536,768]{0,1:T(8,128)} %convolution_bitcast_fusion.1), kind=kLoop, calls=%fused_computation.21 | loop fusion | flops 10616832 | bytes 16521216 | tf_op jit(solution)/shard_map/sub | solution.py:44
  150.7 9.9 %multiply_add_fusion.2 = f32[1536,384]{0,1:T(8,128)S(1)} fusion(f32[1536,384]{0,1:T(8,128)S(1)} %get-tuple-element.7, f32[1536,384]{0,1:T(8,128)S(1)} %get-tuple-element.6, s32[1536]{0:T(1024)S(1)} %mul.177), kind=kLoop, calls=%fused_computation.20 | loop fusion | flops 7077888 | bytes 7084032 | tf_op jit(solution)/shard_map/add | solution.py:45
  160.6 2.0 %copy.9 = f32[1536,384]{1,0:T(8,128)} copy(f32[1536,384]{0,1:T(8,128)S(1)} %multiply_add_fusion.2) | data formatting | bytes 4718592 | tf_op jit(solution)/shard_map/add | solution.py:45
  162.6 2.0 %reduce_sum.39 = f32[32,384]{1,0:T(8,128)S(1)} reduce(f32[32,48,384]{2,1,0:T(8,128)} %bitcast.19, f32[]{:T(128)} %constant.26.clone.1), dimensions={1}, to_apply=%region_3.4 | reduce | flops 577536 | bytes 2408452 | tf_op jit(solution)/shard_map/reduce_sum | solution.py:45
  164.6 1.9 %reduce_sum.37 = f32[32,384]{1,0:T(8,128)S(1)} reduce(f32[32,48,384]{2,1,0:T(8,128)} %bitcast.20, f32[]{:T(128)} %constant.26.clone.1), dimensions={1}, to_apply=%region_1.2 | reduce | flops 577536 | bytes 2408452 | tf_op jit(solution)/shard_map/reduce_sum | solution.py:45
  166.5 2.0 %copy.11 = f32[1536,384]{1,0:T(8,128)} copy(f32[1536,384]{0,1:T(8,128)S(1)} %copy-done) | data formatting | bytes 4718592 | tf_op jit(solution)/shard_map/sub | solution.py:44
  168.5 2.0 %reduce_sum.38 = f32[32,384]{1,0:T(8,128)S(1)} reduce(f32[32,48,384]{2,1,0:T(8,128)} %bitcast.22, f32[]{:T(128)} %constant.26.clone.1), dimensions={1}, to_apply=%region_2.3 | reduce | flops 577536 | bytes 2408452 | tf_op jit(solution)/shard_map/reduce_sum | solution.py:44
  170.8 2.0 %copy.8 = f32[1536,384]{1,0:T(8,128)} copy(f32[1536,384]{0,1:T(8,128)S(1)} %copy-done.1) | data formatting | bytes 4718592 | tf_op jit(solution)/shard_map/sub | solution.py:44
  172.8 1.9 %reduce_sum.36 = f32[32,384]{1,0:T(8,128)S(1)} reduce(f32[32,48,384]{2,1,0:T(8,128)} %bitcast.21, f32[]{:T(128)} %constant.26.clone.1), dimensions={1}, to_apply=%region_0.1 | reduce | flops 577536 | bytes 2408452 | tf_op jit(solution)/shard_map/reduce_sum | solution.py:44
  174.8 1.5 fusion.24
  176.3 1.5 fusion.25
  (27 shorter events, 2.5 us)
Async XLA Ops:
  6.5 77.9 %all-gather.2.cloned.1.call-start = ((), (), s32[]{:S(2)}) async-start(), calls=%async_computation | async-start | bytes 2433024 | tf_op jit(solution)/shard_map/all_gather | solution.py:64
  7.3 24.7 %copy-start.5 = (bf16[2,32,48,200]{3,2,1,0:T(8,128)(2,1)S(1)}, bf16[2,32,48,200]{3,2,1,0:T(8,128)(2,1)}, u32[]{:S(2)}) copy-start(bf16[2,32,48,200]{3,2,1,0:T(8,128)(2,1)} %param.5) | copy-start | bytes 3686404
  7.3 11.0 %collective-permute-start = (bf16[48,254]{1,0:T(8,128)(2,1)S(1)}, bf16[48,254]{1,0:T(8,128)(2,1)S(1)}, u32[]{:S(2)}, u32[]{:S(2)}) collective-permute-start(bf16[48,254]{1,0:T(8,128)(2,1)S(1)} %slice.52), channel_id=1, source_target_pairs={{1,0},{2,1},{3,2},{4,3},{5,4},{6,5},{7,6},{9,8},{10,9},{11,10},{12... | collective-permute-start | bytes 73160 | tf_op jit(solution)/shard_map/ppermute | solution.py:15
  26.6 0.8 copy-start.3
  26.6 1.1 copy-start.4
  162.6 3.9 %copy-start = (f32[1536,384]{0,1:T(8,128)S(1)}, f32[1536,384]{0,1:T(8,128)}, u32[]{:S(2)}) copy-start(f32[1536,384]{0,1:T(8,128)} %get-tuple-element.8) | copy-start | bytes 7077892
  168.5 2.4 %copy-start.1 = (f32[1536,384]{0,1:T(8,128)S(1)}, f32[1536,384]{0,1:T(8,128)}, u32[]{:S(2)}) copy-start(f32[1536,384]{0,1:T(8,128)} %get-tuple-element.5) | copy-start | bytes 7077892
  172.8 2.0 %copy-start.2 = (f32[512,384]{1,0:T(8,128)S(1)}, f32[512,384]{1,0:T(8,128)}, u32[]{:S(2)}) copy-start(f32[512,384]{1,0:T(8,128)} %get-tuple-element.24) | copy-start | bytes 2359300
Sparse Core Ops, SparseCore 0:
  19.8 64.5 all-gather.1
where the time goes:
time: 186 us; the launch traced here: 185 us
  other arithmetic  69.9 us (38%)
  waiting for transfers between devices  56 us (30%)
  local copies, waits for them, and re-layouts  31.5 us (17%)
  between operations  13.6 us (7%)
  matrix products  13 us (7%)
    all_gather x1, waiting for transfers between devices, per_device(): lax.all_gather(window, 'tmpl', axis=0, tiled=True)  46.4 us
    sub x2, other arithmetic, detect(): prod_a * c_theta - prod_b * s_theta  27.1 us
    add x2, other arithmetic, detect(): prod_a * s_theta + prod_b * c_theta  20.6 us
    gather x4, local copies, waits for them, and re-layouts, detect(): picked = spectra[chans.reshape(-1)].astype(jnp.float32)  18.4 us
    ppermute x1, waiting for transfers between devices, from_behind(): return lax.ppermute(block, axis, route)  9.56 us
    dot_general x2, matrix products, detect(): jnp.dot(waves.reshape(-1, waves.shape[2]), forward[:waves.shape[2]], pref...  5.98 us
    add x2, local copies, waits for them, and re-layouts, detect(): prod_a * s_theta + prod_b * c_theta  5.11 us
    another operation x1, other arithmetic  5 us
  transfers between devices with their start and end apart: 2, of which 2 were waited for; matrix products, arithmetic and copies ran while one was open for 9% of the time, Pallas kernels for 0%

commit v1 on v0

v1 whole, which is shorter than its diff:
```python
import functools
import math

import jax
import jax.numpy as jnp
import numpy as np
from jax import lax
from jax.experimental import pallas as pl
from jax.experimental.pallas import tpu as pltpu
from jax.sharding import PartitionSpec as P

L = 200
LAGS = 56
EXTRA = L + LAGS - 2
HOLD = 128


def angles(samples, freqs, width):
    return 2.0 * math.pi / width * (samples[:, None] * freqs[None, :] % width)


def host_tables(time_dev):
    width = time_dev + EXTRA
    freqs = width // 2 + 1
    freq = np.arange(freqs)
    ang = angles(np.arange(time_dev), freq, width)
    forward = np.concatenate([np.cos(ang), np.sin(ang)], axis=1).astype(np.float32).astype(jnp.bfloat16)
    turn = angles(np.arange(LAGS), freq, width)
    cos, sin = (f(turn).reshape(LAGS, freqs // HOLD, HOLD) for f in (np.cos, np.sin))
    phase = np.zeros((LAGS, 16, HOLD), np.float32)
    phase[:, 0:3], phase[:, 4:7] = cos, cos
    phase[:, 8:11], phase[:, 12:15] = -sin, sin
    weight = np.where((freq == 0) | (freq == freqs - 1), 1.0, 2.0) / width
    early = np.arange(time_dev // 2, time_dev) + EXTRA
    tau = np.concatenate([np.arange(time_dev), early])
    back = angles(tau, freq, width)
    inverse = np.concatenate([np.cos(back) * weight, np.sin(back) * weight], axis=1)
    inverse[time_dev:][early < time_dev] = 0.0
    inverse = inverse.T.astype(np.float32)
    high = inverse.astype(jnp.bfloat16)
    low = (inverse - high.astype(np.float32)).astype(jnp.bfloat16)
    return forward, phase.reshape(LAGS * 16, HOLD), high, low


def template_kernel(rows, freqs, lag_ref, wave_ref, forward_ref, phase_ref, out_ref, spec, swap):
    chunks = freqs // HOLD

    @pl.when(pl.program_id(0) == 0)
    def _():
        for pad in (chunks, 4 + chunks):
            spec[pl.ds(pad, rows, stride=8), :] = jnp.zeros((rows, HOLD), jnp.float32)
            swap[pl.ds(pad, rows, stride=8), :] = jnp.zeros((rows, HOLD), jnp.float32)

    dft = jnp.dot(wave_ref[...], forward_ref[...], preferred_element_type=jnp.float32)
    for j in range(chunks):
        real = dft[:, j * HOLD : (j + 1) * HOLD]
        imag = dft[:, freqs + j * HOLD : freqs + (j + 1) * HOLD]
        spec[pl.ds(j, rows, stride=8), :] = real
        spec[pl.ds(4 + j, rows, stride=8), :] = imag
        swap[pl.ds(j, rows, stride=8), :] = imag
        swap[pl.ds(4 + j, rows, stride=8), :] = real
    base = pl.program_id(0) * rows

    def group(g, carry):
        for u in range(8):
            row = g * 8 + u
            lag = pl.multiple_of(lag_ref[base + row], 16)
            at = pl.ds(pl.multiple_of(row * 8, 8), 8)
            out_ref[at, :] = spec[at, :] * phase_ref[pl.ds(lag, 8), :] + swap[at, :] * phase_ref[pl.ds(lag + 8, 8), :]
        return carry

    lax.fori_loop(0, rows // 8, group, 0)


def template_spectra(waves, lags, forward, phase, freqs, rows):
    count, length = waves.shape
    grid = pltpu.PrefetchScalarGridSpec(
        num_scalar_prefetch=1,
        grid=(count // rows,),
        in_specs=[
            pl.BlockSpec((rows, length), lambda i, lag: (i, 0)),
            pl.BlockSpec((length, 2 * freqs), lambda i, lag: (0, 0)),
            pl.BlockSpec(phase.shape, lambda i, lag: (0, 0)),
        ],
        out_specs=pl.BlockSpec((rows * 8, HOLD), lambda i, lag: (i, 0)),
        scratch_shapes=[pltpu.VMEM((rows * 8, HOLD), jnp.float32)] * 2,
    )
    return pl.pallas_call(
        functools.partial(template_kernel, rows, freqs),
        grid_spec=grid,
        out_shape=jax.ShapeDtypeStruct((count * 8, HOLD), jnp.float32),
        compiler_params=pltpu.CompilerParams(vmem_limit_bytes=20 << 20),
        cost_estimate=pl.CostEstimate(flops=count * length * freqs * 4, bytes_accessed=count * 8 * HOLD * 4, transcendentals=0),
        name="template_spectra",
    )(lags, waves, forward[:length], phase)


def detect_kernel(n_blocks, count, stations, freqs, groups, slot_ref, *refs):
    blocks, (forward_ref, high_ref, low_ref, q_hbm, main_ref, early_ref, table, q, acc, sems) = refs[:n_blocks], refs[n_blocks:]
    chunks = freqs // HOLD
    share = count // groups
    span = share * stations * 8
    loads = [pltpu.make_async_copy(q_hbm.at[pl.ds(g * span, span)], q.at[pl.ds(g * span, span)], sems.at[g]) for g in range(groups)]
    for load in loads:
        load.start()
    size = blocks[0].shape[0]
    for b, block in enumerate(blocks):
        dft = jnp.dot(block[...], forward_ref[...], preferred_element_type=jnp.float32)
        for j in range(chunks):
            real = dft[:, j * HOLD : (j + 1) * HOLD]
            imag = dft[:, freqs + j * HOLD : freqs + (j + 1) * HOLD]
            start = b * size * 16
            table[pl.ds(start + j, size, stride=16), :] = real
            table[pl.ds(start + 4 + j, size, stride=16), :] = imag
            table[pl.ds(start + 8 + j, size, stride=16), :] = imag
            table[pl.ds(start + 12 + j, size, stride=16), :] = -real

    def one(t, carry):
        first = second = jnp.zeros((8, HOLD), jnp.float32)
        for k in range(stations):
            row = t * stations + k
            slot = pl.multiple_of(slot_ref[row], 16)
            weight = q[pl.ds(pl.multiple_of(row * 8, 8), 8), :]
            first += weight * table[pl.ds(slot, 8), :]
            second += weight * table[pl.ds(slot + 8, 8), :]
        acc[pl.ds(pl.multiple_of(t * 16, 16), 8), :] = first
        acc[pl.ds(pl.multiple_of(t * 16 + 8, 8), 8), :] = second
        return carry

    for g, load in enumerate(loads):
        load.wait()
        lax.fori_loop(g * share, (g + 1) * share, one, 0)
    joint = jnp.concatenate(
        [
            acc[pl.ds(8 * part + j, count, stride=16), :] + acc[pl.ds(8 * part + 4 + j, count, stride=16), :]
            for part in range(2)
            for j in range(chunks)
        ],
        axis=1,
    )
    top = joint.astype(jnp.bfloat16)
    rest = (joint - top.astype(jnp.float32)).astype(jnp.bfloat16)
    out = (
        jnp.dot(top, high_ref[...], preferred_element_type=jnp.float32)
        + jnp.dot(rest, high_ref[...], preferred_element_type=jnp.float32)
        + jnp.dot(top, low_ref[...], preferred_element_type=jnp.float32)
    )
    time_dev = main_ref.shape[1]
    main_ref[...] = out[:, :time_dev]
    early_ref[...] = out[:, time_dev:]


def detect(slots, blocks, forward, high, low, q, count, stations, freqs, time_dev):
    groups = 8
    rows = sum(b.shape[0] for b in blocks)
    whole = pl.BlockSpec(memory_space=pltpu.VMEM)
    return pl.pallas_call(
        functools.partial(detect_kernel, len(blocks), count, stations, freqs, groups),
        in_specs=[pl.BlockSpec(memory_space=pltpu.SMEM)] + [whole] * (len(blocks) + 3) + [pl.BlockSpec(memory_space=pl.ANY)],
        out_specs=[whole, whole],
        out_shape=[
            jax.ShapeDtypeStruct((count, time_dev), jnp.float32),
            jax.ShapeDtypeStruct((count, time_dev // 2), jnp.float32),
        ],
        scratch_shapes=[
            pltpu.VMEM((rows * 16, HOLD), jnp.float32),
            pltpu.VMEM((count * stations * 8, HOLD), jnp.float32),
            pltpu.VMEM((count * 16, HOLD), jnp.float32),
            pltpu.SemaphoreType.DMA((groups,)),
        ],
        compiler_params=pltpu.CompilerParams(vmem_limit_bytes=40 << 20),
        cost_estimate=pl.CostEstimate(flops=rows * time_dev * freqs * 4, bytes_accessed=count * stations * 8 * HOLD * 4, transcendentals=0),
        name="detect",
    )(slots, *blocks, forward, high, low, q)


def route(change):
    dx, dz, dc = change
    code = (dx * 4 + dz) * 2 + dc
    return [(i, i ^ code) for i in range(32)]


def per_device(records, templates, channels, moveouts):
    per, time_dev = records.shape
    batches, count, stations, length = templates.shape
    freqs = (time_dev + EXTRA) // 2 + 1
    forward, phase, high, low = (jnp.asarray(t) for t in host_tables(time_dev))
    swap = lambda block, change: lax.ppermute(block, "tmpl", route(change))

    line = jnp.concatenate([records] + [swap(records, (0, d, 0)) for d in (1, 2, 3)], axis=0)
    plane = [line] + [swap(line, (d, 0, 0)) for d in (1, 2, 3)]
    blocks = plane + [swap(block, (0, 0, 1)) for block in plane]

    apart = (channels // per) ^ lax.axis_index("tmpl")
    place = ((apart & 1) * 16 + (apart >> 1)) * per + channels % per
    slots = (place * 16).reshape(-1)

    q = template_spectra(
        templates.reshape(-1, length), (moveouts * 16).reshape(-1), forward, phase, freqs, 384
    )
    main, early = detect(slots, blocks, forward, high, low, q, batches * count, stations, freqs, time_dev)
    earlier = lax.ppermute(early, "tm", [(i, i - 1) for i in range(1, lax.axis_size("tm"))])
    out = main + jnp.pad(earlier, ((0, 0), (time_dev - earlier.shape[1], 0)))
    return out.reshape(batches, count, time_dev)


def solution(mesh):
    placed = (
        P("tmpl", "tm"),
        P(None, "tmpl", None, None),
        P(None, "tmpl", None),
        P(None, "tmpl", None),
    )
    return jax.shard_map(
        per_device, mesh=mesh, in_specs=placed, out_specs=P(None, "tmpl", "tm"), check_vma=False
    )
```

time: 186 us -> 64.4 us (0.35)
  other arithmetic: 69.9 us -> 2.23 us
  waiting for transfers between devices: 56 us -> 14.9 us
  local copies, waits for them, and re-layouts: 31.5 us -> 8.96 us
  Pallas kernels: 0 us -> 21.4 us
  starting transfers between devices: 1.41 us -> 16.2 us
  between operations: 13.6 us -> 0.1 us
  matrix products: 13 us -> 0 us
    all_gather x1 -> x0, waiting for transfers between devices: 46.4 us -> none  [per_device(): lax.all_gather(window, 'tmpl', axis=0, tiled=True)]
    sub x2 -> x0, other arithmetic: 27.1 us -> none  [detect(): prod_a * c_theta - prod_b * s_theta]
    pallas_call x0 -> x2, Pallas kernels: none -> 21.4 us  [the longest x1 11.2 us: template_spectra(): pl.pallas_call(functools.partial(template_kernel, rows, freqs), grid_spec...]
    add x2 -> x1, other arithmetic: 20.6 us -> 0.67 us  [per_device(): out = main + jnp.pad(earlier, ((0, 0), (time_dev - earlier.shape[1], 0)))]
    gather x4 -> x0, local copies, waits for them, and re-layouts: 18.4 us -> none  [detect(): picked = spectra[chans.reshape(-1)].astype(jnp.float32)]
    ppermute x1 -> x11, starting transfers between devices: 1.41 us -> 16.2 us  [the longest x10 14.9 us: per_device(): swap = lambda block, change: lax.ppermute(block, 'tmpl', route(change))]
    dot_general x5 -> x0, matrix products: 13 us -> none  [the longest x2 5.98 us: detect(): jnp.dot(waves.reshape(-1, waves.shape[2]), forward[:waves.shape[2]], pref...]
    reduce_sum x4 -> x0, other arithmetic: 7.81 us -> none  [the longest x2 3.94 us: detect(): (prod_a * c_theta - prod_b * s_theta).reshape(count, -1, freqs).sum(axis=1)]
  transfers between devices with their start and end apart: 2 -> 11, of which waited for: 2 -> 4; matrix products, arithmetic and copies ran while one was open for 9% -> 4% of each run, Pallas kernels for 0% -> 18%
where the time goes in v1:
time: 64.4 us; the launch traced here: 63.8 us
  Pallas kernels  21.4 us (33%)
  starting transfers between devices  16.2 us (25%)
  waiting for transfers between devices  14.9 us (23%)
  local copies, waits for them, and re-layouts  8.96 us (14%)
  other arithmetic  2.23 us (3%)
    ppermute x10, starting transfers between devices, per_device(): swap = lambda block, change: lax.ppermute(block, 'tmpl', route(change))  14.9 us
    pallas_call x1, Pallas kernels, template_spectra(): pl.pallas_call(functools.partial(template_kernel, rows, freqs), grid_spec...  11.2 us
    pallas_call x1, Pallas kernels, detect(): pl.pallas_call(functools.partial(detect_kernel, len(blocks), count, stati...  10.2 us
    unnamed x17, local copies, waits for them, and re-layouts  8.81 us
    ppermute x1, waiting for transfers between devices, per_device(): lax.ppermute(early, 'tm', [(i, i - 1) for i in range(1, lax.axis_size('tm...  7.62 us
    ppermute x10, waiting for transfers between devices, per_device(): swap = lambda block, change: lax.ppermute(block, 'tmpl', route(change))  7.29 us
    ppermute x1, starting transfers between devices, per_device(): lax.ppermute(early, 'tm', [(i, i - 1) for i in range(1, lax.axis_size('tm...  1.29 us
  transfers between devices with their start and end apart: 11, of which 4 were waited for; matrix products, arithmetic and copies ran while one was open for 4% of the time, Pallas kernels for 18%

profile of v1, /device:TPU:1, one launch (start us, length us, event | category | flops | bytes accessed | tf_op | source)
XLA Modules:
  0.0 63.8 jit_solution(9441618147905037861)
XLA Ops:
  0.0 3.8 %collective-permute-start.1 = (bf16[48,512]{1,0:T(8,128)(2,1)}, bf16[48,512]{1,0:T(8,128)(2,1)S(1)}, u32[]{:S(2)}, u32[]{:S(2)}) collective-permute-start(bf16[48,512]{1,0:T(8,128)(2,1)} %param.8), channel_id=1, source_target_pairs={{0,32},{8,40},{16,48},{24,56},{32,0},{40,8},{48,16},{56,24},{64,96... | collective-permute-start | bytes 147464 | tf_op jit(solution)/shard_map/ppermute | solution.py:188
  3.8 1.6 %collective-permute-start = (bf16[48,512]{1,0:T(8,128)(2,1)}, bf16[48,512]{1,0:T(8,128)(2,1)S(1)}, u32[]{:S(2)}, u32[]{:S(2)}) collective-permute-start(bf16[48,512]{1,0:T(8,128)(2,1)} %param.8), channel_id=1, source_target_pairs={{0,16},{8,24},{16,0},{24,8},{32,48},{40,56},{48,32},{56,40},{64,80... | collective-permute-start | bytes 147464 | tf_op jit(solution)/shard_map/ppermute | solution.py:188
  5.5 0.0 collective-permute-start.2
  5.5 0.9 %constant_dynamic-update-slice_fusion.3 = bf16[192,512]{1,0:T(8,128)(2,1)S(1)} fusion(bf16[48,512]{1,0:T(8,128)(2,1)} %param.8), kind=kLoop, calls=%fused_computation.13 | loop fusion | bytes 98304
  6.3 0.8 %collective-permute-done = bf16[48,512]{1,0:T(8,128)(2,1)S(1)} collective-permute-done((bf16[48,512]{1,0:T(8,128)(2,1)}, bf16[48,512]{1,0:T(8,128)(2,1)S(1)}, u32[]{:S(2)}, u32[]{:S(2)}) %collective-permute-start) | collective-permute-done | bytes 49184 | tf_op jit(solution)/shard_map/ppermute | solution.py:188
  7.2 0.0 collective-permute-done.1
  7.2 3.2 %collective-permute-done.2 = bf16[48,512]{1,0:T(8,128)(2,1)S(1)} collective-permute-done((bf16[48,512]{1,0:T(8,128)(2,1)}, bf16[48,512]{1,0:T(8,128)(2,1)S(1)}, u32[]{:S(2)}, u32[]{:S(2)}) %collective-permute-start.2) | collective-permute-done | bytes 49184 | tf_op jit(solution)/shard_map/ppermute | solution.py:188
  10.4 2.5 %collective-permute-start.5 = (bf16[192,512]{1,0:T(8,128)(2,1)S(1)}, bf16[192,512]{1,0:T(8,128)(2,1)S(1)}, u32[]{:S(2)}, u32[]{:S(2)}) collective-permute-start(bf16[192,512]{1,0:T(8,128)(2,1)S(1)} %constant_dynamic-update-slice_fusion.refs_0_), channel_id=1, source_target_pairs={{0,192},{8,200},{16,208},{24,216},{32,224},{40,232},{48,240},{56,2... | collective-permute-start | bytes 589832 | tf_op jit(solution)/shard_map/ppermute | solution.py:188
  12.9 0.5 collective-permute-start.4
  13.4 0.3 collective-permute-start.3
  13.7 0.8 %broadcast_multiply_fusion = s32[2,32,48]{2,1,0:T(8,128)S(1)} fusion(s32[2,32,48]{2,1,0:T(8,128)} %param.11), kind=kLoop, calls=%fused_computation.9 | loop fusion | flops 3072 | bytes 24576 | tf_op jit(solution)/shard_map/mul | solution.py:199
  14.4 3.2 %collective-permute-start.6 = (bf16[192,512]{1,0:T(8,128)(2,1)S(1)}, bf16[192,512]{1,0:T(8,128)(2,1)S(1)}, u32[]{:S(2)}, u32[]{:S(2)}) collective-permute-start(bf16[192,512]{1,0:T(8,128)(2,1)S(1)} %constant_dynamic-update-slice_fusion.refs_0_), channel_id=1, source_target_pairs={{0,8},{8,0},{16,24},{24,16},{32,40},{40,32},{48,56},{56,48},{64,72... | collective-permute-start | bytes 589832 | tf_op jit(solution)/shard_map/ppermute | solution.py:188
  17.7 3.2 %collective-permute-done.5.refs_3_ = bf16[192,512]{1,0:T(8,128)(2,1)S(1)} collective-permute-done((bf16[192,512]{1,0:T(8,128)(2,1)S(1)}, bf16[192,512]{1,0:T(8,128)(2,1)S(1)}, u32[]{:S(2)}, u32[]{:S(2)}) %collective-permute-start.5) | collective-permute-done | bytes 196640 | tf_op jit(solution)/shard_map/ppermute | solution.py:188
  20.9 1.9 %collective-permute-start.9 = (bf16[192,512]{1,0:T(8,128)(2,1)S(1)}, bf16[192,512]{1,0:T(8,128)(2,1)S(1)}, u32[]{:S(2)}, u32[]{:S(2)}) collective-permute-start(bf16[192,512]{1,0:T(8,128)(2,1)S(1)} %collective-permute-done.5.refs_3_), channel_id=1, source_target_pairs={{0,8},{8,0},{16,24},{24,16},{32,40},{40,32},{48,56},{56,48},{64,72... | collective-permute-start | bytes 589832 | tf_op jit(solution)/shard_map/ppermute | solution.py:188
  22.7 0.0 collective-permute-done.4.refs_2_
  22.7 1.1 %collective-permute-start.8 = (bf16[192,512]{1,0:T(8,128)(2,1)S(1)}, bf16[192,512]{1,0:T(8,128)(2,1)S(1)}, u32[]{:S(2)}, u32[]{:S(2)}) collective-permute-start(bf16[192,512]{1,0:T(8,128)(2,1)S(1)} %collective-permute-done.4.refs_2_), channel_id=1, source_target_pairs={{0,8},{8,0},{16,24},{24,16},{32,40},{40,32},{48,56},{56,48},{64,72... | collective-permute-start | bytes 589832 | tf_op jit(solution)/shard_map/ppermute | solution.py:188
  23.9 0.0 collective-permute-done.3.refs_1_
  23.9 0.0 collective-permute-start.7
  23.9 0.8 %fusion.2 = s32[2,32,48]{2,1,0:T(8,128)S(1)} fusion(s32[2,32,48]{2,1,0:T(8,128)} %param.10, s32[]{:T(128)S(6)} %axis_index.15), kind=kLoop, calls=%fused_computation.5 | loop fusion | flops 61440 | bytes 24580 | tf_op jit(solution)/shard_map/mul | solution.py:196
  24.7 0.1 reshape.12.slot_ref
  24.8 0.1 reshape.13.lag_ref
  24.8 1.4 %copy-done.1 = bf16[2,32,48,200]{3,2,1,0:T(8,128)(2,1)S(1)} copy-done((bf16[2,32,48,200]{3,2,1,0:T(8,128)(2,1)S(1)}, bf16[2,32,48,200]{3,2,1,0:T(8,128)(2,1)}, u32[]{:S(2)}) %copy-start.1) | copy-done | bytes 1228824
  26.2 1.0 %copy-done.5 = f32[896,128]{1,0:T(8,128)S(1)} copy-done((f32[896,128]{1,0:T(8,128)S(1)}, f32[896,128]{1,0:T(8,128)}, u32[]{:S(2)}) %copy-start.5) | copy-done | bytes 458776
  27.3 1.0 %copy-done.6 = bf16[200,768]{1,0:T(8,128)(2,1)S(1)} copy-done((bf16[200,768]{1,0:T(8,128)(2,1)S(1)}, bf16[200,768]{1,0:T(8,128)(2,1)}, u32[]{:S(2)}) %copy-start.6) | copy-done | bytes 307224
  28.2 11.2 %template_spectra.1.refs_11_ = f32[24576,128]{1,0:T(8,128)S(1)} custom-call(s32[3072]{0:T(1024)S(1)} %reshape.13.lag_ref, bf16[3072,200]{1,0:T(8,128)(2,1)S(1)} %bitcast.2, bf16[200,768]{1,0:T(8,128)(2,1)S(1)} %copy-done.6, f32[896,128]{1,0:T(8,128)S(1)} %copy-done.5), custom_call_target="tpu_custom_call" | custom-call | flops 943718400 | bytes 12582912 | tf_op jit(solution)/shard_map/template_spectra/pallas_call | solution.py:88
  39.4 4.5 %copy-done = f32[24576,128]{1,0:T(8,128)} copy-done((f32[24576,128]{1,0:T(8,128)}, f32[24576,128]{1,0:T(8,128)S(1)}, u32[]{:S(2)}) %copy-start) | copy-done | bytes 12582936
  44.0 0.0 collective-permute-done.9.refs_7_
  44.0 0.0 collective-permute-done.8.refs_6_
  44.0 10.2 %detect.1 = (f32[64,512]{1,0:T(8,128)S(1)}, f32[64,256]{1,0:T(8,128)S(1)}) custom-call(s32[3072]{0:T(1024)S(1)} %reshape.12.slot_ref, bf16[192,512]{1,0:T(8,128)(2,1)S(1)} %constant_dynamic-update-slice_fusion.refs_0_, bf16[192,512]{1,0:T(8,128)(2,1)S(1)} %collective-permute-done.3.refs_1_, bf16[192,512]{1,0:T(8,128)(2,1)S(1)} %collective-permute-done.4.refs_2_, ...), custom_call_target="tpu_custom_call" | custom-call | flops 1207959552 | bytes 12582912 | tf_op jit(solution)/shard_map/detect/pallas_call | solution.py:157
  54.3 1.3 %collective-permute-start.10 = (f32[64,256]{1,0:T(8,128)S(1)}, f32[64,256]{1,0:T(8,128)S(1)}, u32[]{:S(2)}, u32[]{:S(2)}) collective-permute-start(f32[64,256]{1,0:T(8,128)S(1)} %get-tuple-element.8), channel_id=1, source_target_pairs={{1,0},{2,1},{3,2},{4,3},{5,4},{6,5},{7,6},{9,8},{10,9},{11,10},{12... | collective-permute-start | bytes 196616 | tf_op jit(solution)/shard_map/ppermute | solution.py:202
  55.6 7.6 %collective-permute-done.10 = f32[64,256]{1,0:T(8,128)S(1)} collective-permute-done((f32[64,256]{1,0:T(8,128)S(1)}, f32[64,256]{1,0:T(8,128)S(1)}, u32[]{:S(2)}, u32[]{:S(2)}) %collective-permute-start.10) | collective-permute-done | bytes 65568 | tf_op jit(solution)/shard_map/ppermute | solution.py:202
  63.2 0.7 %pad_add_fusion = f32[64,512]{1,0:T(8,128)} fusion(f32[64,512]{1,0:T(8,128)S(1)} %get-tuple-element.7, f32[64,256]{1,0:T(8,128)S(1)} %collective-permute-done.10), kind=kLoop, calls=%fused_computation | loop fusion | flops 32768 | bytes 327680 | tf_op jit(solution)/shard_map/add | solution.py:203
  (15 shorter events, 0.0 us)
Async XLA Ops:
  0.0 7.2 %collective-permute-start.1 = (bf16[48,512]{1,0:T(8,128)(2,1)}, bf16[48,512]{1,0:T(8,128)(2,1)S(1)}, u32[]{:S(2)}, u32[]{:S(2)}) collective-permute-start(bf16[48,512]{1,0:T(8,128)(2,1)} %param.8), channel_id=1, source_target_pairs={{0,32},{8,40},{16,48},{24,56},{32,0},{40,8},{48,16},{56,24},{64,96... | collective-permute-start | bytes 147464 | tf_op jit(solution)/shard_map/ppermute | solution.py:188
  3.8 3.4 %collective-permute-start = (bf16[48,512]{1,0:T(8,128)(2,1)}, bf16[48,512]{1,0:T(8,128)(2,1)S(1)}, u32[]{:S(2)}, u32[]{:S(2)}) collective-permute-start(bf16[48,512]{1,0:T(8,128)(2,1)} %param.8), channel_id=1, source_target_pairs={{0,16},{8,24},{16,0},{24,8},{32,48},{40,56},{48,32},{56,40},{64,80... | collective-permute-start | bytes 147464 | tf_op jit(solution)/shard_map/ppermute | solution.py:188
  5.5 4.9 %collective-permute-start.2 = (bf16[48,512]{1,0:T(8,128)(2,1)}, bf16[48,512]{1,0:T(8,128)(2,1)S(1)}, u32[]{:S(2)}, u32[]{:S(2)}) collective-permute-start(bf16[48,512]{1,0:T(8,128)(2,1)} %param.8), channel_id=1, source_target_pairs={{0,48},{8,56},{16,32},{24,40},{32,16},{40,24},{48,0},{56,8},{64,11... | collective-permute-start | bytes 147464 | tf_op jit(solution)/shard_map/ppermute | solution.py:188
  10.4 10.5 %collective-permute-start.5 = (bf16[192,512]{1,0:T(8,128)(2,1)S(1)}, bf16[192,512]{1,0:T(8,128)(2,1)S(1)}, u32[]{:S(2)}, u32[]{:S(2)}) collective-permute-start(bf16[192,512]{1,0:T(8,128)(2,1)S(1)} %constant_dynamic-update-slice_fusion.refs_0_), channel_id=1, source_target_pairs={{0,192},{8,200},{16,208},{24,216},{32,224},{40,232},{48,240},{56,2... | collective-permute-start | bytes 589832 | tf_op jit(solution)/shard_map/ppermute | solution.py:188
  12.9 9.8 %collective-permute-start.4 = (bf16[192,512]{1,0:T(8,128)(2,1)S(1)}, bf16[192,512]{1,0:T(8,128)(2,1)S(1)}, u32[]{:S(2)}, u32[]{:S(2)}) collective-permute-start(bf16[192,512]{1,0:T(8,128)(2,1)S(1)} %constant_dynamic-update-slice_fusion.refs_0_), channel_id=1, source_target_pairs={{0,128},{8,136},{16,144},{24,152},{32,160},{40,168},{48,176},{56,1... | collective-permute-start | bytes 589832 | tf_op jit(solution)/shard_map/ppermute | solution.py:188
  13.4 10.5 %collective-permute-start.3 = (bf16[192,512]{1,0:T(8,128)(2,1)S(1)}, bf16[192,512]{1,0:T(8,128)(2,1)S(1)}, u32[]{:S(2)}, u32[]{:S(2)}) collective-permute-start(bf16[192,512]{1,0:T(8,128)(2,1)S(1)} %constant_dynamic-update-slice_fusion.refs_0_), channel_id=1, source_target_pairs={{0,64},{8,72},{16,80},{24,88},{32,96},{40,104},{48,112},{56,120},{... | collective-permute-start | bytes 589832 | tf_op jit(solution)/shard_map/ppermute | solution.py:188
  14.4 29.5 %collective-permute-start.6 = (bf16[192,512]{1,0:T(8,128)(2,1)S(1)}, bf16[192,512]{1,0:T(8,128)(2,1)S(1)}, u32[]{:S(2)}, u32[]{:S(2)}) collective-permute-start(bf16[192,512]{1,0:T(8,128)(2,1)S(1)} %constant_dynamic-update-slice_fusion.refs_0_), channel_id=1, source_target_pairs={{0,8},{8,0},{16,24},{24,16},{32,40},{40,32},{48,56},{56,48},{64,72... | collective-permute-start | bytes 589832 | tf_op jit(solution)/shard_map/ppermute | solution.py:188
  20.9 23.1 %collective-permute-start.9 = (bf16[192,512]{1,0:T(8,128)(2,1)S(1)}, bf16[192,512]{1,0:T(8,128)(2,1)S(1)}, u32[]{:S(2)}, u32[]{:S(2)}) collective-permute-start(bf16[192,512]{1,0:T(8,128)(2,1)S(1)} %collective-permute-done.5.refs_3_), channel_id=1, source_target_pairs={{0,8},{8,0},{16,24},{24,16},{32,40},{40,32},{48,56},{56,48},{64,72... | collective-permute-start | bytes 589832 | tf_op jit(solution)/shard_map/ppermute | solution.py:188
  22.7 21.2 %collective-permute-start.8 = (bf16[192,512]{1,0:T(8,128)(2,1)S(1)}, bf16[192,512]{1,0:T(8,128)(2,1)S(1)}, u32[]{:S(2)}, u32[]{:S(2)}) collective-permute-start(bf16[192,512]{1,0:T(8,128)(2,1)S(1)} %collective-permute-done.4.refs_2_), channel_id=1, source_target_pairs={{0,8},{8,0},{16,24},{24,16},{32,40},{40,32},{48,56},{56,48},{64,72... | collective-permute-start | bytes 589832 | tf_op jit(solution)/shard_map/ppermute | solution.py:188
  23.9 20.1 %collective-permute-start.7 = (bf16[192,512]{1,0:T(8,128)(2,1)S(1)}, bf16[192,512]{1,0:T(8,128)(2,1)S(1)}, u32[]{:S(2)}, u32[]{:S(2)}) collective-permute-start(bf16[192,512]{1,0:T(8,128)(2,1)S(1)} %collective-permute-done.3.refs_1_), channel_id=1, source_target_pairs={{0,8},{8,0},{16,24},{24,16},{32,40},{40,32},{48,56},{56,48},{64,72... | collective-permute-start | bytes 589832 | tf_op jit(solution)/shard_map/ppermute | solution.py:188
  24.8 1.4 %copy-start.1 = (bf16[2,32,48,200]{3,2,1,0:T(8,128)(2,1)S(1)}, bf16[2,32,48,200]{3,2,1,0:T(8,128)(2,1)}, u32[]{:S(2)}) copy-start(bf16[2,32,48,200]{3,2,1,0:T(8,128)(2,1)} %param.9) | copy-start | bytes 3686404
  26.2 1.0 %copy-start.5 = (f32[896,128]{1,0:T(8,128)S(1)}, f32[896,128]{1,0:T(8,128)}, u32[]{:S(2)}) copy-start(f32[896,128]{1,0:T(8,128)} %constant.42.clone.phase_ref) | copy-start | bytes 1376260
  27.3 1.0 %copy-start.6 = (bf16[200,768]{1,0:T(8,128)(2,1)S(1)}, bf16[200,768]{1,0:T(8,128)(2,1)}, u32[]{:S(2)}) copy-start(bf16[200,768]{1,0:T(8,128)(2,1)} %constant.48.forward_ref) | copy-start | bytes 921604
  28.2 15.8 %copy-start.2 = (bf16[768,768]{1,0:T(8,128)(2,1)S(1)}, bf16[768,768]{1,0:T(8,128)(2,1)}, u32[]{:S(2)}) copy-start(bf16[768,768]{1,0:T(8,128)(2,1)} %constant.44.clone.refs_10_) | copy-start | bytes 3538948
  28.2 15.8 %copy-start.3 = (bf16[768,768]{1,0:T(8,128)(2,1)S(1)}, bf16[768,768]{1,0:T(8,128)(2,1)}, u32[]{:S(2)}) copy-start(bf16[768,768]{1,0:T(8,128)(2,1)} %constant.43.clone.refs_9_) | copy-start | bytes 3538948
  28.2 15.8 %copy-start.4 = (bf16[512,768]{1,0:T(8,128)(2,1)S(1)}, bf16[512,768]{1,0:T(8,128)(2,1)}, u32[]{:S(2)}) copy-start(bf16[512,768]{1,0:T(8,128)(2,1)} %constant.41.clone.refs_8_) | copy-start | bytes 2359300
  39.4 4.5 %copy-start = (f32[24576,128]{1,0:T(8,128)}, f32[24576,128]{1,0:T(8,128)S(1)}, u32[]{:S(2)}) copy-start(f32[24576,128]{1,0:T(8,128)S(1)} %template_spectra.1.refs_11_) | copy-start | bytes 37748740
  54.3 8.9 %collective-permute-start.10 = (f32[64,256]{1,0:T(8,128)S(1)}, f32[64,256]{1,0:T(8,128)S(1)}, u32[]{:S(2)}, u32[]{:S(2)}) collective-permute-start(f32[64,256]{1,0:T(8,128)S(1)} %get-tuple-element.8), channel_id=1, source_target_pairs={{1,0},{2,1},{3,2},{4,3},{5,4},{6,5},{7,6},{9,8},{10,9},{11,10},{12... | collective-permute-start | bytes 196616 | tf_op jit(solution)/shard_map/ppermute | solution.py:202

commit v2 on v1

v2 whole, which is shorter than its diff:
```python
import functools
import math

import jax
import jax.numpy as jnp
import numpy as np
from jax import lax
from jax.experimental import pallas as pl
from jax.experimental.pallas import tpu as pltpu
from jax.sharding import PartitionSpec as P

L = 200
LAGS = 56
EXTRA = L + LAGS - 2
HOLD = 128
LAG_ROWS = 64
VMEM_K1 = 20 << 20
VMEM_K2 = 34 << 20
GROUPS = 8


def angles(samples, freqs, width):
    return 2.0 * math.pi / width * (samples[:, None] * freqs[None, :] % width)


def host_tables(time_dev):
    width = time_dev + EXTRA
    freqs = width // 2 + 1
    freq = np.arange(freqs)
    ang = angles(np.arange(time_dev), freq, width)
    forward = np.concatenate([np.cos(ang), np.sin(ang)], axis=1).astype(np.float32).astype(jnp.bfloat16)
    turn = angles(np.arange(LAGS), freq, width)
    phase = np.zeros((2 * LAG_ROWS, 2 * freqs), jnp.bfloat16)
    phase[:LAGS], phase[LAG_ROWS : LAG_ROWS + LAGS] = halves(np.concatenate([np.cos(turn), np.sin(turn)], axis=1))
    weight = np.where((freq == 0) | (freq == freqs - 1), 1.0, 2.0) / width
    early = np.arange(time_dev // 2, time_dev) + EXTRA
    tau = np.concatenate([np.arange(time_dev), early])
    back = angles(tau, freq, width)
    inverse = np.concatenate([np.cos(back) * weight, np.sin(back) * weight], axis=1)
    inverse[time_dev:][early < time_dev] = 0.0
    return forward, phase, *halves(inverse.T)


def halves(table):
    table = table.astype(np.float32)
    high = table.astype(jnp.bfloat16)
    return high, (table - high.astype(np.float32)).astype(jnp.bfloat16)


def template_kernel(step, freqs, lag_ref, record_ref, wave_hbm, forward_hbm, phase_hbm, out_hbm, own_ref, waves, forward, phases, out, sems, out_sems):
    starts = range(0, wave_hbm.shape[0], step)
    loads = [pltpu.make_async_copy(forward_hbm, forward, sems.at[0]), pltpu.make_async_copy(phase_hbm, phases, sems.at[1])]
    for n, start in enumerate(starts):
        part = pl.ds(start, step)
        loads.append(pltpu.make_async_copy(wave_hbm.at[part], waves.at[part], sems.at[2 + n]))
    for load in loads:
        load.start()
    own_ref[...] = record_ref[...]
    stores = []
    for n, start in enumerate(starts):
        for load in loads[:3] if n == 0 else loads[2 + n : 3 + n]:
            load.wait()
        lag = jnp.concatenate([lag_ref[pl.ds((start + at) // HOLD, 1), :] for at in range(0, step, HOLD)], axis=1)
        lag_row = lax.broadcasted_iota(jnp.int32, (2 * LAG_ROWS, step), 0) & (LAG_ROWS - 1)
        chosen = (lag_row == lag).astype(jnp.float32).astype(jnp.bfloat16)
        phase = lax.dot_general(chosen, phases[...], (((0,), (0,)), ((), ())), preferred_element_type=jnp.float32)
        dft = jnp.dot(waves[pl.ds(start, step), :], forward[...], preferred_element_type=jnp.float32)
        for j in range(freqs // HOLD):
            low, high = slice(j * HOLD, (j + 1) * HOLD), slice(freqs + j * HOLD, freqs + (j + 1) * HOLD)
            h_cos, h_sin, c_theta, s_theta = dft[:, low], dft[:, high], phase[:, low], phase[:, high]
            out[pl.ds(start * 8 + j, step, stride=8), :] = h_cos * c_theta - h_sin * s_theta
            out[pl.ds(start * 8 + 4 + j, step, stride=8), :] = h_cos * s_theta + h_sin * c_theta
        part = pl.ds(start * 8, step * 8)
        stores.append(pltpu.make_async_copy(out.at[part], out_hbm.at[part], out_sems.at[n]))
        stores[-1].start()
    for store in stores:
        store.wait()


def template_spectra(waves, lags, records, forward, phase, freqs):
    count, length = waves.shape
    whole = pl.BlockSpec(memory_space=pltpu.VMEM)
    step = 512
    return pl.pallas_call(
        functools.partial(template_kernel, step, freqs),
        in_specs=[whole] * 2 + [pl.BlockSpec(memory_space=pltpu.HBM)] * 3,
        out_specs=[pl.BlockSpec(memory_space=pltpu.HBM), whole],
        out_shape=[pltpu.HBM((count * 8, HOLD), jnp.float32), jax.ShapeDtypeStruct(records.shape, records.dtype)],
        scratch_shapes=[
            pltpu.VMEM(waves.shape, waves.dtype),
            pltpu.VMEM((length, 2 * freqs), forward.dtype),
            pltpu.VMEM(phase.shape, phase.dtype),
            pltpu.VMEM((count * 8, HOLD), jnp.float32),
            pltpu.SemaphoreType.DMA((2 + count // step,)),
            pltpu.SemaphoreType.DMA((count // step,)),
        ],
        compiler_params=pltpu.CompilerParams(vmem_limit_bytes=VMEM_K1),
        cost_estimate=pl.CostEstimate(flops=count * length * freqs * 4, bytes_accessed=count * 8 * HOLD * 4, transcendentals=0),
        name="template_spectra",
    )(lags, records, *(pltpu.with_memory_space_constraint(a, pltpu.HBM) for a in (waves, forward[:length], phase)))


def detect_kernel(n_blocks, count, stations, freqs, slot_ref, *refs):
    blocks, (q_hbm, forward_ref, high_ref, low_ref, main_ref, early_ref, table, acc, q, sems) = refs[:n_blocks], refs[n_blocks:]
    share = count // GROUPS
    loads = []
    for g in range(GROUPS):
        part = pl.ds(g * share * stations * 8, share * stations * 8)
        loads.append(pltpu.make_async_copy(q_hbm.at[part], q.at[part], sems.at[g]))
        loads[g].start()
    chunks = freqs // HOLD
    size = blocks[0].shape[0]
    for b, block in enumerate(blocks):
        dft = jnp.dot(block[...], forward_ref[...], preferred_element_type=jnp.float32)
        for j in range(chunks):
            real = dft[:, j * HOLD : (j + 1) * HOLD]
            imag = dft[:, freqs + j * HOLD : freqs + (j + 1) * HOLD]
            start = b * size * 16
            table[pl.ds(start + j, size, stride=16), :] = real
            table[pl.ds(start + 4 + j, size, stride=16), :] = imag
            table[pl.ds(start + 8 + j, size, stride=16), :] = imag
            table[pl.ds(start + 12 + j, size, stride=16), :] = -real

    def one(t, carry):
        first = [jnp.zeros((8, HOLD), jnp.float32)] * 2
        second = list(first)
        weights = q.at[pl.ds(pl.multiple_of(t * stations * 8, stations * 8), stations * 8), :]
        for k in range(stations):
            slot = pl.multiple_of(slot_ref[t, k], 16)
            weight = weights[k * 8 : k * 8 + 8, :]
            first[k % 2] += weight * table[pl.ds(slot, 8), :]
            second[k % 2] += weight * table[pl.ds(slot + 8, 8), :]
        acc[pl.ds(pl.multiple_of(t * 16, 16), 8), :] = first[0] + first[1]
        acc[pl.ds(pl.multiple_of(t * 16 + 8, 8), 8), :] = second[0] + second[1]
        return carry

    for g, load in enumerate(loads):
        load.wait()
        lax.fori_loop(g * share, (g + 1) * share, one, 0)
    joint = jnp.concatenate(
        [
            acc[pl.ds(8 * part + j, count, stride=16), :] + acc[pl.ds(8 * part + 4 + j, count, stride=16), :]
            for part in range(2)
            for j in range(chunks)
        ],
        axis=1,
    )
    top = joint.astype(jnp.bfloat16)
    rest = (joint - top.astype(jnp.float32)).astype(jnp.bfloat16)
    both = jnp.dot(jnp.concatenate([top, rest], axis=0), high_ref[...], preferred_element_type=jnp.float32)
    out = both[:count] + both[count:] + jnp.dot(top, low_ref[...], preferred_element_type=jnp.float32)
    time_dev = main_ref.shape[1]
    main_ref[...] = out[:, :time_dev]
    early_ref[...] = out[:, time_dev:]


def detect(slots, blocks, q, forward, high, low, count, stations, freqs, time_dev):
    rows = sum(b.shape[0] for b in blocks)
    whole = pl.BlockSpec(memory_space=pltpu.VMEM)
    return pl.pallas_call(
        functools.partial(detect_kernel, len(blocks), count, stations, freqs),
        in_specs=[pl.BlockSpec(memory_space=pltpu.SMEM)] + [whole] * len(blocks)
        + [pl.BlockSpec(memory_space=pltpu.HBM)]
        + [whole] * 3,
        out_specs=[whole, whole],
        out_shape=[
            jax.ShapeDtypeStruct((count, time_dev), jnp.float32),
            jax.ShapeDtypeStruct((count, time_dev // 2), jnp.float32),
        ],
        scratch_shapes=[
            pltpu.VMEM((rows * 16, HOLD), jnp.float32),
            pltpu.VMEM((count * 16, HOLD), jnp.float32),
            pltpu.VMEM(q.shape, q.dtype),
            pltpu.SemaphoreType.DMA((GROUPS,)),
        ],
        compiler_params=pltpu.CompilerParams(vmem_limit_bytes=VMEM_K2),
        cost_estimate=pl.CostEstimate(flops=rows * time_dev * freqs * 4, bytes_accessed=count * stations * 8 * HOLD * 4, transcendentals=0),
        name="detect",
    )(slots, *blocks, pltpu.with_memory_space_constraint(q, pltpu.HBM), forward, high, low)


def route(change):
    dx, dz, dc = change
    code = (dx * 4 + dz) * 2 + dc
    return [(i, i ^ code) for i in range(32)]


def per_device(records, templates, channels, moveouts):
    per, time_dev = records.shape
    batches, count, stations, length = templates.shape
    freqs = (time_dev + EXTRA) // 2 + 1
    forward, phase, high, low = (jnp.asarray(t) for t in host_tables(time_dev))
    swap = lambda block, change: lax.ppermute(block, "tmpl", route(change))

    q, own = template_spectra(templates.reshape(-1, length), moveouts.reshape(-1, HOLD), records, forward, phase, freqs)
    line = [own] + [swap(records, (0, d, 0)) for d in (1, 2, 3)]
    line = jnp.concatenate(line, axis=0)
    plane = [line] + [swap(line, (d, 0, 0)) for d in (1, 2, 3)]
    blocks = plane + [swap(block, (0, 0, 1)) for block in plane]

    apart = (channels // per) ^ lax.axis_index("tmpl")
    place = ((apart & 1) * 16 + (apart >> 1)) * per + channels % per
    slots = (place * 16).reshape(-1, stations)

    main, early = detect(slots, blocks, q, forward, high, low, batches * count, stations, freqs, time_dev)
    earlier = lax.ppermute(early, "tm", [(i, i - 1) for i in range(1, lax.axis_size("tm"))])
    out = main + jnp.pad(earlier, ((0, 0), (time_dev - earlier.shape[1], 0)))
    return out.reshape(batches, count, time_dev)


def solution(mesh):
    placed = (
        P("tmpl", "tm"),
        P(None, "tmpl", None, None),
        P(None, "tmpl", None),
        P(None, "tmpl", None),
    )
    return jax.shard_map(
        per_device, mesh=mesh, in_specs=placed, out_specs=P(None, "tmpl", "tm"), check_vma=False
    )
```

time: 64.4 us -> 50.7 us (0.79)
  the two profiles are of different devices: /device:TPU:1 before, /device:TPU:201 now
where the time goes in v2:
time: 50.7 us; the launch traced here: 50.4 us
  Pallas kernels  17 us (34%)
  waiting for transfers between devices  15.6 us (31%)
  starting transfers between devices  14.5 us (29%)
  local copies, waits for them, and re-layouts  1.67 us (3%)
  other arithmetic  1.47 us (3%)
    ppermute x10, starting transfers between devices, per_device(): swap = lambda block, change: lax.ppermute(block, 'tmpl', route(change))  12.2 us
    pallas_call x1, Pallas kernels, detect(): pl.pallas_call(functools.partial(detect_kernel, len(blocks), count, stati...  9.84 us
    ppermute x1, waiting for transfers between devices, per_device(): lax.ppermute(early, 'tm', [(i, i - 1) for i in range(1, lax.axis_size('tm...  9.79 us
    pallas_call x1, Pallas kernels, template_spectra(): pl.pallas_call(functools.partial(template_kernel, step, freqs), in_specs=...  7.19 us
    ppermute x10, waiting for transfers between devices, per_device(): swap = lambda block, change: lax.ppermute(block, 'tmpl', route(change))  5.84 us
    ppermute x1, starting transfers between devices, per_device(): lax.ppermute(early, 'tm', [(i, i - 1) for i in range(1, lax.axis_size('tm...  2.34 us
  transfers between devices with their start and end apart: 11, of which 4 were waited for; matrix products, arithmetic and copies ran while one was open for 3% of the time, Pallas kernels for 14%

profile of v2, /device:TPU:201, one launch (start us, length us, event | category | flops | bytes accessed | tf_op | source)
XLA Modules:
  0.0 50.4 jit_solution(15912796115989716124)
XLA Ops:
  0.0 0.7 %collective-permute-start = (bf16[48,512]{1,0:T(8,128)(2,1)}, bf16[48,512]{1,0:T(8,128)(2,1)S(1)}, u32[]{:S(2)}, u32[]{:S(2)}) collective-permute-start(bf16[48,512]{1,0:T(8,128)(2,1)} %record_ref.1), channel_id=1, source_target_pairs={{0,16},{8,24},{16,0},{24,8},{32,48},{40,56},{48,32},{56,40},{64,80... | collective-permute-start | bytes 147464 | tf_op jit(solution)/shard_map/ppermute | solution.py:193
  0.7 0.7 %collective-permute-start.2 = (bf16[48,512]{1,0:T(8,128)(2,1)}, bf16[48,512]{1,0:T(8,128)(2,1)S(1)}, u32[]{:S(2)}, u32[]{:S(2)}) collective-permute-start(bf16[48,512]{1,0:T(8,128)(2,1)} %record_ref.1), channel_id=1, source_target_pairs={{0,48},{8,56},{16,32},{24,40},{32,16},{40,24},{48,0},{56,8},{64,11... | collective-permute-start | bytes 147464 | tf_op jit(solution)/shard_map/ppermute | solution.py:193
  1.5 2.1 %collective-permute-start.1 = (bf16[48,512]{1,0:T(8,128)(2,1)}, bf16[48,512]{1,0:T(8,128)(2,1)S(1)}, u32[]{:S(2)}, u32[]{:S(2)}) collective-permute-start(bf16[48,512]{1,0:T(8,128)(2,1)} %record_ref.1), channel_id=1, source_target_pairs={{0,32},{8,40},{16,48},{24,56},{32,0},{40,8},{48,16},{56,24},{64,96... | collective-permute-start | bytes 147464 | tf_op jit(solution)/shard_map/ppermute | solution.py:193
  3.5 0.8 %reshape.13.lag_ref = s32[24,128]{1,0:T(8,128)S(1)} reshape(s32[2,32,48]{2,1,0:T(8,128)} %param.11) | data formatting | bytes 24576 | tf_op jit(solution)/shard_map/reshape | solution.py:195
  4.4 0.0 copy-start.3
  4.4 0.8 %copy-done.3 = bf16[48,512]{1,0:T(8,128)(2,1)S(1)} copy-done((bf16[48,512]{1,0:T(8,128)(2,1)S(1)}, bf16[48,512]{1,0:T(8,128)(2,1)}, u32[]{:S(2)}) %copy-start.3) | copy-done | bytes 49176
  5.2 7.2 %template_spectra.1 = (f32[24576,128]{1,0:T(8,128)}, bf16[48,512]{1,0:T(8,128)(2,1)S(1)}) custom-call(s32[24,128]{1,0:T(8,128)S(1)} %reshape.13.lag_ref, bf16[48,512]{1,0:T(8,128)(2,1)S(1)} %copy-done.3, bf16[3072,200]{1,0:T(8,128)(2,1)} %bitcast.4, bf16[200,768]{1,0:T(8,128)(2,1)} %constant.48.forward_hbm, bf16[128,768]{1,0:T(8,128)(2,1)} %constant.42.clone.phase_hbm), custom_call_target="tpu_custom_call" | custom-call | flops 943718400 | bytes 12582912 | tf_op jit(solution)/shard_map/template_spectra/pallas_call | solution.py:84
  12.4 0.0 collective-permute-done
  12.4 0.0 collective-permute-done.1
  12.4 0.0 collective-permute-done.2
  12.5 2.6 %collective-permute-start.5 = (bf16[192,512]{1,0:T(8,128)(2,1)S(1)}, bf16[192,512]{1,0:T(8,128)(2,1)S(1)}, u32[]{:S(2)}, u32[]{:S(2)}) collective-permute-start(bf16[192,512]{1,0:T(8,128)(2,1)S(1)} %constant_dynamic-update-slice_fusion.refs_0_), channel_id=1, source_target_pairs={{0,192},{8,200},{16,208},{24,216},{32,224},{40,232},{48,240},{56,2... | collective-permute-start | bytes 589832 | tf_op jit(solution)/shard_map/ppermute | solution.py:193
  15.0 0.5 %collective-permute-start.4 = (bf16[192,512]{1,0:T(8,128)(2,1)S(1)}, bf16[192,512]{1,0:T(8,128)(2,1)}, u32[]{:S(2)}, u32[]{:S(2)}) collective-permute-start(bf16[192,512]{1,0:T(8,128)(2,1)S(1)} %constant_dynamic-update-slice_fusion.refs_0_), channel_id=1, source_target_pairs={{0,128},{8,136},{16,144},{24,152},{32,160},{40,168},{48,176},{56,1... | collective-permute-start | bytes 589832 | tf_op jit(solution)/shard_map/ppermute | solution.py:193
  15.6 0.3 collective-permute-start.3
  15.8 2.4 %collective-permute-start.6 = (bf16[192,512]{1,0:T(8,128)(2,1)S(1)}, bf16[192,512]{1,0:T(8,128)(2,1)S(1)}, u32[]{:S(2)}, u32[]{:S(2)}) collective-permute-start(bf16[192,512]{1,0:T(8,128)(2,1)S(1)} %constant_dynamic-update-slice_fusion.refs_0_), channel_id=1, source_target_pairs={{0,8},{8,0},{16,24},{24,16},{32,40},{40,32},{48,56},{56,48},{64,72... | collective-permute-start | bytes 589832 | tf_op jit(solution)/shard_map/ppermute | solution.py:193
  18.2 5.0 %collective-permute-done.5.refs_3_ = bf16[192,512]{1,0:T(8,128)(2,1)S(1)} collective-permute-done((bf16[192,512]{1,0:T(8,128)(2,1)S(1)}, bf16[192,512]{1,0:T(8,128)(2,1)S(1)}, u32[]{:S(2)}, u32[]{:S(2)}) %collective-permute-start.5) | collective-permute-done | bytes 196640 | tf_op jit(solution)/shard_map/ppermute | solution.py:193
  23.2 1.2 %collective-permute-start.9 = (bf16[192,512]{1,0:T(8,128)(2,1)S(1)}, bf16[192,512]{1,0:T(8,128)(2,1)S(1)}, u32[]{:S(2)}, u32[]{:S(2)}) collective-permute-start(bf16[192,512]{1,0:T(8,128)(2,1)S(1)} %collective-permute-done.5.refs_3_), channel_id=1, source_target_pairs={{0,8},{8,0},{16,24},{24,16},{32,40},{40,32},{48,56},{56,48},{64,72... | collective-permute-start | bytes 589832 | tf_op jit(solution)/shard_map/ppermute | solution.py:193
  24.4 0.0 collective-permute-done.4.refs_2_
  24.4 1.7 %collective-permute-start.8 = (bf16[192,512]{1,0:T(8,128)(2,1)}, bf16[192,512]{1,0:T(8,128)(2,1)S(1)}, u32[]{:S(2)}, u32[]{:S(2)}) collective-permute-start(bf16[192,512]{1,0:T(8,128)(2,1)} %collective-permute-done.4.refs_2_), channel_id=1, source_target_pairs={{0,8},{8,0},{16,24},{24,16},{32,40},{40,32},{48,56},{56,48},{64,72... | collective-permute-start | bytes 589832 | tf_op jit(solution)/shard_map/ppermute | solution.py:193
  26.1 0.0 collective-permute-done.3.refs_1_
  26.1 0.0 collective-permute-start.7
  26.1 0.8 %fusion.2 = s32[2,32,48]{2,1,0:T(8,128)S(1)} fusion(s32[2,32,48]{2,1,0:T(8,128)} %param.10, s32[]{:T(128)S(6)} %axis_index.15), kind=kLoop, calls=%fused_computation.5 | loop fusion | flops 61440 | bytes 24580 | tf_op jit(solution)/shard_map/mul | solution.py:203
  26.9 0.0 collective-permute-done.6.refs_4_
  26.9 0.0 collective-permute-done.9.refs_7_
  27.0 0.4 collective-permute-done.8.refs_6_
  27.4 0.4 collective-permute-done.7.refs_5_
  27.8 0.0 copy-done
  27.8 0.0 copy-done.1
  27.8 0.0 copy-done.2
  27.8 9.8 %detect.1 = (f32[64,512]{1,0:T(8,128)S(1)}, f32[64,256]{1,0:T(8,128)S(1)}) custom-call(s32[64,48]{1,0:T(8,128)S(1)} %bitcast.3, bf16[192,512]{1,0:T(8,128)(2,1)S(1)} %constant_dynamic-update-slice_fusion.refs_0_, bf16[192,512]{1,0:T(8,128)(2,1)} %collective-permute-done.3.refs_1_, bf16[192,512]{1,0:T(8,128)(2,1)} %collective-permute-done.4.refs_2_, ...), custom_call_target="tpu_custom_call" | custom-call | flops 1207959552 | bytes 12582912 | tf_op jit(solution)/shard_map/detect/pallas_call | solution.py:160
  37.6 2.3 %collective-permute-start.10 = (f32[64,256]{1,0:T(8,128)S(1)}, f32[64,256]{1,0:T(8,128)S(1)}, u32[]{:S(2)}, u32[]{:S(2)}) collective-permute-start(f32[64,256]{1,0:T(8,128)S(1)} %get-tuple-element.12), channel_id=1, source_target_pairs={{1,0},{2,1},{3,2},{4,3},{5,4},{6,5},{7,6},{9,8},{10,9},{11,10},{12... | collective-permute-start | bytes 196616 | tf_op jit(solution)/shard_map/ppermute | solution.py:206
  40.0 9.8 %collective-permute-done.10 = f32[64,256]{1,0:T(8,128)S(1)} collective-permute-done((f32[64,256]{1,0:T(8,128)S(1)}, f32[64,256]{1,0:T(8,128)S(1)}, u32[]{:S(2)}, u32[]{:S(2)}) %collective-permute-start.10) | collective-permute-done | bytes 65568 | tf_op jit(solution)/shard_map/ppermute | solution.py:206
  49.8 0.7 %pad_add_fusion = f32[64,512]{1,0:T(8,128)} fusion(f32[64,512]{1,0:T(8,128)S(1)} %get-tuple-element.11, f32[64,256]{1,0:T(8,128)S(1)} %collective-permute-done.10), kind=kLoop, calls=%fused_computation | loop fusion | flops 32768 | bytes 327680 | tf_op jit(solution)/shard_map/add | solution.py:207
  (7 shorter events, 0.0 us)
Async XLA Ops:
  0.0 12.4 %collective-permute-start = (bf16[48,512]{1,0:T(8,128)(2,1)}, bf16[48,512]{1,0:T(8,128)(2,1)S(1)}, u32[]{:S(2)}, u32[]{:S(2)}) collective-permute-start(bf16[48,512]{1,0:T(8,128)(2,1)} %record_ref.1), channel_id=1, source_target_pairs={{0,16},{8,24},{16,0},{24,8},{32,48},{40,56},{48,32},{56,40},{64,80... | collective-permute-start | bytes 147464 | tf_op jit(solution)/shard_map/ppermute | solution.py:193
  0.7 11.7 %collective-permute-start.2 = (bf16[48,512]{1,0:T(8,128)(2,1)}, bf16[48,512]{1,0:T(8,128)(2,1)S(1)}, u32[]{:S(2)}, u32[]{:S(2)}) collective-permute-start(bf16[48,512]{1,0:T(8,128)(2,1)} %record_ref.1), channel_id=1, source_target_pairs={{0,48},{8,56},{16,32},{24,40},{32,16},{40,24},{48,0},{56,8},{64,11... | collective-permute-start | bytes 147464 | tf_op jit(solution)/shard_map/ppermute | solution.py:193
  1.5 11.0 %collective-permute-start.1 = (bf16[48,512]{1,0:T(8,128)(2,1)}, bf16[48,512]{1,0:T(8,128)(2,1)S(1)}, u32[]{:S(2)}, u32[]{:S(2)}) collective-permute-start(bf16[48,512]{1,0:T(8,128)(2,1)} %record_ref.1), channel_id=1, source_target_pairs={{0,32},{8,40},{16,48},{24,56},{32,0},{40,8},{48,16},{56,24},{64,96... | collective-permute-start | bytes 147464 | tf_op jit(solution)/shard_map/ppermute | solution.py:193
  4.4 0.8 %copy-start.3 = (bf16[48,512]{1,0:T(8,128)(2,1)S(1)}, bf16[48,512]{1,0:T(8,128)(2,1)}, u32[]{:S(2)}) copy-start(bf16[48,512]{1,0:T(8,128)(2,1)} %record_ref.1) | copy-start | bytes 147460
  5.2 22.6 %copy-start = (bf16[768,768]{1,0:T(8,128)(2,1)S(1)}, bf16[768,768]{1,0:T(8,128)(2,1)}, u32[]{:S(2)}) copy-start(bf16[768,768]{1,0:T(8,128)(2,1)} %constant.44.clone.refs_11_) | copy-start | bytes 3538948
  5.2 22.6 %copy-start.1 = (bf16[768,768]{1,0:T(8,128)(2,1)S(1)}, bf16[768,768]{1,0:T(8,128)(2,1)}, u32[]{:S(2)}) copy-start(bf16[768,768]{1,0:T(8,128)(2,1)} %constant.43.clone.refs_10_) | copy-start | bytes 3538948
  5.2 22.6 %copy-start.2 = (bf16[512,768]{1,0:T(8,128)(2,1)S(1)}, bf16[512,768]{1,0:T(8,128)(2,1)}, u32[]{:S(2)}) copy-start(bf16[512,768]{1,0:T(8,128)(2,1)} %constant.41.clone.refs_9_) | copy-start | bytes 2359300
  12.5 10.7 %collective-permute-start.5 = (bf16[192,512]{1,0:T(8,128)(2,1)S(1)}, bf16[192,512]{1,0:T(8,128)(2,1)S(1)}, u32[]{:S(2)}, u32[]{:S(2)}) collective-permute-start(bf16[192,512]{1,0:T(8,128)(2,1)S(1)} %constant_dynamic-update-slice_fusion.refs_0_), channel_id=1, source_target_pairs={{0,192},{8,200},{16,208},{24,216},{32,224},{40,232},{48,240},{56,2... | collective-permute-start | bytes 589832 | tf_op jit(solution)/shard_map/ppermute | solution.py:193
  15.0 9.4 %collective-permute-start.4 = (bf16[192,512]{1,0:T(8,128)(2,1)S(1)}, bf16[192,512]{1,0:T(8,128)(2,1)}, u32[]{:S(2)}, u32[]{:S(2)}) collective-permute-start(bf16[192,512]{1,0:T(8,128)(2,1)S(1)} %constant_dynamic-update-slice_fusion.refs_0_), channel_id=1, source_target_pairs={{0,128},{8,136},{16,144},{24,152},{32,160},{40,168},{48,176},{56,1... | collective-permute-start | bytes 589832 | tf_op jit(solution)/shard_map/ppermute | solution.py:193
  15.6 10.6 %collective-permute-start.3 = (bf16[192,512]{1,0:T(8,128)(2,1)S(1)}, bf16[192,512]{1,0:T(8,128)(2,1)}, u32[]{:S(2)}, u32[]{:S(2)}) collective-permute-start(bf16[192,512]{1,0:T(8,128)(2,1)S(1)} %constant_dynamic-update-slice_fusion.refs_0_), channel_id=1, source_target_pairs={{0,64},{8,72},{16,80},{24,88},{32,96},{40,104},{48,112},{56,120},{... | collective-permute-start | bytes 589832 | tf_op jit(solution)/shard_map/ppermute | solution.py:193
  15.8 11.1 %collective-permute-start.6 = (bf16[192,512]{1,0:T(8,128)(2,1)S(1)}, bf16[192,512]{1,0:T(8,128)(2,1)S(1)}, u32[]{:S(2)}, u32[]{:S(2)}) collective-permute-start(bf16[192,512]{1,0:T(8,128)(2,1)S(1)} %constant_dynamic-update-slice_fusion.refs_0_), channel_id=1, source_target_pairs={{0,8},{8,0},{16,24},{24,16},{32,40},{40,32},{48,56},{56,48},{64,72... | collective-permute-start | bytes 589832 | tf_op jit(solution)/shard_map/ppermute | solution.py:193
  23.2 3.8 %collective-permute-start.9 = (bf16[192,512]{1,0:T(8,128)(2,1)S(1)}, bf16[192,512]{1,0:T(8,128)(2,1)S(1)}, u32[]{:S(2)}, u32[]{:S(2)}) collective-permute-start(bf16[192,512]{1,0:T(8,128)(2,1)S(1)} %collective-permute-done.5.refs_3_), channel_id=1, source_target_pairs={{0,8},{8,0},{16,24},{24,16},{32,40},{40,32},{48,56},{56,48},{64,72... | collective-permute-start | bytes 589832 | tf_op jit(solution)/shard_map/ppermute | solution.py:193
  24.4 3.0 %collective-permute-start.8 = (bf16[192,512]{1,0:T(8,128)(2,1)}, bf16[192,512]{1,0:T(8,128)(2,1)S(1)}, u32[]{:S(2)}, u32[]{:S(2)}) collective-permute-start(bf16[192,512]{1,0:T(8,128)(2,1)} %collective-permute-done.4.refs_2_), channel_id=1, source_target_pairs={{0,8},{8,0},{16,24},{24,16},{32,40},{40,32},{48,56},{56,48},{64,72... | collective-permute-start | bytes 589832 | tf_op jit(solution)/shard_map/ppermute | solution.py:193
  26.1 1.7 %collective-permute-start.7 = (bf16[192,512]{1,0:T(8,128)(2,1)}, bf16[192,512]{1,0:T(8,128)(2,1)S(1)}, u32[]{:S(2)}, u32[]{:S(2)}) collective-permute-start(bf16[192,512]{1,0:T(8,128)(2,1)} %collective-permute-done.3.refs_1_), channel_id=1, source_target_pairs={{0,8},{8,0},{16,24},{24,16},{32,40},{40,32},{48,56},{56,48},{64,72... | collective-permute-start | bytes 589832 | tf_op jit(solution)/shard_map/ppermute | solution.py:193
  37.6 12.1 %collective-permute-start.10 = (f32[64,256]{1,0:T(8,128)S(1)}, f32[64,256]{1,0:T(8,128)S(1)}, u32[]{:S(2)}, u32[]{:S(2)}) collective-permute-start(f32[64,256]{1,0:T(8,128)S(1)} %get-tuple-element.12), channel_id=1, source_target_pairs={{1,0},{2,1},{3,2},{4,3},{5,4},{6,5},{7,6},{9,8},{10,9},{11,10},{12... | collective-permute-start | bytes 196616 | tf_op jit(solution)/shard_map/ppermute | solution.py:206

commit v3 on v2

--- a/solution.py
+++ b/solution.py
@@ -14,9 +14,8 @@
 EXTRA = L + LAGS - 2
 HOLD = 128
 LAG_ROWS = 64
-VMEM_K1 = 20 << 20
-VMEM_K2 = 34 << 20
-GROUPS = 8
+VMEM_K1 = 8 << 20
+VMEM_K2 = 18 << 20
 
 
 def angles(samples, freqs, width):
@@ -47,7 +46,7 @@
     return high, (table - high.astype(np.float32)).astype(jnp.bfloat16)
 
 
-def template_kernel(step, freqs, lag_ref, record_ref, wave_hbm, forward_hbm, phase_hbm, out_hbm, own_ref, waves, forward, phases, out, sems, out_sems):
+def template_kernel(step, freqs, lag_ref, slot_ref, record_hbm, wave_hbm, forward_hbm, phase_hbm, out, own_ref, place_ref, waves, forward, phases, sems, own_sem):
     starts = range(0, wave_hbm.shape[0], step)
     loads = [pltpu.make_async_copy(forward_hbm, forward, sems.at[0]), pltpu.make_async_copy(phase_hbm, phases, sems.at[1])]
     for n, start in enumerate(starts):
@@ -55,8 +54,9 @@
         loads.append(pltpu.make_async_copy(wave_hbm.at[part], waves.at[part], sems.at[2 + n]))
     for load in loads:
         load.start()
-    own_ref[...] = record_ref[...]
-    stores = []
+    own = pltpu.make_async_copy(record_hbm, own_ref, own_sem)
+    own.start()
+    place_ref[...] = slot_ref[...]
     for n, start in enumerate(starts):
         for load in loads[:3] if n == 0 else loads[2 + n : 3 + n]:
             load.wait()
@@ -70,44 +70,58 @@
             h_cos, h_sin, c_theta, s_theta = dft[:, low], dft[:, high], phase[:, low], phase[:, high]
             out[pl.ds(start * 8 + j, step, stride=8), :] = h_cos * c_theta - h_sin * s_theta
             out[pl.ds(start * 8 + 4 + j, step, stride=8), :] = h_cos * s_theta + h_sin * c_theta
-        part = pl.ds(start * 8, step * 8)
-        stores.append(pltpu.make_async_copy(out.at[part], out_hbm.at[part], out_sems.at[n]))
-        stores[-1].start()
-    for store in stores:
-        store.wait()
-
-
-def template_spectra(waves, lags, records, forward, phase, freqs):
+    own.wait()
+
+
+def template_spectra(waves, lags, slots, records, forward, phase, freqs):
     count, length = waves.shape
     whole = pl.BlockSpec(memory_space=pltpu.VMEM)
     step = 512
     return pl.pallas_call(
         functools.partial(template_kernel, step, freqs),
-        in_specs=[whole] * 2 + [pl.BlockSpec(memory_space=pltpu.HBM)] * 3,
-        out_specs=[pl.BlockSpec(memory_space=pltpu.HBM), whole],
-        out_shape=[pltpu.HBM((count * 8, HOLD), jnp.float32), jax.ShapeDtypeStruct(records.shape, records.dtype)],
+        in_specs=[whole] * 2 + [pl.BlockSpec(memory_space=pltpu.HBM)] * 4,
+        out_specs=[whole] * 3,
+        out_shape=[
+            jax.ShapeDtypeStruct((count * 8, HOLD), jnp.float32),
+            jax.ShapeDtypeStruct(records.shape, records.dtype),
+            jax.ShapeDtypeStruct(slots.shape, slots.dtype),
+        ],
         scratch_shapes=[
             pltpu.VMEM(waves.shape, waves.dtype),
             pltpu.VMEM((length, 2 * freqs), forward.dtype),
             pltpu.VMEM(phase.shape, phase.dtype),
-            pltpu.VMEM((count * 8, HOLD), jnp.float32),
             pltpu.SemaphoreType.DMA((2 + count // step,)),
-            pltpu.SemaphoreType.DMA((count // step,)),
+            pltpu.SemaphoreType.DMA,
         ],
         compiler_params=pltpu.CompilerParams(vmem_limit_bytes=VMEM_K1),
         cost_estimate=pl.CostEstimate(flops=count * length * freqs * 4, bytes_accessed=count * 8 * HOLD * 4, transcendentals=0),
         name="template_spectra",
-    )(lags, records, *(pltpu.with_memory_space_constraint(a, pltpu.HBM) for a in (waves, forward[:length], phase)))
+    )(lags, slots, *(pltpu.with_memory_space_constraint(a, pltpu.HBM) for a in (records, waves, forward[:length], phase)))
+
+
+def join_kernel(*refs):
+    *parts, out = refs
+    at = 0
+    for part in parts:
+        out[pl.ds(at, part.shape[0]), :] = part[...]
+        at += part.shape[0]
+
+
+def join(parts):
+    rows = sum(part.shape[0] for part in parts)
+    whole = pl.BlockSpec(memory_space=pltpu.VMEM)
+    return pl.pallas_call(
+        join_kernel,
+        in_specs=[whole] * len(parts),
+        out_specs=whole,
+        out_shape=jax.ShapeDtypeStruct((rows, parts[0].shape[1]), parts[0].dtype),
+        compiler_params=pltpu.CompilerParams(vmem_limit_bytes=2 << 20),
+        name="join",
+    )(*parts)
 
 
 def detect_kernel(n_blocks, count, stations, freqs, slot_ref, *refs):
-    blocks, (q_hbm, forward_ref, high_ref, low_ref, main_ref, early_ref, table, acc, q, sems) = refs[:n_blocks], refs[n_blocks:]
-    share = count // GROUPS
-    loads = []
-    for g in range(GROUPS):
-        part = pl.ds(g * share * stations * 8, share * stations * 8)
-        loads.append(pltpu.make_async_copy(q_hbm.at[part], q.at[part], sems.at[g]))
-        loads[g].start()
+    blocks, (q, forward_ref, high_ref, low_ref, main_ref, early_ref, table, acc) = refs[:n_blocks], refs[n_blocks:]
     chunks = freqs // HOLD
     size = blocks[0].shape[0]
     for b, block in enumerate(blocks):
@@ -134,9 +148,7 @@
         acc[pl.ds(pl.multiple_of(t * 16 + 8, 8), 8), :] = second[0] + second[1]
         return carry
 
-    for g, load in enumerate(loads):
-        load.wait()
-        lax.fori_loop(g * share, (g + 1) * share, one, 0)
+    lax.fori_loop(0, count, one, 0)
     joint = jnp.concatenate(
         [
             acc[pl.ds(8 * part + j, count, stride=16), :] + acc[pl.ds(8 * part + 4 + j, count, stride=16), :]
@@ -159,9 +171,7 @@
     whole = pl.BlockSpec(memory_space=pltpu.VMEM)
     return pl.pallas_call(
         functools.partial(detect_kernel, len(blocks), count, stations, freqs),
-        in_specs=[pl.BlockSpec(memory_space=pltpu.SMEM)] + [whole] * len(blocks)
-        + [pl.BlockSpec(memory_space=pltpu.HBM)]
-        + [whole] * 3,
+        in_specs=[pl.BlockSpec(memory_space=pltpu.SMEM)] + [whole] * (len(blocks) + 4),
         out_specs=[whole, whole],
         out_shape=[
             jax.ShapeDtypeStruct((count, time_dev), jnp.float32),
@@ -170,13 +180,11 @@
         scratch_shapes=[
             pltpu.VMEM((rows * 16, HOLD), jnp.float32),
             pltpu.VMEM((count * 16, HOLD), jnp.float32),
-            pltpu.VMEM(q.shape, q.dtype),
-            pltpu.SemaphoreType.DMA((GROUPS,)),
         ],
         compiler_params=pltpu.CompilerParams(vmem_limit_bytes=VMEM_K2),
         cost_estimate=pl.CostEstimate(flops=rows * time_dev * freqs * 4, bytes_accessed=count * stations * 8 * HOLD * 4, transcendentals=0),
         name="detect",
-    )(slots, *blocks, pltpu.with_memory_space_constraint(q, pltpu.HBM), forward, high, low)
+    )(slots, *blocks, q, forward, high, low)
 
 
 def route(change):
@@ -192,15 +200,16 @@
     forward, phase, high, low = (jnp.asarray(t) for t in host_tables(time_dev))
     swap = lambda block, change: lax.ppermute(block, "tmpl", route(change))
 
-    q, own = template_spectra(templates.reshape(-1, length), moveouts.reshape(-1, HOLD), records, forward, phase, freqs)
-    line = [own] + [swap(records, (0, d, 0)) for d in (1, 2, 3)]
-    line = jnp.concatenate(line, axis=0)
-    plane = [line] + [swap(line, (d, 0, 0)) for d in (1, 2, 3)]
-    blocks = plane + [swap(block, (0, 0, 1)) for block in plane]
-
     apart = (channels // per) ^ lax.axis_index("tmpl")
     place = ((apart & 1) * 16 + (apart >> 1)) * per + channels % per
     slots = (place * 16).reshape(-1, stations)
+
+    q, own, slots = template_spectra(
+        templates.reshape(-1, length), moveouts.reshape(-1, HOLD), slots, records, forward, phase, freqs
+    )
+    line = join([own] + [swap(records, (0, d, 0)) for d in (1, 2, 3)])
+    plane = [line] + [swap(line, (d, 0, 0)) for d in (1, 2, 3)]
+    blocks = plane + [swap(block, (0, 0, 1)) for block in plane]
 
     main, early = detect(slots, blocks, q, forward, high, low, batches * count, stations, freqs, time_dev)
     earlier = lax.ppermute(early, "tm", [(i, i - 1) for i in range(1, lax.axis_size("tm"))])

time: 50.7 us -> 47.2 us (0.931)
  Pallas kernels: 17 us -> 13.9 us
  local copies, waits for them, and re-layouts: 1.67 us -> 0.85 us
  waiting for transfers between devices: 15.6 us -> 16.2 us
    pallas_call x1, Pallas kernels: 9.84 us -> 8.03 us  [detect(): pl.pallas_call(functools.partial(detect_kernel, len(blocks), count, stati...]
    pallas_call x1, Pallas kernels: 7.19 us -> 5.82 us  [template_spectra(): pl.pallas_call(functools.partial(template_kernel, step, freqs), in_specs=...]
    unnamed x11 -> x6, local copies, waits for them, and re-layouts: 0.83 us -> 0.02 us
    ppermute x10, waiting for transfers between devices: 5.84 us -> 6.44 us  [per_device(): swap = lambda block, change: lax.ppermute(block, 'tmpl', route(change))]
  transfers between devices with their start and end apart: 11 -> 11, of which waited for: 4 -> 4; matrix products, arithmetic and copies ran while one was open for 3% -> 3% of each run, Pallas kernels for 14% -> 12%
where the time goes in v3:
time: 47.2 us; the launch traced here: 46.9 us
  waiting for transfers between devices  16.2 us (34%)
  starting transfers between devices  14.4 us (31%)
  Pallas kernels  13.9 us (29%)
  other arithmetic  1.48 us (3%)
  local copies, waits for them, and re-layouts  0.85 us (2%)
    ppermute x10, starting transfers between devices, per_device(): swap = lambda block, change: lax.ppermute(block, 'tmpl', route(change))  12.1 us
    ppermute x1, waiting for transfers between devices, per_device(): lax.ppermute(early, 'tm', [(i, i - 1) for i in range(1, lax.axis_size('tm...  9.79 us
    pallas_call x1, Pallas kernels, detect(): pl.pallas_call(functools.partial(detect_kernel, len(blocks), count, stati...  8.03 us
    ppermute x10, waiting for transfers between devices, per_device(): swap = lambda block, change: lax.ppermute(block, 'tmpl', route(change))  6.44 us
    pallas_call x1, Pallas kernels, template_spectra(): pl.pallas_call(functools.partial(template_kernel, step, freqs), in_specs=...  5.82 us
    ppermute x1, starting transfers between devices, per_device(): lax.ppermute(early, 'tm', [(i, i - 1) for i in range(1, lax.axis_size('tm...  2.33 us
  transfers between devices with their start and end apart: 11, of which 4 were waited for; matrix products, arithmetic and copies ran while one was open for 3% of the time, Pallas kernels for 12%

profile of v3, /device:TPU:201, one launch (start us, length us, event | category | flops | bytes accessed | tf_op | source)
XLA Modules:
  0.0 46.9 jit_solution(12787957748685043739)
XLA Ops:
  0.0 0.7 %collective-permute-start = (bf16[48,512]{1,0:T(8,128)(2,1)}, bf16[48,512]{1,0:T(8,128)(2,1)S(1)}, u32[]{:S(2)}, u32[]{:S(2)}) collective-permute-start(bf16[48,512]{1,0:T(8,128)(2,1)} %record_hbm.1), channel_id=1, source_target_pairs={{0,16},{8,24},{16,0},{24,8},{32,48},{40,56},{48,32},{56,40},{64,80... | collective-permute-start | bytes 147464 | tf_op jit(solution)/shard_map/ppermute | solution.py:201
  0.7 0.7 %collective-permute-start.2 = (bf16[48,512]{1,0:T(8,128)(2,1)}, bf16[48,512]{1,0:T(8,128)(2,1)S(1)}, u32[]{:S(2)}, u32[]{:S(2)}) collective-permute-start(bf16[48,512]{1,0:T(8,128)(2,1)} %record_hbm.1), channel_id=1, source_target_pairs={{0,48},{8,56},{16,32},{24,40},{32,16},{40,24},{48,0},{56,8},{64,11... | collective-permute-start | bytes 147464 | tf_op jit(solution)/shard_map/ppermute | solution.py:201
  1.5 2.1 %collective-permute-start.1 = (bf16[48,512]{1,0:T(8,128)(2,1)}, bf16[48,512]{1,0:T(8,128)(2,1)S(1)}, u32[]{:S(2)}, u32[]{:S(2)}) collective-permute-start(bf16[48,512]{1,0:T(8,128)(2,1)} %record_hbm.1), channel_id=1, source_target_pairs={{0,32},{8,40},{16,48},{24,56},{32,0},{40,8},{48,16},{56,24},{64,96... | collective-permute-start | bytes 147464 | tf_op jit(solution)/shard_map/ppermute | solution.py:201
  3.5 0.8 %reshape.12.lag_ref = s32[24,128]{1,0:T(8,128)S(1)} reshape(s32[2,32,48]{2,1,0:T(8,128)} %param.11) | data formatting | bytes 24576 | tf_op jit(solution)/shard_map/reshape | solution.py:208
  4.4 0.8 %fusion.2 = s32[2,32,48]{2,1,0:T(8,128)S(1)} fusion(s32[2,32,48]{2,1,0:T(8,128)} %param.10, s32[]{:T(128)S(6)} %axis_index.15), kind=kLoop, calls=%fused_computation.5 | loop fusion | flops 61440 | bytes 24580 | tf_op jit(solution)/shard_map/mul | solution.py:205
  5.2 0.0 copy-start
  5.2 0.0 copy-start.1
  5.2 0.0 copy-start.2
  5.2 5.8 %template_spectra.1 = (f32[24576,128]{1,0:T(8,128)S(1)}, bf16[48,512]{1,0:T(8,128)(2,1)S(1)}, s32[64,48]{1,0:T(8,128)S(1)}) custom-call(s32[24,128]{1,0:T(8,128)S(1)} %reshape.12.lag_ref, s32[64,48]{1,0:T(8,128)S(1)} %bitcast.3, bf16[48,512]{1,0:T(8,128)(2,1)} %record_hbm.1, bf16[3072,200]{1,0:T(8,128)(2,1)} %bitcast.4, ...), custom_call_target="tpu_custom_call" | custom-call | flops 943718400 | bytes 12582912 | tf_op jit(solution)/shard_map/template_spectra/pallas_call | solution.py:80
  11.1 0.0 collective-permute-done.refs_1_
  11.1 0.0 collective-permute-done.2.refs_3_
  11.1 0.0 collective-permute-done.1.refs_2_
  11.1 2.6 %collective-permute-start.5 = (bf16[192,512]{1,0:T(8,128)(2,1)S(1)}, bf16[192,512]{1,0:T(8,128)(2,1)S(1)}, u32[]{:S(2)}, u32[]{:S(2)}) collective-permute-start(bf16[192,512]{1,0:T(8,128)(2,1)S(1)} %join.1.refs_0_), channel_id=1, source_target_pairs={{0,192},{8,200},{16,208},{24,216},{32,224},{40,232},{48,240},{56,2... | collective-permute-start | bytes 589832 | tf_op jit(solution)/shard_map/ppermute | solution.py:201
  13.7 0.5 %collective-permute-start.4 = (bf16[192,512]{1,0:T(8,128)(2,1)S(1)}, bf16[192,512]{1,0:T(8,128)(2,1)S(1)}, u32[]{:S(2)}, u32[]{:S(2)}) collective-permute-start(bf16[192,512]{1,0:T(8,128)(2,1)S(1)} %join.1.refs_0_), channel_id=1, source_target_pairs={{0,128},{8,136},{16,144},{24,152},{32,160},{40,168},{48,176},{56,1... | collective-permute-start | bytes 589832 | tf_op jit(solution)/shard_map/ppermute | solution.py:201
  14.2 0.3 collective-permute-start.3
  14.4 2.4 %collective-permute-start.6 = (bf16[192,512]{1,0:T(8,128)(2,1)S(1)}, bf16[192,512]{1,0:T(8,128)(2,1)S(1)}, u32[]{:S(2)}, u32[]{:S(2)}) collective-permute-start(bf16[192,512]{1,0:T(8,128)(2,1)S(1)} %join.1.refs_0_), channel_id=1, source_target_pairs={{0,8},{8,0},{16,24},{24,16},{32,40},{40,32},{48,56},{56,48},{64,72... | collective-permute-start | bytes 589832 | tf_op jit(solution)/shard_map/ppermute | solution.py:201
  16.8 5.0 %collective-permute-done.5.refs_3_ = bf16[192,512]{1,0:T(8,128)(2,1)S(1)} collective-permute-done((bf16[192,512]{1,0:T(8,128)(2,1)S(1)}, bf16[192,512]{1,0:T(8,128)(2,1)S(1)}, u32[]{:S(2)}, u32[]{:S(2)}) %collective-permute-start.5) | collective-permute-done | bytes 196640 | tf_op jit(solution)/shard_map/ppermute | solution.py:201
  21.8 1.2 %collective-permute-start.9 = (bf16[192,512]{1,0:T(8,128)(2,1)S(1)}, bf16[192,512]{1,0:T(8,128)(2,1)S(1)}, u32[]{:S(2)}, u32[]{:S(2)}) collective-permute-start(bf16[192,512]{1,0:T(8,128)(2,1)S(1)} %collective-permute-done.5.refs_3_), channel_id=1, source_target_pairs={{0,8},{8,0},{16,24},{24,16},{32,40},{40,32},{48,56},{56,48},{64,72... | collective-permute-start | bytes 589832 | tf_op jit(solution)/shard_map/ppermute | solution.py:201
  23.1 0.0 collective-permute-done.4.refs_2_
  23.1 1.6 %collective-permute-start.8 = (bf16[192,512]{1,0:T(8,128)(2,1)S(1)}, bf16[192,512]{1,0:T(8,128)(2,1)S(1)}, u32[]{:S(2)}, u32[]{:S(2)}) collective-permute-start(bf16[192,512]{1,0:T(8,128)(2,1)S(1)} %collective-permute-done.4.refs_2_), channel_id=1, source_target_pairs={{0,8},{8,0},{16,24},{24,16},{32,40},{40,32},{48,56},{56,48},{64,72... | collective-permute-start | bytes 589832 | tf_op jit(solution)/shard_map/ppermute | solution.py:201
  24.6 0.0 collective-permute-done.3.refs_1_
  24.7 0.0 collective-permute-start.7
  24.7 0.0 collective-permute-done.6.refs_4_
  24.7 0.0 collective-permute-done.9.refs_7_
  24.7 1.0 %collective-permute-done.8.refs_6_ = bf16[192,512]{1,0:T(8,128)(2,1)S(1)} collective-permute-done((bf16[192,512]{1,0:T(8,128)(2,1)S(1)}, bf16[192,512]{1,0:T(8,128)(2,1)S(1)}, u32[]{:S(2)}, u32[]{:S(2)}) %collective-permute-start.8) | collective-permute-done | bytes 196640 | tf_op jit(solution)/shard_map/ppermute | solution.py:201
  25.7 0.4 collective-permute-done.7.refs_5_
  26.1 0.0 copy-done
  26.1 0.0 copy-done.2
  26.1 8.0 %detect.1 = (f32[64,512]{1,0:T(8,128)S(1)}, f32[64,256]{1,0:T(8,128)S(1)}) custom-call(s32[64,48]{1,0:T(8,128)S(1)} %get-tuple-element.10.slot_ref, bf16[192,512]{1,0:T(8,128)(2,1)S(1)} %join.1.refs_0_, bf16[192,512]{1,0:T(8,128)(2,1)S(1)} %collective-permute-done.3.refs_1_, bf16[192,512]{1,0:T(8,128)(2,1)S(1)} %collective-permute-done.4.refs_2_, ...), custom_call_target="tpu_custom_call" | custom-call | flops 1207959552 | bytes 12582912 | tf_op jit(solution)/shard_map/detect/pallas_call | solution.py:172
  34.1 2.3 %collective-permute-start.10 = (f32[64,256]{1,0:T(8,128)S(1)}, f32[64,256]{1,0:T(8,128)S(1)}, u32[]{:S(2)}, u32[]{:S(2)}) collective-permute-start(f32[64,256]{1,0:T(8,128)S(1)} %get-tuple-element.14), channel_id=1, source_target_pairs={{1,0},{2,1},{3,2},{4,3},{5,4},{6,5},{7,6},{9,8},{10,9},{11,10},{12... | collective-permute-start | bytes 196616 | tf_op jit(solution)/shard_map/ppermute | solution.py:215
  36.5 9.8 %collective-permute-done.10 = f32[64,256]{1,0:T(8,128)S(1)} collective-permute-done((f32[64,256]{1,0:T(8,128)S(1)}, f32[64,256]{1,0:T(8,128)S(1)}, u32[]{:S(2)}, u32[]{:S(2)}) %collective-permute-start.10) | collective-permute-done | bytes 65568 | tf_op jit(solution)/shard_map/ppermute | solution.py:215
  46.3 0.7 %pad_add_fusion = f32[64,512]{1,0:T(8,128)} fusion(f32[64,512]{1,0:T(8,128)S(1)} %get-tuple-element.13, f32[64,256]{1,0:T(8,128)S(1)} %collective-permute-done.10), kind=kLoop, calls=%fused_computation | loop fusion | flops 32768 | bytes 327680 | tf_op jit(solution)/shard_map/add | solution.py:216
  (2 shorter events, 0.0 us)
Async XLA Ops:
  0.0 11.1 %collective-permute-start = (bf16[48,512]{1,0:T(8,128)(2,1)}, bf16[48,512]{1,0:T(8,128)(2,1)S(1)}, u32[]{:S(2)}, u32[]{:S(2)}) collective-permute-start(bf16[48,512]{1,0:T(8,128)(2,1)} %record_hbm.1), channel_id=1, source_target_pairs={{0,16},{8,24},{16,0},{24,8},{32,48},{40,56},{48,32},{56,40},{64,80... | collective-permute-start | bytes 147464 | tf_op jit(solution)/shard_map/ppermute | solution.py:201
  0.7 10.3 %collective-permute-start.2 = (bf16[48,512]{1,0:T(8,128)(2,1)}, bf16[48,512]{1,0:T(8,128)(2,1)S(1)}, u32[]{:S(2)}, u32[]{:S(2)}) collective-permute-start(bf16[48,512]{1,0:T(8,128)(2,1)} %record_hbm.1), channel_id=1, source_target_pairs={{0,48},{8,56},{16,32},{24,40},{32,16},{40,24},{48,0},{56,8},{64,11... | collective-permute-start | bytes 147464 | tf_op jit(solution)/shard_map/ppermute | solution.py:201
  1.5 9.6 %collective-permute-start.1 = (bf16[48,512]{1,0:T(8,128)(2,1)}, bf16[48,512]{1,0:T(8,128)(2,1)S(1)}, u32[]{:S(2)}, u32[]{:S(2)}) collective-permute-start(bf16[48,512]{1,0:T(8,128)(2,1)} %record_hbm.1), channel_id=1, source_target_pairs={{0,32},{8,40},{16,48},{24,56},{32,0},{40,8},{48,16},{56,24},{64,96... | collective-permute-start | bytes 147464 | tf_op jit(solution)/shard_map/ppermute | solution.py:201
  5.2 20.9 %copy-start = (bf16[768,768]{1,0:T(8,128)(2,1)S(1)}, bf16[768,768]{1,0:T(8,128)(2,1)}, u32[]{:S(2)}) copy-start(bf16[768,768]{1,0:T(8,128)(2,1)} %constant.44.clone.refs_11_) | copy-start | bytes 3538948
  5.2 20.9 %copy-start.1 = (bf16[768,768]{1,0:T(8,128)(2,1)S(1)}, bf16[768,768]{1,0:T(8,128)(2,1)}, u32[]{:S(2)}) copy-start(bf16[768,768]{1,0:T(8,128)(2,1)} %constant.43.clone.refs_10_) | copy-start | bytes 3538948
  5.2 20.9 %copy-start.2 = (bf16[512,768]{1,0:T(8,128)(2,1)S(1)}, bf16[512,768]{1,0:T(8,128)(2,1)}, u32[]{:S(2)}) copy-start(bf16[512,768]{1,0:T(8,128)(2,1)} %constant.41.clone.refs_9_) | copy-start | bytes 2359300
  11.1 10.7 %collective-permute-start.5 = (bf16[192,512]{1,0:T(8,128)(2,1)S(1)}, bf16[192,512]{1,0:T(8,128)(2,1)S(1)}, u32[]{:S(2)}, u32[]{:S(2)}) collective-permute-start(bf16[192,512]{1,0:T(8,128)(2,1)S(1)} %join.1.refs_0_), channel_id=1, source_target_pairs={{0,192},{8,200},{16,208},{24,216},{32,224},{40,232},{48,240},{56,2... | collective-permute-start | bytes 589832 | tf_op jit(solution)/shard_map/ppermute | solution.py:201
  13.7 9.4 %collective-permute-start.4 = (bf16[192,512]{1,0:T(8,128)(2,1)S(1)}, bf16[192,512]{1,0:T(8,128)(2,1)S(1)}, u32[]{:S(2)}, u32[]{:S(2)}) collective-permute-start(bf16[192,512]{1,0:T(8,128)(2,1)S(1)} %join.1.refs_0_), channel_id=1, source_target_pairs={{0,128},{8,136},{16,144},{24,152},{32,160},{40,168},{48,176},{56,1... | collective-permute-start | bytes 589832 | tf_op jit(solution)/shard_map/ppermute | solution.py:201
  14.2 10.5 %collective-permute-start.3 = (bf16[192,512]{1,0:T(8,128)(2,1)S(1)}, bf16[192,512]{1,0:T(8,128)(2,1)S(1)}, u32[]{:S(2)}, u32[]{:S(2)}) collective-permute-start(bf16[192,512]{1,0:T(8,128)(2,1)S(1)} %join.1.refs_0_), channel_id=1, source_target_pairs={{0,64},{8,72},{16,80},{24,88},{32,96},{40,104},{48,112},{56,120},{... | collective-permute-start | bytes 589832 | tf_op jit(solution)/shard_map/ppermute | solution.py:201
  14.4 10.2 %collective-permute-start.6 = (bf16[192,512]{1,0:T(8,128)(2,1)S(1)}, bf16[192,512]{1,0:T(8,128)(2,1)S(1)}, u32[]{:S(2)}, u32[]{:S(2)}) collective-permute-start(bf16[192,512]{1,0:T(8,128)(2,1)S(1)} %join.1.refs_0_), channel_id=1, source_target_pairs={{0,8},{8,0},{16,24},{24,16},{32,40},{40,32},{48,56},{56,48},{64,72... | collective-permute-start | bytes 589832 | tf_op jit(solution)/shard_map/ppermute | solution.py:201
  21.8 2.9 %collective-permute-start.9 = (bf16[192,512]{1,0:T(8,128)(2,1)S(1)}, bf16[192,512]{1,0:T(8,128)(2,1)S(1)}, u32[]{:S(2)}, u32[]{:S(2)}) collective-permute-start(bf16[192,512]{1,0:T(8,128)(2,1)S(1)} %collective-permute-done.5.refs_3_), channel_id=1, source_target_pairs={{0,8},{8,0},{16,24},{24,16},{32,40},{40,32},{48,56},{56,48},{64,72... | collective-permute-start | bytes 589832 | tf_op jit(solution)/shard_map/ppermute | solution.py:201
  23.1 2.7 %collective-permute-start.8 = (bf16[192,512]{1,0:T(8,128)(2,1)S(1)}, bf16[192,512]{1,0:T(8,128)(2,1)S(1)}, u32[]{:S(2)}, u32[]{:S(2)}) collective-permute-start(bf16[192,512]{1,0:T(8,128)(2,1)S(1)} %collective-permute-done.4.refs_2_), channel_id=1, source_target_pairs={{0,8},{8,0},{16,24},{24,16},{32,40},{40,32},{48,56},{56,48},{64,72... | collective-permute-start | bytes 589832 | tf_op jit(solution)/shard_map/ppermute | solution.py:201
  24.7 1.4 %collective-permute-start.7 = (bf16[192,512]{1,0:T(8,128)(2,1)S(1)}, bf16[192,512]{1,0:T(8,128)(2,1)S(1)}, u32[]{:S(2)}, u32[]{:S(2)}) collective-permute-start(bf16[192,512]{1,0:T(8,128)(2,1)S(1)} %collective-permute-done.3.refs_1_), channel_id=1, source_target_pairs={{0,8},{8,0},{16,24},{24,16},{32,40},{40,32},{48,56},{56,48},{64,72... | collective-permute-start | bytes 589832 | tf_op jit(solution)/shard_map/ppermute | solution.py:201
  34.1 12.1 %collective-permute-start.10 = (f32[64,256]{1,0:T(8,128)S(1)}, f32[64,256]{1,0:T(8,128)S(1)}, u32[]{:S(2)}, u32[]{:S(2)}) collective-permute-start(f32[64,256]{1,0:T(8,128)S(1)} %get-tuple-element.14), channel_id=1, source_target_pairs={{1,0},{2,1},{3,2},{4,3},{5,4},{6,5},{7,6},{9,8},{10,9},{11,10},{12... | collective-permute-start | bytes 196616 | tf_op jit(solution)/shard_map/ppermute | solution.py:215

commit v4 on v3

--- a/solution.py
+++ b/solution.py
@@ -14,8 +14,8 @@
 EXTRA = L + LAGS - 2
 HOLD = 128
 LAG_ROWS = 64
-VMEM_K1 = 8 << 20
-VMEM_K2 = 18 << 20
+VMEM_K1 = 20 << 20
+VMEM_K2 = 24 << 20
 
 
 def angles(samples, freqs, width):
@@ -46,20 +46,31 @@
     return high, (table - high.astype(np.float32)).astype(jnp.bfloat16)
 
 
-def template_kernel(step, freqs, lag_ref, slot_ref, record_hbm, wave_hbm, forward_hbm, phase_hbm, out, own_ref, place_ref, waves, forward, phases, sems, own_sem):
-    starts = range(0, wave_hbm.shape[0], step)
-    loads = [pltpu.make_async_copy(forward_hbm, forward, sems.at[0]), pltpu.make_async_copy(phase_hbm, phases, sems.at[1])]
-    for n, start in enumerate(starts):
-        part = pl.ds(start, step)
-        loads.append(pltpu.make_async_copy(wave_hbm.at[part], waves.at[part], sems.at[2 + n]))
-    for load in loads:
-        load.start()
-    own = pltpu.make_async_copy(record_hbm, own_ref, own_sem)
-    own.start()
-    place_ref[...] = slot_ref[...]
-    for n, start in enumerate(starts):
-        for load in loads[:3] if n == 0 else loads[2 + n : 3 + n]:
-            load.wait()
+def load_kernel(count, *refs):
+    sources, targets, sems = refs[:count], refs[count:-1], refs[-1]
+    copies = [pltpu.make_async_copy(src, dst, sems.at[n]) for n, (src, dst) in enumerate(zip(sources, targets))]
+    for copy in copies:
+        copy.start()
+    for copy in copies:
+        copy.wait()
+
+
+def load(arrays):
+    return pl.pallas_call(
+        functools.partial(load_kernel, len(arrays)),
+        in_specs=[pl.BlockSpec(memory_space=pltpu.HBM)] * len(arrays),
+        out_specs=[pl.BlockSpec(memory_space=pltpu.VMEM)] * len(arrays),
+        out_shape=[jax.ShapeDtypeStruct(a.shape, a.dtype) for a in arrays],
+        scratch_shapes=[pltpu.SemaphoreType.DMA((len(arrays),))],
+        compiler_params=pltpu.CompilerParams(vmem_limit_bytes=8 << 20),
+        name="load",
+    )(*(pltpu.with_memory_space_constraint(a, pltpu.HBM) for a in arrays))
+
+
+def template_kernel(step, freqs, lag_ref, slot_ref, line_ref, waves, forward, phases, out, line_out, slot_out):
+    line_out[...] = line_ref[...]
+    slot_out[...] = slot_ref[...]
+    for start in range(0, waves.shape[0], step):
         lag = jnp.concatenate([lag_ref[pl.ds((start + at) // HOLD, 1), :] for at in range(0, step, HOLD)], axis=1)
         lag_row = lax.broadcasted_iota(jnp.int32, (2 * LAG_ROWS, step), 0) & (LAG_ROWS - 1)
         chosen = (lag_row == lag).astype(jnp.float32).astype(jnp.bfloat16)
@@ -70,33 +81,24 @@
             h_cos, h_sin, c_theta, s_theta = dft[:, low], dft[:, high], phase[:, low], phase[:, high]
             out[pl.ds(start * 8 + j, step, stride=8), :] = h_cos * c_theta - h_sin * s_theta
             out[pl.ds(start * 8 + 4 + j, step, stride=8), :] = h_cos * s_theta + h_sin * c_theta
-    own.wait()
-
-
-def template_spectra(waves, lags, slots, records, forward, phase, freqs):
+
+
+def template_spectra(lags, slots, line, waves, forward, phase, freqs):
     count, length = waves.shape
     whole = pl.BlockSpec(memory_space=pltpu.VMEM)
-    step = 512
-    return pl.pallas_call(
-        functools.partial(template_kernel, step, freqs),
-        in_specs=[whole] * 2 + [pl.BlockSpec(memory_space=pltpu.HBM)] * 4,
+    return pl.pallas_call(
+        functools.partial(template_kernel, 512, freqs),
+        in_specs=[whole] * 6,
         out_specs=[whole] * 3,
         out_shape=[
             jax.ShapeDtypeStruct((count * 8, HOLD), jnp.float32),
-            jax.ShapeDtypeStruct(records.shape, records.dtype),
+            jax.ShapeDtypeStruct(line.shape, line.dtype),
             jax.ShapeDtypeStruct(slots.shape, slots.dtype),
-        ],
-        scratch_shapes=[
-            pltpu.VMEM(waves.shape, waves.dtype),
-            pltpu.VMEM((length, 2 * freqs), forward.dtype),
-            pltpu.VMEM(phase.shape, phase.dtype),
-            pltpu.SemaphoreType.DMA((2 + count // step,)),
-            pltpu.SemaphoreType.DMA,
         ],
         compiler_params=pltpu.CompilerParams(vmem_limit_bytes=VMEM_K1),
         cost_estimate=pl.CostEstimate(flops=count * length * freqs * 4, bytes_accessed=count * 8 * HOLD * 4, transcendentals=0),
         name="template_spectra",
-    )(lags, slots, *(pltpu.with_memory_space_constraint(a, pltpu.HBM) for a in (records, waves, forward[:length], phase)))
+    )(lags, slots, line, waves, forward, phase)
 
 
 def join_kernel(*refs):
@@ -127,34 +129,27 @@
     for b, block in enumerate(blocks):
         dft = jnp.dot(block[...], forward_ref[...], preferred_element_type=jnp.float32)
         for j in range(chunks):
-            real = dft[:, j * HOLD : (j + 1) * HOLD]
-            imag = dft[:, freqs + j * HOLD : freqs + (j + 1) * HOLD]
-            start = b * size * 16
-            table[pl.ds(start + j, size, stride=16), :] = real
-            table[pl.ds(start + 4 + j, size, stride=16), :] = imag
-            table[pl.ds(start + 8 + j, size, stride=16), :] = imag
-            table[pl.ds(start + 12 + j, size, stride=16), :] = -real
+            start = b * size * 8
+            table[pl.ds(start + j, size, stride=8), :] = dft[:, j * HOLD : (j + 1) * HOLD]
+            table[pl.ds(start + 4 + j, size, stride=8), :] = dft[:, freqs + j * HOLD : freqs + (j + 1) * HOLD]
 
     def one(t, carry):
         first = [jnp.zeros((8, HOLD), jnp.float32)] * 2
         second = list(first)
         weights = q.at[pl.ds(pl.multiple_of(t * stations * 8, stations * 8), stations * 8), :]
         for k in range(stations):
-            slot = pl.multiple_of(slot_ref[t, k], 16)
+            record = table[pl.ds(pl.multiple_of(slot_ref[t, k], 8), 8), :]
             weight = weights[k * 8 : k * 8 + 8, :]
-            first[k % 2] += weight * table[pl.ds(slot, 8), :]
-            second[k % 2] += weight * table[pl.ds(slot + 8, 8), :]
+            first[k % 2] += weight * record
+            second[k % 2] += weight * pltpu.roll(record, 4, 0)
         acc[pl.ds(pl.multiple_of(t * 16, 16), 8), :] = first[0] + first[1]
         acc[pl.ds(pl.multiple_of(t * 16 + 8, 8), 8), :] = second[0] + second[1]
         return carry
 
     lax.fori_loop(0, count, one, 0)
     joint = jnp.concatenate(
-        [
-            acc[pl.ds(8 * part + j, count, stride=16), :] + acc[pl.ds(8 * part + 4 + j, count, stride=16), :]
-            for part in range(2)
-            for j in range(chunks)
-        ],
+        [acc[pl.ds(j, count, stride=16), :] + acc[pl.ds(4 + j, count, stride=16), :] for j in range(chunks)]
+        + [acc[pl.ds(8 + j, count, stride=16), :] - acc[pl.ds(12 + j, count, stride=16), :] for j in range(chunks)],
         axis=1,
     )
     top = joint.astype(jnp.bfloat16)
@@ -178,7 +173,7 @@
             jax.ShapeDtypeStruct((count, time_dev // 2), jnp.float32),
         ],
         scratch_shapes=[
-            pltpu.VMEM((rows * 16, HOLD), jnp.float32),
+            pltpu.VMEM((rows * 8, HOLD), jnp.float32),
             pltpu.VMEM((count * 16, HOLD), jnp.float32),
         ],
         compiler_params=pltpu.CompilerParams(vmem_limit_bytes=VMEM_K2),
@@ -202,14 +197,13 @@
 
     apart = (channels // per) ^ lax.axis_index("tmpl")
     place = ((apart & 1) * 16 + (apart >> 1)) * per + channels % per
-    slots = (place * 16).reshape(-1, stations)
-
-    q, own, slots = template_spectra(
-        templates.reshape(-1, length), moveouts.reshape(-1, HOLD), slots, records, forward, phase, freqs
-    )
+    slots = (place * 8).reshape(-1, stations)
+
+    own, waves, head, phase = load([records, templates.reshape(-1, length), forward[:length], phase])
     line = join([own] + [swap(records, (0, d, 0)) for d in (1, 2, 3)])
-    plane = [line] + [swap(line, (d, 0, 0)) for d in (1, 2, 3)]
-    blocks = plane + [swap(block, (0, 0, 1)) for block in plane]
+    plane = [swap(line, (d, 0, 0)) for d in (1, 2, 3)]
+    q, line_q, slots = template_spectra(moveouts.reshape(-1, HOLD), slots, line, waves, head, phase, freqs)
+    blocks = [line] + plane + [swap(block, (0, 0, 1)) for block in [line_q] + plane]
 
     main, early = detect(slots, blocks, q, forward, high, low, batches * count, stations, freqs, time_dev)
     earlier = lax.ppermute(early, "tm", [(i, i - 1) for i in range(1, lax.axis_size("tm"))])

time: 47.2 us -> 43.3 us (0.917)
  the two profiles are of different devices: /device:TPU:201 before, /device:TPU:1 now
where the time goes in v4:
time: 43.3 us; the launch traced here: 43.2 us
  starting transfers between devices  18.8 us (43%)
  waiting for transfers between devices  12.1 us (28%)
  Pallas kernels  11.4 us (26%)
  other arithmetic  0.72 us (2%)
    ppermute x10, starting transfers between devices, per_device(): swap = lambda block, change: lax.ppermute(block, 'tmpl', route(change))  17.5 us
    ppermute x1, waiting for transfers between devices, per_device(): lax.ppermute(early, 'tm', [(i, i - 1) for i in range(1, lax.axis_size('tm...  7.62 us
    pallas_call x1, Pallas kernels, detect(): pl.pallas_call(functools.partial(detect_kernel, len(blocks), count, stati...  6.16 us
    ppermute x10, waiting for transfers between devices, per_device(): swap = lambda block, change: lax.ppermute(block, 'tmpl', route(change))  4.46 us
    pallas_call x1, Pallas kernels, template_spectra(): pl.pallas_call(functools.partial(template_kernel, 512, freqs), in_specs=[...  3.72 us
    pallas_call x1, Pallas kernels, load(): pl.pallas_call(functools.partial(load_kernel, len(arrays)), in_specs=[pl....  1.56 us
    ppermute x1, starting transfers between devices, per_device(): lax.ppermute(early, 'tm', [(i, i - 1) for i in range(1, lax.axis_size('tm...  1.29 us
  transfers between devices with their start and end apart: 11, of which 4 were waited for; matrix products, arithmetic and copies ran while one was open for 0% of the time, Pallas kernels for 12%

profile of v4, /device:TPU:1, one launch (start us, length us, event | category | flops | bytes accessed | tf_op | source)
XLA Modules:
  0.0 43.2 jit_solution(15028978891102056652)
XLA Ops:
  0.0 2.5 %collective-permute-start = (bf16[48,512]{1,0:T(8,128)(2,1)}, bf16[48,512]{1,0:T(8,128)(2,1)S(1)}, u32[]{:S(2)}, u32[]{:S(2)}) collective-permute-start(bf16[48,512]{1,0:T(8,128)(2,1)} %refs_0_.1), channel_id=1, source_target_pairs={{0,16},{8,24},{16,0},{24,8},{32,48},{40,56},{48,32},{56,40},{64,80... | collective-permute-start | bytes 147464 | tf_op jit(solution)/shard_map/ppermute | solution.py:196
  2.5 3.0 %collective-permute-start.1 = (bf16[48,512]{1,0:T(8,128)(2,1)}, bf16[48,512]{1,0:T(8,128)(2,1)S(1)}, u32[]{:S(2)}, u32[]{:S(2)}) collective-permute-start(bf16[48,512]{1,0:T(8,128)(2,1)} %refs_0_.1), channel_id=1, source_target_pairs={{0,32},{8,40},{16,48},{24,56},{32,0},{40,8},{48,16},{56,24},{64,96... | collective-permute-start | bytes 147464 | tf_op jit(solution)/shard_map/ppermute | solution.py:196
  5.5 0.0 collective-permute-start.2
  5.5 1.6 %load.1 = (bf16[48,512]{1,0:T(8,128)(2,1)S(1)}, bf16[3072,200]{1,0:T(8,128)(2,1)S(1)}, bf16[200,768]{1,0:T(8,128)(2,1)S(1)}, bf16[128,768]{1,0:T(8,128)(2,1)S(1)}) custom-call(bf16[48,512]{1,0:T(8,128)(2,1)} %refs_0_.1, bf16[3072,200]{1,0:T(8,128)(2,1)} %bitcast.4, bf16[200,768]{1,0:T(8,128)(2,1)} %constant.50.refs_2_, bf16[128,768]{1,0:T(8,128)(2,1)} %constant.44.clone.refs_3_), custom_call_target="tpu_custom_call" | custom-call | tf_op jit(solution)/shard_map/load/pallas_call | solution.py:59
  7.0 0.0 collective-permute-done.refs_1_
  7.0 0.7 %collective-permute-done.1.refs_2_ = bf16[48,512]{1,0:T(8,128)(2,1)S(1)} collective-permute-done((bf16[48,512]{1,0:T(8,128)(2,1)}, bf16[48,512]{1,0:T(8,128)(2,1)S(1)}, u32[]{:S(2)}, u32[]{:S(2)}) %collective-permute-start.1) | collective-permute-done | bytes 49184 | tf_op jit(solution)/shard_map/ppermute | solution.py:196
  7.7 2.7 %collective-permute-done.2.refs_3_ = bf16[48,512]{1,0:T(8,128)(2,1)S(1)} collective-permute-done((bf16[48,512]{1,0:T(8,128)(2,1)}, bf16[48,512]{1,0:T(8,128)(2,1)S(1)}, u32[]{:S(2)}, u32[]{:S(2)}) %collective-permute-start.2) | collective-permute-done | bytes 49184 | tf_op jit(solution)/shard_map/ppermute | solution.py:196
  10.4 1.3 %collective-permute-start.3 = (bf16[192,512]{1,0:T(8,128)(2,1)S(1)}, bf16[192,512]{1,0:T(8,128)(2,1)S(1)}, u32[]{:S(2)}, u32[]{:S(2)}) collective-permute-start(bf16[192,512]{1,0:T(8,128)(2,1)S(1)} %join.1.line_ref.refs_0_), channel_id=1, source_target_pairs={{0,64},{8,72},{16,80},{24,88},{32,96},{40,104},{48,112},{56,120},{... | collective-permute-start | bytes 589832 | tf_op jit(solution)/shard_map/ppermute | solution.py:196
  11.7 2.5 %collective-permute-start.4 = (bf16[192,512]{1,0:T(8,128)(2,1)S(1)}, bf16[192,512]{1,0:T(8,128)(2,1)S(1)}, u32[]{:S(2)}, u32[]{:S(2)}) collective-permute-start(bf16[192,512]{1,0:T(8,128)(2,1)S(1)} %join.1.line_ref.refs_0_), channel_id=1, source_target_pairs={{0,128},{8,136},{16,144},{24,152},{32,160},{40,168},{48,176},{56,1... | collective-permute-start | bytes 589832 | tf_op jit(solution)/shard_map/ppermute | solution.py:196
  14.2 0.2 collective-permute-start.5
  14.4 0.0 copy-done.3
  14.4 0.0 copy-done.4
  14.5 0.1 reshape.12.lag_ref
  14.5 0.0 copy-start.2
  14.6 3.7 %template_spectra.1 = (f32[24576,128]{1,0:T(8,128)S(1)}, bf16[192,512]{1,0:T(8,128)(2,1)S(1)}, s32[64,48]{1,0:T(8,128)S(1)}) custom-call(s32[24,128]{1,0:T(8,128)S(1)} %reshape.12.lag_ref, s32[64,48]{1,0:T(8,128)S(1)} %bitcast.3, bf16[192,512]{1,0:T(8,128)(2,1)S(1)} %join.1.line_ref.refs_0_, bf16[3072,200]{1,0:T(8,128)(2,1)S(1)} %get-tuple-element.15.waves, ...), custom_call_target="tpu_custom_call" | custom-call | flops 943718400 | bytes 12582912 | tf_op jit(solution)/shard_map/template_spectra/pallas_call | solution.py:89
  18.3 3.3 %collective-permute-start.6 = (bf16[192,512]{1,0:T(8,128)(2,1)S(1)}, bf16[192,512]{1,0:T(8,128)(2,1)S(1)}, u32[]{:S(2)}, u32[]{:S(2)}) collective-permute-start(bf16[192,512]{1,0:T(8,128)(2,1)S(1)} %get-tuple-element.19), channel_id=1, source_target_pairs={{0,8},{8,0},{16,24},{24,16},{32,40},{40,32},{48,56},{56,48},{64,72... | collective-permute-start | bytes 589832 | tf_op jit(solution)/shard_map/ppermute | solution.py:196
  21.6 0.0 collective-permute-done.3.refs_1_
  21.6 0.1 collective-permute-start.7
  21.7 0.0 collective-permute-done.4.refs_2_
  21.7 2.6 %collective-permute-start.8 = (bf16[192,512]{1,0:T(8,128)(2,1)S(1)}, bf16[192,512]{1,0:T(8,128)(2,1)S(1)}, u32[]{:S(2)}, u32[]{:S(2)}) collective-permute-start(bf16[192,512]{1,0:T(8,128)(2,1)S(1)} %collective-permute-done.4.refs_2_), channel_id=1, source_target_pairs={{0,8},{8,0},{16,24},{24,16},{32,40},{40,32},{48,56},{56,48},{64,72... | collective-permute-start | bytes 589832 | tf_op jit(solution)/shard_map/ppermute | solution.py:196
  24.3 0.0 collective-permute-done.5.refs_3_
  24.3 2.0 %collective-permute-start.9 = (bf16[192,512]{1,0:T(8,128)(2,1)S(1)}, bf16[192,512]{1,0:T(8,128)(2,1)S(1)}, u32[]{:S(2)}, u32[]{:S(2)}) collective-permute-start(bf16[192,512]{1,0:T(8,128)(2,1)S(1)} %collective-permute-done.5.refs_3_), channel_id=1, source_target_pairs={{0,8},{8,0},{16,24},{24,16},{32,40},{40,32},{48,56},{56,48},{64,72... | collective-permute-start | bytes 589832 | tf_op jit(solution)/shard_map/ppermute | solution.py:196
  26.4 0.0 collective-permute-done.6.refs_4_
  26.4 0.0 collective-permute-done.7.refs_5_
  26.4 0.0 collective-permute-done.8.refs_6_
  26.4 1.1 %collective-permute-done.9.refs_7_ = bf16[192,512]{1,0:T(8,128)(2,1)S(1)} collective-permute-done((bf16[192,512]{1,0:T(8,128)(2,1)S(1)}, bf16[192,512]{1,0:T(8,128)(2,1)S(1)}, u32[]{:S(2)}, u32[]{:S(2)}) %collective-permute-start.9) | collective-permute-done | bytes 196640 | tf_op jit(solution)/shard_map/ppermute | solution.py:196
  27.4 0.0 copy-done
  27.4 0.0 copy-done.2
  27.4 6.2 %detect.1 = (f32[64,512]{1,0:T(8,128)S(1)}, f32[64,256]{1,0:T(8,128)S(1)}) custom-call(s32[64,48]{1,0:T(8,128)S(1)} %get-tuple-element.18.slot_ref, bf16[192,512]{1,0:T(8,128)(2,1)S(1)} %join.1.line_ref.refs_0_, bf16[192,512]{1,0:T(8,128)(2,1)S(1)} %collective-permute-done.3.refs_1_, bf16[192,512]{1,0:T(8,128)(2,1)S(1)} %collective-permute-done.4.refs_2_, ...), custom_call_target="tpu_custom_call" | custom-call | flops 1207959552 | bytes 12582912 | tf_op jit(solution)/shard_map/detect/pallas_call | solution.py:167
  33.6 1.3 %collective-permute-start.10 = (f32[64,256]{1,0:T(8,128)S(1)}, f32[64,256]{1,0:T(8,128)S(1)}, u32[]{:S(2)}, u32[]{:S(2)}) collective-permute-start(f32[64,256]{1,0:T(8,128)S(1)} %get-tuple-element.22), channel_id=1, source_target_pairs={{1,0},{2,1},{3,2},{4,3},{5,4},{6,5},{7,6},{9,8},{10,9},{11,10},{12... | collective-permute-start | bytes 196616 | tf_op jit(solution)/shard_map/ppermute | solution.py:209
  34.9 7.6 %collective-permute-done.10 = f32[64,256]{1,0:T(8,128)S(1)} collective-permute-done((f32[64,256]{1,0:T(8,128)S(1)}, f32[64,256]{1,0:T(8,128)S(1)}, u32[]{:S(2)}, u32[]{:S(2)}) %collective-permute-start.10) | collective-permute-done | bytes 65568 | tf_op jit(solution)/shard_map/ppermute | solution.py:209
  42.5 0.7 %pad_add_fusion = f32[64,512]{1,0:T(8,128)} fusion(f32[64,512]{1,0:T(8,128)S(1)} %get-tuple-element.21, f32[64,256]{1,0:T(8,128)S(1)} %collective-permute-done.10), kind=kLoop, calls=%fused_computation | loop fusion | flops 32768 | bytes 327680 | tf_op jit(solution)/shard_map/add | solution.py:210
  (7 shorter events, 0.1 us)
Async XLA Ops:
  0.0 14.4 %copy-start.3 = (s32[2,32,48]{2,1,0:T(8,128)S(1)}, s32[2,32,48]{2,1,0:T(8,128)}, u32[]{:S(2)}) copy-start(s32[2,32,48]{2,1,0:T(8,128)} %param.10) | copy-start | bytes 36868
  0.0 14.4 %copy-start.4 = (s32[2,32,48]{2,1,0:T(8,128)S(1)}, s32[2,32,48]{2,1,0:T(8,128)}, u32[]{:S(2)}) copy-start(s32[2,32,48]{2,1,0:T(8,128)} %param.11) | copy-start | bytes 36868
  0.0 7.0 %collective-permute-start = (bf16[48,512]{1,0:T(8,128)(2,1)}, bf16[48,512]{1,0:T(8,128)(2,1)S(1)}, u32[]{:S(2)}, u32[]{:S(2)}) collective-permute-start(bf16[48,512]{1,0:T(8,128)(2,1)} %refs_0_.1), channel_id=1, source_target_pairs={{0,16},{8,24},{16,0},{24,8},{32,48},{40,56},{48,32},{56,40},{64,80... | collective-permute-start | bytes 147464 | tf_op jit(solution)/shard_map/ppermute | solution.py:196
  2.5 5.2 %collective-permute-start.1 = (bf16[48,512]{1,0:T(8,128)(2,1)}, bf16[48,512]{1,0:T(8,128)(2,1)S(1)}, u32[]{:S(2)}, u32[]{:S(2)}) collective-permute-start(bf16[48,512]{1,0:T(8,128)(2,1)} %refs_0_.1), channel_id=1, source_target_pairs={{0,32},{8,40},{16,48},{24,56},{32,0},{40,8},{48,16},{56,24},{64,96... | collective-permute-start | bytes 147464 | tf_op jit(solution)/shard_map/ppermute | solution.py:196
  5.5 5.0 %collective-permute-start.2 = (bf16[48,512]{1,0:T(8,128)(2,1)}, bf16[48,512]{1,0:T(8,128)(2,1)S(1)}, u32[]{:S(2)}, u32[]{:S(2)}) collective-permute-start(bf16[48,512]{1,0:T(8,128)(2,1)} %refs_0_.1), channel_id=1, source_target_pairs={{0,48},{8,56},{16,32},{24,40},{32,16},{40,24},{48,0},{56,8},{64,11... | collective-permute-start | bytes 147464 | tf_op jit(solution)/shard_map/ppermute | solution.py:196
  10.4 11.1 %collective-permute-start.3 = (bf16[192,512]{1,0:T(8,128)(2,1)S(1)}, bf16[192,512]{1,0:T(8,128)(2,1)S(1)}, u32[]{:S(2)}, u32[]{:S(2)}) collective-permute-start(bf16[192,512]{1,0:T(8,128)(2,1)S(1)} %join.1.line_ref.refs_0_), channel_id=1, source_target_pairs={{0,64},{8,72},{16,80},{24,88},{32,96},{40,104},{48,112},{56,120},{... | collective-permute-start | bytes 589832 | tf_op jit(solution)/shard_map/ppermute | solution.py:196
  11.7 10.0 %collective-permute-start.4 = (bf16[192,512]{1,0:T(8,128)(2,1)S(1)}, bf16[192,512]{1,0:T(8,128)(2,1)S(1)}, u32[]{:S(2)}, u32[]{:S(2)}) collective-permute-start(bf16[192,512]{1,0:T(8,128)(2,1)S(1)} %join.1.line_ref.refs_0_), channel_id=1, source_target_pairs={{0,128},{8,136},{16,144},{24,152},{32,160},{40,168},{48,176},{56,1... | collective-permute-start | bytes 589832 | tf_op jit(solution)/shard_map/ppermute | solution.py:196
  14.2 10.1 %collective-permute-start.5 = (bf16[192,512]{1,0:T(8,128)(2,1)S(1)}, bf16[192,512]{1,0:T(8,128)(2,1)S(1)}, u32[]{:S(2)}, u32[]{:S(2)}) collective-permute-start(bf16[192,512]{1,0:T(8,128)(2,1)S(1)} %join.1.line_ref.refs_0_), channel_id=1, source_target_pairs={{0,192},{8,200},{16,208},{24,216},{32,224},{40,232},{48,240},{56,2... | collective-permute-start | bytes 589832 | tf_op jit(solution)/shard_map/ppermute | solution.py:196
  14.5 12.9 %copy-start = (bf16[768,768]{1,0:T(8,128)(2,1)S(1)}, bf16[768,768]{1,0:T(8,128)(2,1)}, u32[]{:S(2)}) copy-start(bf16[768,768]{1,0:T(8,128)(2,1)} %constant.45.clone.refs_10_) | copy-start | bytes 3538948
  14.5 12.9 %copy-start.1 = (bf16[768,768]{1,0:T(8,128)(2,1)S(1)}, bf16[768,768]{1,0:T(8,128)(2,1)}, u32[]{:S(2)}) copy-start(bf16[768,768]{1,0:T(8,128)(2,1)} %constant.46.clone.refs_11_) | copy-start | bytes 3538948
  14.5 12.9 %copy-start.2 = (bf16[512,768]{1,0:T(8,128)(2,1)S(1)}, bf16[512,768]{1,0:T(8,128)(2,1)}, u32[]{:S(2)}) copy-start(bf16[512,768]{1,0:T(8,128)(2,1)} %constant.43.clone.refs_9_) | copy-start | bytes 2359300
  18.3 8.1 %collective-permute-start.6 = (bf16[192,512]{1,0:T(8,128)(2,1)S(1)}, bf16[192,512]{1,0:T(8,128)(2,1)S(1)}, u32[]{:S(2)}, u32[]{:S(2)}) collective-permute-start(bf16[192,512]{1,0:T(8,128)(2,1)S(1)} %get-tuple-element.19), channel_id=1, source_target_pairs={{0,8},{8,0},{16,24},{24,16},{32,40},{40,32},{48,56},{56,48},{64,72... | collective-permute-start | bytes 589832 | tf_op jit(solution)/shard_map/ppermute | solution.py:196
  21.6 4.8 %collective-permute-start.7 = (bf16[192,512]{1,0:T(8,128)(2,1)S(1)}, bf16[192,512]{1,0:T(8,128)(2,1)S(1)}, u32[]{:S(2)}, u32[]{:S(2)}) collective-permute-start(bf16[192,512]{1,0:T(8,128)(2,1)S(1)} %collective-permute-done.3.refs_1_), channel_id=1, source_target_pairs={{0,8},{8,0},{16,24},{24,16},{32,40},{40,32},{48,56},{56,48},{64,72... | collective-permute-start | bytes 589832 | tf_op jit(solution)/shard_map/ppermute | solution.py:196
  21.7 4.7 %collective-permute-start.8 = (bf16[192,512]{1,0:T(8,128)(2,1)S(1)}, bf16[192,512]{1,0:T(8,128)(2,1)S(1)}, u32[]{:S(2)}, u32[]{:S(2)}) collective-permute-start(bf16[192,512]{1,0:T(8,128)(2,1)S(1)} %collective-permute-done.4.refs_2_), channel_id=1, source_target_pairs={{0,8},{8,0},{16,24},{24,16},{32,40},{40,32},{48,56},{56,48},{64,72... | collective-permute-start | bytes 589832 | tf_op jit(solution)/shard_map/ppermute | solution.py:196
  24.3 3.1 %collective-permute-start.9 = (bf16[192,512]{1,0:T(8,128)(2,1)S(1)}, bf16[192,512]{1,0:T(8,128)(2,1)S(1)}, u32[]{:S(2)}, u32[]{:S(2)}) collective-permute-start(bf16[192,512]{1,0:T(8,128)(2,1)S(1)} %collective-permute-done.5.refs_3_), channel_id=1, source_target_pairs={{0,8},{8,0},{16,24},{24,16},{32,40},{40,32},{48,56},{56,48},{64,72... | collective-permute-start | bytes 589832 | tf_op jit(solution)/shard_map/ppermute | solution.py:196
  33.6 8.9 %collective-permute-start.10 = (f32[64,256]{1,0:T(8,128)S(1)}, f32[64,256]{1,0:T(8,128)S(1)}, u32[]{:S(2)}, u32[]{:S(2)}) collective-permute-start(f32[64,256]{1,0:T(8,128)S(1)} %get-tuple-element.22), channel_id=1, source_target_pairs={{1,0},{2,1},{3,2},{4,3},{5,4},{6,5},{7,6},{9,8},{10,9},{11,10},{12... | collective-permute-start | bytes 196616 | tf_op jit(solution)/shard_map/ppermute | solution.py:209

commit v5 on v4

--- a/solution.py
+++ b/solution.py
@@ -14,8 +14,11 @@
 EXTRA = L + LAGS - 2
 HOLD = 128
 LAG_ROWS = 64
+Z_ORDER = (3, 2, 1)
+X_ORDER = (3, 1, 2)
 VMEM_K1 = 20 << 20
 VMEM_K2 = 24 << 20
+VMEM_D1 = 10 << 20
 
 
 def angles(samples, freqs, width):
@@ -122,16 +125,39 @@
     )(*parts)
 
 
+def fill_table(blocks, forward_ref, table, first, freqs):
+    for b, block in enumerate(blocks):
+        size = block.shape[0]
+        dft = jnp.dot(block[...], forward_ref[...], preferred_element_type=jnp.float32)
+        for j in range(freqs // HOLD):
+            start = (first + b * size) * 8 + j
+            table[pl.ds(start, size, stride=8), :] = dft[:, j * HOLD : (j + 1) * HOLD]
+            table[pl.ds(start + 4, size, stride=8), :] = dft[:, freqs + j * HOLD : freqs + (j + 1) * HOLD]
+
+
+def record_kernel(freqs, *refs):
+    *blocks, forward_ref, table = refs
+    fill_table(blocks, forward_ref, table, 0, freqs)
+
+
+def record_spectra(blocks, forward, freqs, parts):
+    rows = sum(b.shape[0] for b in blocks)
+    whole = pl.BlockSpec(memory_space=pltpu.VMEM)
+    return pl.pallas_call(
+        functools.partial(record_kernel, freqs),
+        in_specs=[whole] * (len(blocks) + 1),
+        out_specs=whole,
+        out_shape=jax.ShapeDtypeStruct((parts * rows * 8, HOLD), jnp.float32),
+        compiler_params=pltpu.CompilerParams(vmem_limit_bytes=VMEM_D1),
+        cost_estimate=pl.CostEstimate(flops=rows * forward.shape[0] * freqs * 4, bytes_accessed=rows * 8 * HOLD * 4, transcendentals=0),
+        name="record_spectra",
+    )(*blocks, forward)
+
+
 def detect_kernel(n_blocks, count, stations, freqs, slot_ref, *refs):
-    blocks, (q, forward_ref, high_ref, low_ref, main_ref, early_ref, table, acc) = refs[:n_blocks], refs[n_blocks:]
+    blocks, (_, q, forward_ref, high_ref, low_ref, main_ref, early_ref, table, acc) = refs[:n_blocks], refs[n_blocks:]
     chunks = freqs // HOLD
-    size = blocks[0].shape[0]
-    for b, block in enumerate(blocks):
-        dft = jnp.dot(block[...], forward_ref[...], preferred_element_type=jnp.float32)
-        for j in range(chunks):
-            start = b * size * 8
-            table[pl.ds(start + j, size, stride=8), :] = dft[:, j * HOLD : (j + 1) * HOLD]
-            table[pl.ds(start + 4 + j, size, stride=8), :] = dft[:, freqs + j * HOLD : freqs + (j + 1) * HOLD]
+    fill_table(blocks, forward_ref, table, table.shape[0] // 16, freqs)
 
     def one(t, carry):
         first = [jnp.zeros((8, HOLD), jnp.float32)] * 2
@@ -146,7 +172,7 @@
         acc[pl.ds(pl.multiple_of(t * 16 + 8, 8), 8), :] = second[0] + second[1]
         return carry
 
-    lax.fori_loop(0, count, one, 0)
+    lax.fori_loop(0, count, one, 0, unroll=2)
     joint = jnp.concatenate(
         [acc[pl.ds(j, count, stride=16), :] + acc[pl.ds(4 + j, count, stride=16), :] for j in range(chunks)]
         + [acc[pl.ds(8 + j, count, stride=16), :] - acc[pl.ds(12 + j, count, stride=16), :] for j in range(chunks)],
@@ -158,34 +184,39 @@
     out = both[:count] + both[count:] + jnp.dot(top, low_ref[...], preferred_element_type=jnp.float32)
     time_dev = main_ref.shape[1]
     main_ref[...] = out[:, :time_dev]
-    early_ref[...] = out[:, time_dev:]
-
-
-def detect(slots, blocks, q, forward, high, low, count, stations, freqs, time_dev):
+    early_ref[...] = out[:, time_dev:].astype(early_ref.dtype)
+
+
+def detect(slots, blocks, table, q, forward, high, low, count, stations, freqs, time_dev):
     rows = sum(b.shape[0] for b in blocks)
     whole = pl.BlockSpec(memory_space=pltpu.VMEM)
     return pl.pallas_call(
         functools.partial(detect_kernel, len(blocks), count, stations, freqs),
-        in_specs=[pl.BlockSpec(memory_space=pltpu.SMEM)] + [whole] * (len(blocks) + 4),
-        out_specs=[whole, whole],
+        in_specs=[pl.BlockSpec(memory_space=pltpu.SMEM)] + [whole] * (len(blocks) + 5),
+        out_specs=[whole] * 3,
         out_shape=[
             jax.ShapeDtypeStruct((count, time_dev), jnp.float32),
-            jax.ShapeDtypeStruct((count, time_dev // 2), jnp.float32),
+            jax.ShapeDtypeStruct((count, time_dev // 2), jnp.bfloat16),
+            jax.ShapeDtypeStruct(table.shape, table.dtype),
         ],
+        input_output_aliases={1 + len(blocks): 2},
         scratch_shapes=[
-            pltpu.VMEM((rows * 8, HOLD), jnp.float32),
             pltpu.VMEM((count * 16, HOLD), jnp.float32),
         ],
         compiler_params=pltpu.CompilerParams(vmem_limit_bytes=VMEM_K2),
         cost_estimate=pl.CostEstimate(flops=rows * time_dev * freqs * 4, bytes_accessed=count * stations * 8 * HOLD * 4, transcendentals=0),
         name="detect",
-    )(slots, *blocks, q, forward, high, low)
+    )(slots, *blocks, table, q, forward, high, low)[:2]
 
 
 def route(change):
     dx, dz, dc = change
     code = (dx * 4 + dz) * 2 + dc
     return [(i, i ^ code) for i in range(32)]
+
+
+def position_bits(order):
+    return sum((1 + n) << (2 * d) for n, d in enumerate(order))
 
 
 def per_device(records, templates, channels, moveouts):
@@ -196,17 +227,22 @@
     swap = lambda block, change: lax.ppermute(block, "tmpl", route(change))
 
     apart = (channels // per) ^ lax.axis_index("tmpl")
-    place = ((apart & 1) * 16 + (apart >> 1)) * per + channels % per
+    rank_z = (position_bits(Z_ORDER) >> (apart & 6)) & 3
+    rank_x = (position_bits(X_ORDER) >> ((apart >> 2) & 6)) & 3
+    place = ((apart & 1) * 16 + rank_x * 4 + rank_z) * per + channels % per
     slots = (place * 8).reshape(-1, stations)
 
     own, waves, head, phase = load([records, templates.reshape(-1, length), forward[:length], phase])
-    line = join([own] + [swap(records, (0, d, 0)) for d in (1, 2, 3)])
-    plane = [swap(line, (d, 0, 0)) for d in (1, 2, 3)]
+    line = join([own] + [swap(records, (0, d, 0)) for d in Z_ORDER])
+    plane = [swap(line, (d, 0, 0)) for d in X_ORDER]
     q, line_q, slots = template_spectra(moveouts.reshape(-1, HOLD), slots, line, waves, head, phase, freqs)
-    blocks = [line] + plane + [swap(block, (0, 0, 1)) for block in [line_q] + plane]
-
-    main, early = detect(slots, blocks, q, forward, high, low, batches * count, stations, freqs, time_dev)
+    near = [line] + plane
+    far = [swap(block, (0, 0, 1)) for block in [line_q] + plane]
+    table = record_spectra(near, forward, freqs, 2)
+
+    main, early = detect(slots, far, table, q, forward, high, low, batches * count, stations, freqs, time_dev)
     earlier = lax.ppermute(early, "tm", [(i, i - 1) for i in range(1, lax.axis_size("tm"))])
+    earlier = earlier.astype(jnp.float32)
     out = main + jnp.pad(earlier, ((0, 0), (time_dev - earlier.shape[1], 0)))
     return out.reshape(batches, count, time_dev)
 

time: 43.3 us -> 39 us (0.901)
  starting transfers between devices: 18.8 us -> 16.2 us
  waiting for transfers between devices: 12.1 us -> 10.1 us
    ppermute x10, starting transfers between devices: 17.5 us -> 14.9 us  [per_device(): swap = lambda block, change: lax.ppermute(block, 'tmpl', route(change))]
    ppermute x10, waiting for transfers between devices: 4.46 us -> 2.77 us  [per_device(): swap = lambda block, change: lax.ppermute(block, 'tmpl', route(change))]
    pallas_call x0 -> x1, Pallas kernels: none -> 0.87 us  [record_spectra(): pl.pallas_call(functools.partial(record_kernel, freqs), in_specs=[whole]...]
    pallas_call x1, Pallas kernels: 6.16 us -> 5.35 us  [detect(): pl.pallas_call(functools.partial(detect_kernel, len(blocks), count, stati...]
  transfers between devices with their start and end apart: 11 -> 11, of which waited for: 4 -> 3; matrix products, arithmetic and copies ran while one was open for 0% -> 0% of each run, Pallas kernels for 12% -> 16%
where the time goes in v5:
time: 39 us; the launch traced here: 38.7 us
  starting transfers between devices  16.2 us (42%)
  Pallas kernels  11.5 us (29%)
  waiting for transfers between devices  10.1 us (26%)
  other arithmetic  0.72 us (2%)
    ppermute x10, starting transfers between devices, per_device(): swap = lambda block, change: lax.ppermute(block, 'tmpl', route(change))  14.9 us
    ppermute x1, waiting for transfers between devices, per_device(): lax.ppermute(early, 'tm', [(i, i - 1) for i in range(1, lax.axis_size('tm...  7.29 us
    pallas_call x1, Pallas kernels, detect(): pl.pallas_call(functools.partial(detect_kernel, len(blocks), count, stati...  5.35 us
    pallas_call x1, Pallas kernels, template_spectra(): pl.pallas_call(functools.partial(template_kernel, 512, freqs), in_specs=[...  3.72 us
    ppermute x10, waiting for transfers between devices, per_device(): swap = lambda block, change: lax.ppermute(block, 'tmpl', route(change))  2.77 us
    pallas_call x1, Pallas kernels, load(): pl.pallas_call(functools.partial(load_kernel, len(arrays)), in_specs=[pl....  1.55 us
    ppermute x1, starting transfers between devices, per_device(): lax.ppermute(early, 'tm', [(i, i - 1) for i in range(1, lax.axis_size('tm...  1.29 us
    pallas_call x1, Pallas kernels, record_spectra(): pl.pallas_call(functools.partial(record_kernel, freqs), in_specs=[whole]...  0.87 us
  transfers between devices with their start and end apart: 11, of which 3 were waited for; matrix products, arithmetic and copies ran while one was open for 0% of the time, Pallas kernels for 16%

profile of v5, /device:TPU:1, one launch (start us, length us, event | category | flops | bytes accessed | tf_op | source)
XLA Modules:
  0.0 38.7 jit_solution(5779370785572892818)
XLA Ops:
  0.0 5.2 %collective-permute-start = (bf16[48,512]{1,0:T(8,128)(2,1)}, bf16[48,512]{1,0:T(8,128)(2,1)S(1)}, u32[]{:S(2)}, u32[]{:S(2)}) collective-permute-start(bf16[48,512]{1,0:T(8,128)(2,1)} %refs_0_.1), channel_id=1, source_target_pairs={{0,48},{8,56},{16,32},{24,40},{32,16},{40,24},{48,0},{56,8},{64,11... | collective-permute-start | bytes 147464 | tf_op jit(solution)/shard_map/ppermute | solution.py:227
  5.2 0.0 collective-permute-start.2
  5.2 0.4 collective-permute-start.1
  5.6 1.6 %load.1 = (bf16[48,512]{1,0:T(8,128)(2,1)S(1)}, bf16[3072,200]{1,0:T(8,128)(2,1)S(1)}, bf16[200,768]{1,0:T(8,128)(2,1)S(1)}, bf16[128,768]{1,0:T(8,128)(2,1)S(1)}) custom-call(bf16[48,512]{1,0:T(8,128)(2,1)} %refs_0_.1, bf16[3072,200]{1,0:T(8,128)(2,1)} %bitcast.4, bf16[200,768]{1,0:T(8,128)(2,1)} %constant.63.refs_2_, bf16[128,768]{1,0:T(8,128)(2,1)} %constant.57.clone.refs_3_), custom_call_target="tpu_custom_call" | custom-call | tf_op jit(solution)/shard_map/load/pallas_call | solution.py:62
  7.1 0.0 collective-permute-done.refs_1_
  7.1 2.6 %collective-permute-done.2.refs_3_ = bf16[48,512]{1,0:T(8,128)(2,1)S(1)} collective-permute-done((bf16[48,512]{1,0:T(8,128)(2,1)}, bf16[48,512]{1,0:T(8,128)(2,1)S(1)}, u32[]{:S(2)}, u32[]{:S(2)}) %collective-permute-start.2) | collective-permute-done | bytes 49184 | tf_op jit(solution)/shard_map/ppermute | solution.py:227
  9.7 0.0 collective-permute-done.1.refs_2_
  9.7 2.3 %collective-permute-start.8 = (bf16[192,512]{1,0:T(8,128)(2,1)S(1)}, bf16[192,512]{1,0:T(8,128)(2,1)S(1)}, u32[]{:S(2)}, u32[]{:S(2)}) collective-permute-start(bf16[192,512]{1,0:T(8,128)(2,1)S(1)} %join.1.line_ref.refs_0_), channel_id=1, source_target_pairs={{0,128},{8,136},{16,144},{24,152},{32,160},{40,168},{48,176},{56,1... | collective-permute-start | bytes 589832 | tf_op jit(solution)/shard_map/ppermute | solution.py:227
  12.1 0.3 collective-permute-start.6
  12.4 0.7 %collective-permute-start.4 = (bf16[192,512]{1,0:T(8,128)(2,1)S(1)}, bf16[192,512]{1,0:T(8,128)(2,1)S(1)}, u32[]{:S(2)}, u32[]{:S(2)}) collective-permute-start(bf16[192,512]{1,0:T(8,128)(2,1)S(1)} %join.1.line_ref.refs_0_), channel_id=1, source_target_pairs={{0,192},{8,200},{16,208},{24,216},{32,224},{40,232},{48,240},{56,2... | collective-permute-start | bytes 589832 | tf_op jit(solution)/shard_map/ppermute | solution.py:227
  13.1 0.1 fusion.2
  13.2 0.1 reshape.12.lag_ref
  13.2 3.7 %template_spectra.1 = (f32[24576,128]{1,0:T(8,128)S(1)}, bf16[192,512]{1,0:T(8,128)(2,1)S(1)}, s32[64,48]{1,0:T(8,128)S(1)}) custom-call(s32[24,128]{1,0:T(8,128)S(1)} %reshape.12.lag_ref, s32[64,48]{1,0:T(8,128)S(1)} %bitcast.3, bf16[192,512]{1,0:T(8,128)(2,1)S(1)} %join.1.line_ref.refs_0_, bf16[3072,200]{1,0:T(8,128)(2,1)S(1)} %get-tuple-element.15.waves, ...), custom_call_target="tpu_custom_call" | custom-call | flops 943718400 | bytes 12582912 | tf_op jit(solution)/shard_map/template_spectra/pallas_call | solution.py:92
  17.0 0.0 copy-start.1
  17.0 0.0 copy-start.2
  17.0 2.9 %collective-permute-start.3 = (bf16[192,512]{1,0:T(8,128)(2,1)S(1)}, bf16[192,512]{1,0:T(8,128)(2,1)S(1)}, u32[]{:S(2)}, u32[]{:S(2)}) collective-permute-start(bf16[192,512]{1,0:T(8,128)(2,1)S(1)} %get-tuple-element.19), channel_id=1, source_target_pairs={{0,8},{8,0},{16,24},{24,16},{32,40},{40,32},{48,56},{56,48},{64,72... | collective-permute-start | bytes 589832 | tf_op jit(solution)/shard_map/ppermute | solution.py:227
  19.9 0.0 collective-permute-done.8.refs_3_
  19.9 1.0 %collective-permute-start.9 = (bf16[192,512]{1,0:T(8,128)(2,1)S(1)}, bf16[192,512]{1,0:T(8,128)(2,1)S(1)}, u32[]{:S(2)}, u32[]{:S(2)}) collective-permute-start(bf16[192,512]{1,0:T(8,128)(2,1)S(1)} %collective-permute-done.8.refs_3_), channel_id=1, source_target_pairs={{0,8},{8,0},{16,24},{24,16},{32,40},{40,32},{48,56},{56,48},{64,72... | collective-permute-start | bytes 589832 | tf_op jit(solution)/shard_map/ppermute | solution.py:227
  20.9 0.0 collective-permute-done.6.refs_2_
  20.9 1.6 %collective-permute-start.7 = (bf16[192,512]{1,0:T(8,128)(2,1)S(1)}, bf16[192,512]{1,0:T(8,128)(2,1)S(1)}, u32[]{:S(2)}, u32[]{:S(2)}) collective-permute-start(bf16[192,512]{1,0:T(8,128)(2,1)S(1)} %collective-permute-done.6.refs_2_), channel_id=1, source_target_pairs={{0,8},{8,0},{16,24},{24,16},{32,40},{40,32},{48,56},{56,48},{64,72... | collective-permute-start | bytes 589832 | tf_op jit(solution)/shard_map/ppermute | solution.py:227
  22.5 0.0 collective-permute-done.4.refs_1_
  22.5 0.6 %collective-permute-start.5 = (bf16[192,512]{1,0:T(8,128)(2,1)S(1)}, bf16[192,512]{1,0:T(8,128)(2,1)S(1)}, u32[]{:S(2)}, u32[]{:S(2)}) collective-permute-start(bf16[192,512]{1,0:T(8,128)(2,1)S(1)} %collective-permute-done.4.refs_1_), channel_id=1, source_target_pairs={{0,8},{8,0},{16,24},{24,16},{32,40},{40,32},{48,56},{56,48},{64,72... | collective-permute-start | bytes 589832 | tf_op jit(solution)/shard_map/ppermute | solution.py:227
  23.0 0.9 %record_spectra.1.refs_4_ = f32[12288,128]{1,0:T(8,128)S(1)} custom-call(bf16[192,512]{1,0:T(8,128)(2,1)S(1)} %join.1.line_ref.refs_0_, bf16[192,512]{1,0:T(8,128)(2,1)S(1)} %collective-permute-done.4.refs_1_, bf16[192,512]{1,0:T(8,128)(2,1)S(1)} %collective-permute-done.6.refs_2_, bf16[192,512]{1,0:T(8,128)(2,1)S(1)} %collective-permute-done.8.refs_3_, ...), custom_call_target="tpu_custom_call" | custom-call | flops 603979776 | bytes 3145728 | tf_op jit(solution)/shard_map/record_spectra/pallas_call | solution.py:146
  23.9 0.0 collective-permute-done.3.refs_0_
  23.9 0.0 collective-permute-done.9.refs_3_
  23.9 0.0 collective-permute-done.7.refs_2_
  23.9 0.2 collective-permute-done.5.refs_1_
  24.1 0.0 copy-done.1
  24.1 5.3 %detect.1 = (f32[64,512]{1,0:T(8,128)S(1)}, bf16[64,256]{1,0:T(8,128)(2,1)S(1)}, f32[12288,128]{1,0:T(8,128)S(1)}) custom-call(s32[64,48]{1,0:T(8,128)S(1)} %get-tuple-element.18.slot_ref, bf16[192,512]{1,0:T(8,128)(2,1)S(1)} %collective-permute-done.3.refs_0_, bf16[192,512]{1,0:T(8,128)(2,1)S(1)} %collective-permute-done.5.refs_1_, ...), custom_call_target="tpu_custom_call", output_to_operand_aliasing={{2}: (5, {})} | custom-call | flops 603979776 | bytes 12582912 | tf_op jit(solution)/shard_map/detect/pallas_call | solution.py:193
  29.5 1.3 %collective-permute-start.10 = (bf16[64,256]{1,0:T(8,128)(2,1)S(1)}, bf16[64,256]{1,0:T(8,128)(2,1)S(1)}, u32[]{:S(2)}, u32[]{:S(2)}) collective-permute-start(bf16[64,256]{1,0:T(8,128)(2,1)S(1)} %get-tuple-element.22), channel_id=1, source_target_pairs={{1,0},{2,1},{3,2},{4,3},{5,4},{6,5},{7,6},{9,8},{10,9},{11,10},{12... | collective-permute-start | bytes 98312 | tf_op jit(solution)/shard_map/ppermute | solution.py:244
  30.8 7.3 %collective-permute-done.10 = bf16[64,256]{1,0:T(8,128)(2,1)S(1)} collective-permute-done((bf16[64,256]{1,0:T(8,128)(2,1)S(1)}, bf16[64,256]{1,0:T(8,128)(2,1)S(1)}, u32[]{:S(2)}, u32[]{:S(2)}) %collective-permute-start.10) | collective-permute-done | bytes 32800 | tf_op jit(solution)/shard_map/ppermute | solution.py:244
  38.1 0.7 %convert_add_fusion = f32[64,512]{1,0:T(8,128)} fusion(f32[64,512]{1,0:T(8,128)S(1)} %get-tuple-element.21, bf16[64,256]{1,0:T(8,128)(2,1)S(1)} %collective-permute-done.10), kind=kLoop, calls=%fused_computation | loop fusion | flops 65536 | bytes 294912 | tf_op jit(solution)/shard_map/add | solution.py:246
  (8 shorter events, 0.0 us)
Async XLA Ops:
  0.0 13.1 %copy-start.3 = (s32[2,32,48]{2,1,0:T(8,128)S(1)}, s32[2,32,48]{2,1,0:T(8,128)}, u32[]{:S(2)}) copy-start(s32[2,32,48]{2,1,0:T(8,128)} %param.10) | copy-start | bytes 36868
  0.0 13.1 %copy-start.4 = (s32[2,32,48]{2,1,0:T(8,128)S(1)}, s32[2,32,48]{2,1,0:T(8,128)}, u32[]{:S(2)}) copy-start(s32[2,32,48]{2,1,0:T(8,128)} %param.11) | copy-start | bytes 36868
  0.0 7.1 %collective-permute-start = (bf16[48,512]{1,0:T(8,128)(2,1)}, bf16[48,512]{1,0:T(8,128)(2,1)S(1)}, u32[]{:S(2)}, u32[]{:S(2)}) collective-permute-start(bf16[48,512]{1,0:T(8,128)(2,1)} %refs_0_.1), channel_id=1, source_target_pairs={{0,48},{8,56},{16,32},{24,40},{32,16},{40,24},{48,0},{56,8},{64,11... | collective-permute-start | bytes 147464 | tf_op jit(solution)/shard_map/ppermute | solution.py:227
  5.2 4.5 %collective-permute-start.2 = (bf16[48,512]{1,0:T(8,128)(2,1)}, bf16[48,512]{1,0:T(8,128)(2,1)S(1)}, u32[]{:S(2)}, u32[]{:S(2)}) collective-permute-start(bf16[48,512]{1,0:T(8,128)(2,1)} %refs_0_.1), channel_id=1, source_target_pairs={{0,16},{8,24},{16,0},{24,8},{32,48},{40,56},{48,32},{56,40},{64,80... | collective-permute-start | bytes 147464 | tf_op jit(solution)/shard_map/ppermute | solution.py:227
  5.2 4.5 %collective-permute-start.1 = (bf16[48,512]{1,0:T(8,128)(2,1)}, bf16[48,512]{1,0:T(8,128)(2,1)S(1)}, u32[]{:S(2)}, u32[]{:S(2)}) collective-permute-start(bf16[48,512]{1,0:T(8,128)(2,1)} %refs_0_.1), channel_id=1, source_target_pairs={{0,32},{8,40},{16,48},{24,56},{32,0},{40,8},{48,16},{56,24},{64,96... | collective-permute-start | bytes 147464 | tf_op jit(solution)/shard_map/ppermute | solution.py:227
  9.7 10.1 %collective-permute-start.8 = (bf16[192,512]{1,0:T(8,128)(2,1)S(1)}, bf16[192,512]{1,0:T(8,128)(2,1)S(1)}, u32[]{:S(2)}, u32[]{:S(2)}) collective-permute-start(bf16[192,512]{1,0:T(8,128)(2,1)S(1)} %join.1.line_ref.refs_0_), channel_id=1, source_target_pairs={{0,128},{8,136},{16,144},{24,152},{32,160},{40,168},{48,176},{56,1... | collective-permute-start | bytes 589832 | tf_op jit(solution)/shard_map/ppermute | solution.py:227
  12.1 8.8 %collective-permute-start.6 = (bf16[192,512]{1,0:T(8,128)(2,1)S(1)}, bf16[192,512]{1,0:T(8,128)(2,1)S(1)}, u32[]{:S(2)}, u32[]{:S(2)}) collective-permute-start(bf16[192,512]{1,0:T(8,128)(2,1)S(1)} %join.1.line_ref.refs_0_), channel_id=1, source_target_pairs={{0,64},{8,72},{16,80},{24,88},{32,96},{40,104},{48,112},{56,120},{... | collective-permute-start | bytes 589832 | tf_op jit(solution)/shard_map/ppermute | solution.py:227
  12.4 10.1 %collective-permute-start.4 = (bf16[192,512]{1,0:T(8,128)(2,1)S(1)}, bf16[192,512]{1,0:T(8,128)(2,1)S(1)}, u32[]{:S(2)}, u32[]{:S(2)}) collective-permute-start(bf16[192,512]{1,0:T(8,128)(2,1)S(1)} %join.1.line_ref.refs_0_), channel_id=1, source_target_pairs={{0,192},{8,200},{16,208},{24,216},{32,224},{40,232},{48,240},{56,2... | collective-permute-start | bytes 589832 | tf_op jit(solution)/shard_map/ppermute | solution.py:227
  13.2 9.8 %copy-start = (bf16[512,768]{1,0:T(8,128)(2,1)S(1)}, bf16[512,768]{1,0:T(8,128)(2,1)}, u32[]{:S(2)}) copy-start(bf16[512,768]{1,0:T(8,128)(2,1)} %constant.56.clone.refs_4_.refs_6_) | copy-start | bytes 2359300
  17.0 7.1 %copy-start.1 = (bf16[768,768]{1,0:T(8,128)(2,1)S(1)}, bf16[768,768]{1,0:T(8,128)(2,1)}, u32[]{:S(2)}) copy-start(bf16[768,768]{1,0:T(8,128)(2,1)} %constant.59.clone.refs_8_) | copy-start | bytes 3538948
  17.0 7.1 %copy-start.2 = (bf16[768,768]{1,0:T(8,128)(2,1)S(1)}, bf16[768,768]{1,0:T(8,128)(2,1)}, u32[]{:S(2)}) copy-start(bf16[768,768]{1,0:T(8,128)(2,1)} %constant.58.clone.refs_7_) | copy-start | bytes 3538948
  17.0 6.9 %collective-permute-start.3 = (bf16[192,512]{1,0:T(8,128)(2,1)S(1)}, bf16[192,512]{1,0:T(8,128)(2,1)S(1)}, u32[]{:S(2)}, u32[]{:S(2)}) collective-permute-start(bf16[192,512]{1,0:T(8,128)(2,1)S(1)} %get-tuple-element.19), channel_id=1, source_target_pairs={{0,8},{8,0},{16,24},{24,16},{32,40},{40,32},{48,56},{56,48},{64,72... | collective-permute-start | bytes 589832 | tf_op jit(solution)/shard_map/ppermute | solution.py:227
  19.9 4.0 %collective-permute-start.9 = (bf16[192,512]{1,0:T(8,128)(2,1)S(1)}, bf16[192,512]{1,0:T(8,128)(2,1)S(1)}, u32[]{:S(2)}, u32[]{:S(2)}) collective-permute-start(bf16[192,512]{1,0:T(8,128)(2,1)S(1)} %collective-permute-done.8.refs_3_), channel_id=1, source_target_pairs={{0,8},{8,0},{16,24},{24,16},{32,40},{40,32},{48,56},{56,48},{64,72... | collective-permute-start | bytes 589832 | tf_op jit(solution)/shard_map/ppermute | solution.py:227
  20.9 3.1 %collective-permute-start.7 = (bf16[192,512]{1,0:T(8,128)(2,1)S(1)}, bf16[192,512]{1,0:T(8,128)(2,1)S(1)}, u32[]{:S(2)}, u32[]{:S(2)}) collective-permute-start(bf16[192,512]{1,0:T(8,128)(2,1)S(1)} %collective-permute-done.6.refs_2_), channel_id=1, source_target_pairs={{0,8},{8,0},{16,24},{24,16},{32,40},{40,32},{48,56},{56,48},{64,72... | collective-permute-start | bytes 589832 | tf_op jit(solution)/shard_map/ppermute | solution.py:227
  22.5 1.6 %collective-permute-start.5 = (bf16[192,512]{1,0:T(8,128)(2,1)S(1)}, bf16[192,512]{1,0:T(8,128)(2,1)S(1)}, u32[]{:S(2)}, u32[]{:S(2)}) collective-permute-start(bf16[192,512]{1,0:T(8,128)(2,1)S(1)} %collective-permute-done.4.refs_1_), channel_id=1, source_target_pairs={{0,8},{8,0},{16,24},{24,16},{32,40},{40,32},{48,56},{56,48},{64,72... | collective-permute-start | bytes 589832 | tf_op jit(solution)/shard_map/ppermute | solution.py:227
  29.5 8.6 %collective-permute-start.10 = (bf16[64,256]{1,0:T(8,128)(2,1)S(1)}, bf16[64,256]{1,0:T(8,128)(2,1)S(1)}, u32[]{:S(2)}, u32[]{:S(2)}) collective-permute-start(bf16[64,256]{1,0:T(8,128)(2,1)S(1)} %get-tuple-element.22), channel_id=1, source_target_pairs={{1,0},{2,1},{3,2},{4,3},{5,4},{6,5},{7,6},{9,8},{10,9},{11,10},{12... | collective-permute-start | bytes 98312 | tf_op jit(solution)/shard_map/ppermute | solution.py:244

commit v6 on v5

--- a/solution.py
+++ b/solution.py
@@ -15,10 +15,10 @@
 HOLD = 128
 LAG_ROWS = 64
 Z_ORDER = (3, 2, 1)
-X_ORDER = (3, 1, 2)
-VMEM_K1 = 20 << 20
-VMEM_K2 = 24 << 20
-VMEM_D1 = 10 << 20
+X_ORDER = (2, 1, 3)
+VMEM_K1 = 12 << 20
+VMEM_K2 = 12 << 20
+VMEM_D1 = 4 << 20
 
 
 def angles(samples, freqs, width):
@@ -70,23 +70,23 @@
     )(*(pltpu.with_memory_space_constraint(a, pltpu.HBM) for a in arrays))
 
 
-def template_kernel(step, freqs, lag_ref, slot_ref, line_ref, waves, forward, phases, out, line_out, slot_out):
+def template_kernel(step, freqs, lag_ref, line_ref, waves, head, forward, phases, out, line_out, table):
     line_out[...] = line_ref[...]
-    slot_out[...] = slot_ref[...]
     for start in range(0, waves.shape[0], step):
         lag = jnp.concatenate([lag_ref[pl.ds((start + at) // HOLD, 1), :] for at in range(0, step, HOLD)], axis=1)
         lag_row = lax.broadcasted_iota(jnp.int32, (2 * LAG_ROWS, step), 0) & (LAG_ROWS - 1)
         chosen = (lag_row == lag).astype(jnp.float32).astype(jnp.bfloat16)
         phase = lax.dot_general(chosen, phases[...], (((0,), (0,)), ((), ())), preferred_element_type=jnp.float32)
-        dft = jnp.dot(waves[pl.ds(start, step), :], forward[...], preferred_element_type=jnp.float32)
+        dft = jnp.dot(waves[pl.ds(start, step), :], head[...], preferred_element_type=jnp.float32)
         for j in range(freqs // HOLD):
             low, high = slice(j * HOLD, (j + 1) * HOLD), slice(freqs + j * HOLD, freqs + (j + 1) * HOLD)
             h_cos, h_sin, c_theta, s_theta = dft[:, low], dft[:, high], phase[:, low], phase[:, high]
             out[pl.ds(start * 8 + j, step, stride=8), :] = h_cos * c_theta - h_sin * s_theta
             out[pl.ds(start * 8 + 4 + j, step, stride=8), :] = h_cos * s_theta + h_sin * c_theta
-
-
-def template_spectra(lags, slots, line, waves, forward, phase, freqs):
+    fill_table([line_ref], forward, table, 0, freqs)
+
+
+def template_spectra(lags, line, waves, head, forward, phase, rows, freqs):
     count, length = waves.shape
     whole = pl.BlockSpec(memory_space=pltpu.VMEM)
     return pl.pallas_call(
@@ -96,12 +96,12 @@
         out_shape=[
             jax.ShapeDtypeStruct((count * 8, HOLD), jnp.float32),
             jax.ShapeDtypeStruct(line.shape, line.dtype),
-            jax.ShapeDtypeStruct(slots.shape, slots.dtype),
+            jax.ShapeDtypeStruct((rows * 8, HOLD), jnp.float32),
         ],
         compiler_params=pltpu.CompilerParams(vmem_limit_bytes=VMEM_K1),
         cost_estimate=pl.CostEstimate(flops=count * length * freqs * 4, bytes_accessed=count * 8 * HOLD * 4, transcendentals=0),
         name="template_spectra",
-    )(lags, slots, line, waves, forward, phase)
+    )(lags, line, waves, head, forward, phase)
 
 
 def join_kernel(*refs):
@@ -135,29 +135,58 @@
             table[pl.ds(start + 4, size, stride=8), :] = dft[:, freqs + j * HOLD : freqs + (j + 1) * HOLD]
 
 
-def record_kernel(freqs, *refs):
-    *blocks, forward_ref, table = refs
-    fill_table(blocks, forward_ref, table, 0, freqs)
-
-
-def record_spectra(blocks, forward, freqs, parts):
+def record_kernel(freqs, first, *refs):
+    *blocks, forward_ref, _, table = refs
+    fill_table(blocks, forward_ref, table, first, freqs)
+
+
+def record_spectra(blocks, forward, table, first, freqs):
     rows = sum(b.shape[0] for b in blocks)
     whole = pl.BlockSpec(memory_space=pltpu.VMEM)
     return pl.pallas_call(
-        functools.partial(record_kernel, freqs),
-        in_specs=[whole] * (len(blocks) + 1),
+        functools.partial(record_kernel, freqs, first),
+        in_specs=[whole] * (len(blocks) + 2),
         out_specs=whole,
-        out_shape=jax.ShapeDtypeStruct((parts * rows * 8, HOLD), jnp.float32),
+        out_shape=jax.ShapeDtypeStruct(table.shape, table.dtype),
+        input_output_aliases={len(blocks) + 1: 0},
         compiler_params=pltpu.CompilerParams(vmem_limit_bytes=VMEM_D1),
         cost_estimate=pl.CostEstimate(flops=rows * forward.shape[0] * freqs * 4, bytes_accessed=rows * 8 * HOLD * 4, transcendentals=0),
         name="record_spectra",
-    )(*blocks, forward)
-
-
-def detect_kernel(n_blocks, count, stations, freqs, slot_ref, *refs):
-    blocks, (_, q, forward_ref, high_ref, low_ref, main_ref, early_ref, table, acc) = refs[:n_blocks], refs[n_blocks:]
+    )(*blocks, forward, table)
+
+
+def inverse(parts, high, low):
+    count = parts.shape[0] // 2
+    both = jnp.dot(parts, high, preferred_element_type=jnp.float32)
+    return both[:count] + both[count:] + jnp.dot(parts[:count], low, preferred_element_type=jnp.float32)
+
+
+def inverse_kernel(parts_ref, high_ref, low_ref, main_ref):
+    columns = slice(0, main_ref.shape[1])
+    main_ref[...] = inverse(parts_ref[...], high_ref[:, columns], low_ref[:, columns])
+
+
+def own_window(parts, high, low, time_dev):
+    whole = pl.BlockSpec(memory_space=pltpu.VMEM)
+    count = parts.shape[0] // 2
+    return pl.pallas_call(
+        inverse_kernel,
+        in_specs=[whole] * 3,
+        out_specs=whole,
+        out_shape=jax.ShapeDtypeStruct((count, time_dev), jnp.float32),
+        compiler_params=pltpu.CompilerParams(vmem_limit_bytes=VMEM_D1),
+        cost_estimate=pl.CostEstimate(flops=6 * count * parts.shape[1] * time_dev, bytes_accessed=1 << 22, transcendentals=0),
+        name="own_window",
+    )(parts, high, low)
+
+
+def detect_kernel(n_blocks, count, stations, freqs, slots, *refs):
+    blocks, (_, q, forward_ref, high_ref, low_ref, parts_ref, early_ref, table, acc, slot_ref, sem) = refs[:n_blocks], refs[n_blocks:]
+    load = pltpu.make_async_copy(slots, slot_ref, sem)
+    load.start()
     chunks = freqs // HOLD
     fill_table(blocks, forward_ref, table, table.shape[0] // 16, freqs)
+    load.wait()
 
     def one(t, carry):
         first = [jnp.zeros((8, HOLD), jnp.float32)] * 2
@@ -180,11 +209,10 @@
     )
     top = joint.astype(jnp.bfloat16)
     rest = (joint - top.astype(jnp.float32)).astype(jnp.bfloat16)
-    both = jnp.dot(jnp.concatenate([top, rest], axis=0), high_ref[...], preferred_element_type=jnp.float32)
-    out = both[:count] + both[count:] + jnp.dot(top, low_ref[...], preferred_element_type=jnp.float32)
-    time_dev = main_ref.shape[1]
-    main_ref[...] = out[:, :time_dev]
-    early_ref[...] = out[:, time_dev:].astype(early_ref.dtype)
+    parts_ref[:count, :] = top
+    parts_ref[count:, :] = rest
+    columns = slice(high_ref.shape[1] - early_ref.shape[1], None)
+    early_ref[...] = inverse(parts_ref[...], high_ref[:, columns], low_ref[:, columns]).astype(early_ref.dtype)
 
 
 def detect(slots, blocks, table, q, forward, high, low, count, stations, freqs, time_dev):
@@ -192,16 +220,18 @@
     whole = pl.BlockSpec(memory_space=pltpu.VMEM)
     return pl.pallas_call(
         functools.partial(detect_kernel, len(blocks), count, stations, freqs),
-        in_specs=[pl.BlockSpec(memory_space=pltpu.SMEM)] + [whole] * (len(blocks) + 5),
+        in_specs=[whole] * (len(blocks) + 6),
         out_specs=[whole] * 3,
         out_shape=[
-            jax.ShapeDtypeStruct((count, time_dev), jnp.float32),
+            jax.ShapeDtypeStruct((2 * count, 2 * freqs), jnp.bfloat16),
             jax.ShapeDtypeStruct((count, time_dev // 2), jnp.bfloat16),
             jax.ShapeDtypeStruct(table.shape, table.dtype),
         ],
         input_output_aliases={1 + len(blocks): 2},
         scratch_shapes=[
             pltpu.VMEM((count * 16, HOLD), jnp.float32),
+            pltpu.SMEM(slots.shape, slots.dtype),
+            pltpu.SemaphoreType.DMA,
         ],
         compiler_params=pltpu.CompilerParams(vmem_limit_bytes=VMEM_K2),
         cost_estimate=pl.CostEstimate(flops=rows * time_dev * freqs * 4, bytes_accessed=count * stations * 8 * HOLD * 4, transcendentals=0),
@@ -232,15 +262,17 @@
     place = ((apart & 1) * 16 + rank_x * 4 + rank_z) * per + channels % per
     slots = (place * 8).reshape(-1, stations)
 
-    own, waves, head, phase = load([records, templates.reshape(-1, length), forward[:length], phase])
+    waves, lags = templates.reshape(-1, length), moveouts.reshape(-1, HOLD)
+    own, waves, head, forward, phase, lags, slots, high, low = load(
+        [records, waves, forward[:length], forward, phase, lags, slots, high, low]
+    )
     line = join([own] + [swap(records, (0, d, 0)) for d in Z_ORDER])
     plane = [swap(line, (d, 0, 0)) for d in X_ORDER]
-    q, line_q, slots = template_spectra(moveouts.reshape(-1, HOLD), slots, line, waves, head, phase, freqs)
-    near = [line] + plane
+    q, line_q, table = template_spectra(lags, line, waves, head, forward, phase, 32 * per, freqs)
     far = [swap(block, (0, 0, 1)) for block in [line_q] + plane]
-    table = record_spectra(near, forward, freqs, 2)
-
-    main, early = detect(slots, far, table, q, forward, high, low, batches * count, stations, freqs, time_dev)
+    table = record_spectra(plane, forward, table, line.shape[0], freqs)
+    parts, early = detect(slots, far, table, q, forward, high, low, batches * count, stations, freqs, time_dev)
+    main = own_window(parts, high, low, time_dev)
     earlier = lax.ppermute(early, "tm", [(i, i - 1) for i in range(1, lax.axis_size("tm"))])
     earlier = earlier.astype(jnp.float32)
     out = main + jnp.pad(earlier, ((0, 0), (time_dev - earlier.shape[1], 0)))

time: 39 us -> 40.3 us (1.033)
  waiting for transfers between devices: 10.1 us -> 7.56 us
  other arithmetic: 0.72 us -> 2.09 us
  local copies, waits for them, and re-layouts: 0.1 us -> 1.43 us
  Pallas kernels: 11.5 us -> 12.5 us
    ppermute x10, waiting for transfers between devices: 2.77 us -> 0.37 us  [per_device(): swap = lambda block, change: lax.ppermute(block, 'tmpl', route(change))]
    mul x1, other arithmetic: 0.06 us -> 1.43 us  [per_device(): slots = (place * 8).reshape(-1, stations)]
    reshape x1, local copies, waits for them, and re-layouts: 0.08 us -> 1.43 us  [per_device(): waves, lags = (templates.reshape(-1, length), moveouts.reshape(-1, HOLD))]
    pallas_call x1, Pallas kernels: 1.55 us -> 2.62 us  [load(): pl.pallas_call(functools.partial(load_kernel, len(arrays)), in_specs=[pl....]
    pallas_call x1, Pallas kernels: 5.35 us -> 4.73 us  [detect(): pl.pallas_call(functools.partial(detect_kernel, len(blocks), count, stati...]
    pallas_call x1 -> x2, Pallas kernels: 0.87 us -> 1.06 us  [the longest x1 0.68 us: record_spectra(): pl.pallas_call(functools.partial(record_kernel, freqs, first), in_specs=[...]
  transfers between devices with their start and end apart: 11 -> 11, of which waited for: 3 -> 2; matrix products, arithmetic and copies ran while one was open for 0% -> 7% of each run, Pallas kernels for 16% -> 19%
where the time goes in v6:
time: 40.3 us; the launch traced here: 40.1 us
  starting transfers between devices  16.4 us (41%)
  Pallas kernels  12.5 us (31%)
  waiting for transfers between devices  7.56 us (19%)
  other arithmetic  2.09 us (5%)
  local copies, waits for them, and re-layouts  1.43 us (4%)
    ppermute x10, starting transfers between devices, per_device(): swap = lambda block, change: lax.ppermute(block, 'tmpl', route(change))  15.1 us
    ppermute x1, waiting for transfers between devices, per_device(): lax.ppermute(early, 'tm', [(i, i - 1) for i in range(1, lax.axis_size('tm...  7.19 us
    pallas_call x1, Pallas kernels, detect(): pl.pallas_call(functools.partial(detect_kernel, len(blocks), count, stati...  4.73 us
    pallas_call x1, Pallas kernels, template_spectra(): pl.pallas_call(functools.partial(template_kernel, 512, freqs), in_specs=[...  4.06 us
    pallas_call x1, Pallas kernels, load(): pl.pallas_call(functools.partial(load_kernel, len(arrays)), in_specs=[pl....  2.62 us
    reshape x1, local copies, waits for them, and re-layouts, per_device(): waves, lags = (templates.reshape(-1, length), moveouts.reshape(-1, HOLD))  1.43 us
    mul x1, other arithmetic, per_device(): slots = (place * 8).reshape(-1, stations)  1.43 us
    ppermute x1, starting transfers between devices, per_device(): lax.ppermute(early, 'tm', [(i, i - 1) for i in range(1, lax.axis_size('tm...  1.29 us
  transfers between devices with their start and end apart: 11, of which 2 were waited for; matrix products, arithmetic and copies ran while one was open for 7% of the time, Pallas kernels for 19%

profile of v6, /device:TPU:1, one launch (start us, length us, event | category | flops | bytes accessed | tf_op | source)
XLA Modules:
  0.0 40.1 jit_solution(2946028163600688814)
XLA Ops:
  0.0 5.2 %collective-permute-start = (bf16[48,512]{1,0:T(8,128)(2,1)}, bf16[48,512]{1,0:T(8,128)(2,1)S(1)}, u32[]{:S(2)}, u32[]{:S(2)}) collective-permute-start(bf16[48,512]{1,0:T(8,128)(2,1)} %refs_0_.1), channel_id=1, source_target_pairs={{0,48},{8,56},{16,32},{24,40},{32,16},{40,24},{48,0},{56,8},{64,11... | collective-permute-start | bytes 147464 | tf_op jit(solution)/shard_map/ppermute | solution.py:257
  5.2 0.0 collective-permute-start.1
  5.2 0.3 collective-permute-start.2
  5.5 1.4 %fusion.2 = s32[2,32,48]{2,1,0:T(8,128)} fusion(s32[2,32,48]{2,1,0:T(8,128)} %param.10, s32[]{:T(128)S(6)} %axis_index.15), kind=kLoop, calls=%fused_computation.5 | loop fusion | flops 86016 | bytes 24580 | tf_op jit(solution)/shard_map/mul | solution.py:263
  6.9 1.4 %reshape.13.refs_5_ = s32[24,128]{1,0:T(8,128)} reshape(s32[2,32,48]{2,1,0:T(8,128)} %param.11) | data formatting | bytes 24576 | tf_op jit(solution)/shard_map/reshape | solution.py:265
  8.3 2.6 %load.1 = (bf16[48,512]{1,0:T(8,128)(2,1)S(1)}, bf16[3072,200]{1,0:T(8,128)(2,1)S(1)}, bf16[200,768]{1,0:T(8,128)(2,1)S(1)}, bf16[512,768]{1,0:T(8,128)(2,1)S(1)...) custom-call(bf16[48,512]{1,0:T(8,128)(2,1)} %refs_0_.1, ...), custom_call_target="tpu_custom_call" | custom-call | tf_op jit(solution)/shard_map/load/pallas_call | solution.py:62
  11.0 0.0 collective-permute-done.refs_1_
  11.0 0.0 collective-permute-done.1.refs_2_
  11.0 0.0 collective-permute-done.2.refs_3_
  11.0 2.8 %collective-permute-start.4 = (bf16[192,512]{1,0:T(8,128)(2,1)S(1)}, bf16[192,512]{1,0:T(8,128)(2,1)S(1)}, u32[]{:S(2)}, u32[]{:S(2)}) collective-permute-start(bf16[192,512]{1,0:T(8,128)(2,1)S(1)} %join.1.line_ref), channel_id=1, source_target_pairs={{0,128},{8,136},{16,144},{24,152},{32,160},{40,168},{48,176},{56,1... | collective-permute-start | bytes 589832 | tf_op jit(solution)/shard_map/ppermute | solution.py:257
  13.8 0.3 collective-permute-start.6
  14.2 0.6 %collective-permute-start.8 = (bf16[192,512]{1,0:T(8,128)(2,1)S(1)}, bf16[192,512]{1,0:T(8,128)(2,1)S(1)}, u32[]{:S(2)}, u32[]{:S(2)}) collective-permute-start(bf16[192,512]{1,0:T(8,128)(2,1)S(1)} %join.1.line_ref), channel_id=1, source_target_pairs={{0,192},{8,200},{16,208},{24,216},{32,224},{40,232},{48,240},{56,2... | collective-permute-start | bytes 589832 | tf_op jit(solution)/shard_map/ppermute | solution.py:257
  14.7 4.1 %template_spectra.1 = (f32[24576,128]{1,0:T(8,128)S(1)}, bf16[192,512]{1,0:T(8,128)(2,1)S(1)}, f32[12288,128]{1,0:T(8,128)S(1)}) custom-call(s32[24,128]{1,0:T(8,128)S(1)} %get-tuple-element.20.lag_ref, bf16[192,512]{1,0:T(8,128)(2,1)S(1)} %join.1.line_ref, bf16[3072,200]{1,0:T(8,128)(2,1)S(1)} %get-tuple-element.22.waves, ...), custom_call_target="tpu_custom_call" | custom-call | flops 943718400 | bytes 12582912 | tf_op jit(solution)/shard_map/template_spectra/pallas_call | solution.py:92
  18.8 2.7 %collective-permute-start.3 = (bf16[192,512]{1,0:T(8,128)(2,1)S(1)}, bf16[192,512]{1,0:T(8,128)(2,1)S(1)}, u32[]{:S(2)}, u32[]{:S(2)}) collective-permute-start(bf16[192,512]{1,0:T(8,128)(2,1)S(1)} %get-tuple-element.26), channel_id=1, source_target_pairs={{0,8},{8,0},{16,24},{24,16},{32,40},{40,32},{48,56},{56,48},{64,72... | collective-permute-start | bytes 589832 | tf_op jit(solution)/shard_map/ppermute | solution.py:257
  21.5 0.0 collective-permute-done.4.refs_0_
  21.5 0.6 %collective-permute-start.5 = (bf16[192,512]{1,0:T(8,128)(2,1)S(1)}, bf16[192,512]{1,0:T(8,128)(2,1)S(1)}, u32[]{:S(2)}, u32[]{:S(2)}) collective-permute-start(bf16[192,512]{1,0:T(8,128)(2,1)S(1)} %collective-permute-done.4.refs_0_), channel_id=1, source_target_pairs={{0,8},{8,0},{16,24},{24,16},{32,40},{40,32},{48,56},{56,48},{64,72... | collective-permute-start | bytes 589832 | tf_op jit(solution)/shard_map/ppermute | solution.py:257
  22.1 0.0 collective-permute-done.6.refs_1_
  22.1 2.1 %collective-permute-start.7 = (bf16[192,512]{1,0:T(8,128)(2,1)S(1)}, bf16[192,512]{1,0:T(8,128)(2,1)S(1)}, u32[]{:S(2)}, u32[]{:S(2)}) collective-permute-start(bf16[192,512]{1,0:T(8,128)(2,1)S(1)} %collective-permute-done.6.refs_1_), channel_id=1, source_target_pairs={{0,8},{8,0},{16,24},{24,16},{32,40},{40,32},{48,56},{56,48},{64,72... | collective-permute-start | bytes 589832 | tf_op jit(solution)/shard_map/ppermute | solution.py:257
  24.2 0.0 collective-permute-done.8.refs_2_
  24.2 0.5 %collective-permute-start.9 = (bf16[192,512]{1,0:T(8,128)(2,1)S(1)}, bf16[192,512]{1,0:T(8,128)(2,1)S(1)}, u32[]{:S(2)}, u32[]{:S(2)}) collective-permute-start(bf16[192,512]{1,0:T(8,128)(2,1)S(1)} %collective-permute-done.8.refs_2_), channel_id=1, source_target_pairs={{0,8},{8,0},{16,24},{24,16},{32,40},{40,32},{48,56},{56,48},{64,72... | collective-permute-start | bytes 589832 | tf_op jit(solution)/shard_map/ppermute | solution.py:257
  24.7 0.7 %record_spectra.1.refs_4_ = f32[12288,128]{1,0:T(8,128)S(1)} custom-call(bf16[192,512]{1,0:T(8,128)(2,1)S(1)} %collective-permute-done.4.refs_0_, bf16[192,512]{1,0:T(8,128)(2,1)S(1)} %collective-permute-done.6.refs_1_, bf16[192,512]{1,0:T(8,128)(2,1)S(1)} %collective-permute-done.8.refs_2_, ...), custom_call_target="tpu_custom_call", output_to_operand_aliasing={{}: (4, {})} | custom-call | flops 452984832 | bytes 2359296 | tf_op jit(solution)/shard_map/record_spectra/pallas_call | solution.py:146
  25.4 0.0 collective-permute-done.3.refs_0_
  25.4 0.0 collective-permute-done.5.refs_1_
  25.5 0.0 collective-permute-done.7.refs_2_
  25.5 0.3 collective-permute-done.9.refs_3_
  25.8 4.7 %detect.1 = (bf16[128,768]{1,0:T(8,128)(2,1)S(1)}, bf16[64,256]{1,0:T(8,128)(2,1)S(1)}, f32[12288,128]{1,0:T(8,128)S(1)}) custom-call(s32[64,48]{1,0:T(8,128)S(1)} %get-tuple-element.19.slots, bf16[192,512]{1,0:T(8,128)(2,1)S(1)} %collective-permute-done.3.refs_0_, ...), custom_call_target="tpu_custom_call", output_to_operand_aliasing={{2}: (5, {})} | custom-call | flops 603979776 | bytes 12582912 | tf_op jit(solution)/shard_map/detect/pallas_call | solution.py:221
  30.6 1.3 %collective-permute-start.10 = (bf16[64,256]{1,0:T(8,128)(2,1)S(1)}, bf16[64,256]{1,0:T(8,128)(2,1)S(1)}, u32[]{:S(2)}, u32[]{:S(2)}) collective-permute-start(bf16[64,256]{1,0:T(8,128)(2,1)S(1)} %get-tuple-element.32), channel_id=1, source_target_pairs={{1,0},{2,1},{3,2},{4,3},{5,4},{6,5},{7,6},{9,8},{10,9},{11,10},{12... | collective-permute-start | bytes 98312 | tf_op jit(solution)/shard_map/ppermute | solution.py:276
  31.9 0.4 own_window.1
  32.2 7.2 %collective-permute-done.10 = bf16[64,256]{1,0:T(8,128)(2,1)S(1)} collective-permute-done((bf16[64,256]{1,0:T(8,128)(2,1)S(1)}, bf16[64,256]{1,0:T(8,128)(2,1)S(1)}, u32[]{:S(2)}, u32[]{:S(2)}) %collective-permute-start.10) | collective-permute-done | bytes 32800 | tf_op jit(solution)/shard_map/ppermute | solution.py:276
  39.4 0.7 %convert_add_fusion = f32[64,512]{1,0:T(8,128)} fusion(f32[64,512]{1,0:T(8,128)S(1)} %own_window.1, bf16[64,256]{1,0:T(8,128)(2,1)S(1)} %collective-permute-done.10), kind=kLoop, calls=%fused_computation | loop fusion | flops 65536 | bytes 294912 | tf_op jit(solution)/shard_map/add | solution.py:278
  (1 shorter events, 0.0 us)
Async XLA Ops:
  0.0 11.0 %collective-permute-start = (bf16[48,512]{1,0:T(8,128)(2,1)}, bf16[48,512]{1,0:T(8,128)(2,1)S(1)}, u32[]{:S(2)}, u32[]{:S(2)}) collective-permute-start(bf16[48,512]{1,0:T(8,128)(2,1)} %refs_0_.1), channel_id=1, source_target_pairs={{0,48},{8,56},{16,32},{24,40},{32,16},{40,24},{48,0},{56,8},{64,11... | collective-permute-start | bytes 147464 | tf_op jit(solution)/shard_map/ppermute | solution.py:257
  5.2 5.8 %collective-permute-start.1 = (bf16[48,512]{1,0:T(8,128)(2,1)}, bf16[48,512]{1,0:T(8,128)(2,1)S(1)}, u32[]{:S(2)}, u32[]{:S(2)}) collective-permute-start(bf16[48,512]{1,0:T(8,128)(2,1)} %refs_0_.1), channel_id=1, source_target_pairs={{0,32},{8,40},{16,48},{24,56},{32,0},{40,8},{48,16},{56,24},{64,96... | collective-permute-start | bytes 147464 | tf_op jit(solution)/shard_map/ppermute | solution.py:257
  5.2 5.8 %collective-permute-start.2 = (bf16[48,512]{1,0:T(8,128)(2,1)}, bf16[48,512]{1,0:T(8,128)(2,1)S(1)}, u32[]{:S(2)}, u32[]{:S(2)}) collective-permute-start(bf16[48,512]{1,0:T(8,128)(2,1)} %refs_0_.1), channel_id=1, source_target_pairs={{0,16},{8,24},{16,0},{24,8},{32,48},{40,56},{48,32},{56,40},{64,80... | collective-permute-start | bytes 147464 | tf_op jit(solution)/shard_map/ppermute | solution.py:257
  11.0 10.5 %collective-permute-start.4 = (bf16[192,512]{1,0:T(8,128)(2,1)S(1)}, bf16[192,512]{1,0:T(8,128)(2,1)S(1)}, u32[]{:S(2)}, u32[]{:S(2)}) collective-permute-start(bf16[192,512]{1,0:T(8,128)(2,1)S(1)} %join.1.line_ref), channel_id=1, source_target_pairs={{0,128},{8,136},{16,144},{24,152},{32,160},{40,168},{48,176},{56,1... | collective-permute-start | bytes 589832 | tf_op jit(solution)/shard_map/ppermute | solution.py:257
  13.8 8.3 %collective-permute-start.6 = (bf16[192,512]{1,0:T(8,128)(2,1)S(1)}, bf16[192,512]{1,0:T(8,128)(2,1)S(1)}, u32[]{:S(2)}, u32[]{:S(2)}) collective-permute-start(bf16[192,512]{1,0:T(8,128)(2,1)S(1)} %join.1.line_ref), channel_id=1, source_target_pairs={{0,64},{8,72},{16,80},{24,88},{32,96},{40,104},{48,112},{56,120},{... | collective-permute-start | bytes 589832 | tf_op jit(solution)/shard_map/ppermute | solution.py:257
  14.2 10.1 %collective-permute-start.8 = (bf16[192,512]{1,0:T(8,128)(2,1)S(1)}, bf16[192,512]{1,0:T(8,128)(2,1)S(1)}, u32[]{:S(2)}, u32[]{:S(2)}) collective-permute-start(bf16[192,512]{1,0:T(8,128)(2,1)S(1)} %join.1.line_ref), channel_id=1, source_target_pairs={{0,192},{8,200},{16,208},{24,216},{32,224},{40,232},{48,240},{56,2... | collective-permute-start | bytes 589832 | tf_op jit(solution)/shard_map/ppermute | solution.py:257
  18.8 6.7 %collective-permute-start.3 = (bf16[192,512]{1,0:T(8,128)(2,1)S(1)}, bf16[192,512]{1,0:T(8,128)(2,1)S(1)}, u32[]{:S(2)}, u32[]{:S(2)}) collective-permute-start(bf16[192,512]{1,0:T(8,128)(2,1)S(1)} %get-tuple-element.26), channel_id=1, source_target_pairs={{0,8},{8,0},{16,24},{24,16},{32,40},{40,32},{48,56},{56,48},{64,72... | collective-permute-start | bytes 589832 | tf_op jit(solution)/shard_map/ppermute | solution.py:257
  21.5 3.9 %collective-permute-start.5 = (bf16[192,512]{1,0:T(8,128)(2,1)S(1)}, bf16[192,512]{1,0:T(8,128)(2,1)S(1)}, u32[]{:S(2)}, u32[]{:S(2)}) collective-permute-start(bf16[192,512]{1,0:T(8,128)(2,1)S(1)} %collective-permute-done.4.refs_0_), channel_id=1, source_target_pairs={{0,8},{8,0},{16,24},{24,16},{32,40},{40,32},{48,56},{56,48},{64,72... | collective-permute-start | bytes 589832 | tf_op jit(solution)/shard_map/ppermute | solution.py:257
  22.1 3.3 %collective-permute-start.7 = (bf16[192,512]{1,0:T(8,128)(2,1)S(1)}, bf16[192,512]{1,0:T(8,128)(2,1)S(1)}, u32[]{:S(2)}, u32[]{:S(2)}) collective-permute-start(bf16[192,512]{1,0:T(8,128)(2,1)S(1)} %collective-permute-done.6.refs_1_), channel_id=1, source_target_pairs={{0,8},{8,0},{16,24},{24,16},{32,40},{40,32},{48,56},{56,48},{64,72... | collective-permute-start | bytes 589832 | tf_op jit(solution)/shard_map/ppermute | solution.py:257
  24.2 1.6 %collective-permute-start.9 = (bf16[192,512]{1,0:T(8,128)(2,1)S(1)}, bf16[192,512]{1,0:T(8,128)(2,1)S(1)}, u32[]{:S(2)}, u32[]{:S(2)}) collective-permute-start(bf16[192,512]{1,0:T(8,128)(2,1)S(1)} %collective-permute-done.8.refs_2_), channel_id=1, source_target_pairs={{0,8},{8,0},{16,24},{24,16},{32,40},{40,32},{48,56},{56,48},{64,72... | collective-permute-start | bytes 589832 | tf_op jit(solution)/shard_map/ppermute | solution.py:257
  30.6 8.9 %collective-permute-start.10 = (bf16[64,256]{1,0:T(8,128)(2,1)S(1)}, bf16[64,256]{1,0:T(8,128)(2,1)S(1)}, u32[]{:S(2)}, u32[]{:S(2)}) collective-permute-start(bf16[64,256]{1,0:T(8,128)(2,1)S(1)} %get-tuple-element.32), channel_id=1, source_target_pairs={{1,0},{2,1},{3,2},{4,3},{5,4},{6,5},{7,6},{9,8},{10,9},{11,10},{12... | collective-permute-start | bytes 98312 | tf_op jit(solution)/shard_map/ppermute | solution.py:276

commit v7 on v6

--- a/solution.py
+++ b/solution.py
@@ -14,6 +14,7 @@
 EXTRA = L + LAGS - 2
 HOLD = 128
 LAG_ROWS = 64
+SPREAD_ROWS = 64
 Z_ORDER = (3, 2, 1)
 X_ORDER = (2, 1, 3)
 VMEM_K1 = 12 << 20
@@ -49,32 +50,61 @@
     return high, (table - high.astype(np.float32)).astype(jnp.bfloat16)
 
 
-def load_kernel(count, *refs):
-    sources, targets, sems = refs[:count], refs[count:-1], refs[-1]
+def load_kernel(count, per, *refs):
+    sources, (*targets, slot_ref, channel_ref, sems) = refs[:count], refs[count:]
+    targets = [channel_ref, *targets]
     copies = [pltpu.make_async_copy(src, dst, sems.at[n]) for n, (src, dst) in enumerate(zip(sources, targets))]
     for copy in copies:
         copy.start()
-    for copy in copies:
+    copies[0].wait()
+    channel = channel_ref[...]
+    owner = (channel * reciprocal(per)) >> 16
+    apart = owner ^ lax.axis_index("tmpl")
+    rank_z = (position_bits(Z_ORDER) >> (apart & 6)) & 3
+    rank_x = (position_bits(X_ORDER) >> ((apart >> 2) & 6)) & 3
+    slot_ref[...] = (((apart & 1) * 16 + rank_x * 4 + rank_z) * per + channel - owner * per) * 8
+    for copy in copies[1:]:
         copy.wait()
 
 
-def load(arrays):
-    return pl.pallas_call(
-        functools.partial(load_kernel, len(arrays)),
-        in_specs=[pl.BlockSpec(memory_space=pltpu.HBM)] * len(arrays),
-        out_specs=[pl.BlockSpec(memory_space=pltpu.VMEM)] * len(arrays),
-        out_shape=[jax.ShapeDtypeStruct(a.shape, a.dtype) for a in arrays],
-        scratch_shapes=[pltpu.SemaphoreType.DMA((len(arrays),))],
-        compiler_params=pltpu.CompilerParams(vmem_limit_bytes=8 << 20),
+def reciprocal(per):
+    m = (1 << 16) // per + 1
+    n = np.arange(32 * per)
+    assert (n * m >> 16 == n // per).all()
+    return m
+
+
+def load(arrays, channels, per):
+    whole = pl.BlockSpec(memory_space=pltpu.VMEM)
+    return pl.pallas_call(
+        functools.partial(load_kernel, len(arrays) + 1, per),
+        in_specs=[pl.BlockSpec(memory_space=pltpu.HBM)] * (len(arrays) + 1),
+        out_specs=[whole] * (len(arrays) + 1),
+        out_shape=[jax.ShapeDtypeStruct(a.shape, a.dtype) for a in (*arrays, channels)],
+        scratch_shapes=[pltpu.VMEM(channels.shape, channels.dtype), pltpu.SemaphoreType.DMA((len(arrays) + 1,))],
+        compiler_params=pltpu.CompilerParams(vmem_limit_bytes=12 << 20),
         name="load",
-    )(*(pltpu.with_memory_space_constraint(a, pltpu.HBM) for a in arrays))
-
-
-def template_kernel(step, freqs, lag_ref, line_ref, waves, head, forward, phases, out, line_out, table):
+    )(*(pltpu.with_memory_space_constraint(a, pltpu.HBM) for a in (channels, *arrays)))
+
+
+def spread_table(stations):
+    at = np.arange(8 * stations)
+    spread = np.zeros((SPREAD_ROWS + 16, 8 * stations), jnp.bfloat16)
+    spread[at % stations, at] = 1
+    spread[SPREAD_ROWS + at // stations, at] = 1
+    return spread
+
+
+def template_kernel(step, freqs, lag_ref, spread_ref, line_ref, waves, head, forward, phases, out, line_out, table):
     line_out[...] = line_ref[...]
+    stations = lag_ref.shape[1]
+    lags = lag_ref[...].astype(jnp.float32).astype(jnp.bfloat16)
+    lags = jnp.dot(lags, spread_ref[:stations, :], preferred_element_type=jnp.float32)
+    stretch = spread_ref[pl.ds(SPREAD_ROWS, 8), :].astype(jnp.float32)
+    lag_row = (lax.broadcasted_iota(jnp.int32, (2 * LAG_ROWS, step), 0) & (LAG_ROWS - 1)).astype(jnp.float32)
     for start in range(0, waves.shape[0], step):
-        lag = jnp.concatenate([lag_ref[pl.ds((start + at) // HOLD, 1), :] for at in range(0, step, HOLD)], axis=1)
-        lag_row = lax.broadcasted_iota(jnp.int32, (2 * LAG_ROWS, step), 0) & (LAG_ROWS - 1)
+        group = start // stations
+        lag = jnp.sum(lags[group : group + 8] * stretch, axis=0, keepdims=True)
         chosen = (lag_row == lag).astype(jnp.float32).astype(jnp.bfloat16)
         phase = lax.dot_general(chosen, phases[...], (((0,), (0,)), ((), ())), preferred_element_type=jnp.float32)
         dft = jnp.dot(waves[pl.ds(start, step), :], head[...], preferred_element_type=jnp.float32)
@@ -86,12 +116,12 @@
     fill_table([line_ref], forward, table, 0, freqs)
 
 
-def template_spectra(lags, line, waves, head, forward, phase, rows, freqs):
+def template_spectra(lags, spread, line, waves, head, forward, phase, rows, freqs):
     count, length = waves.shape
     whole = pl.BlockSpec(memory_space=pltpu.VMEM)
     return pl.pallas_call(
-        functools.partial(template_kernel, 512, freqs),
-        in_specs=[whole] * 6,
+        functools.partial(template_kernel, 8 * lags.shape[1], freqs),
+        in_specs=[whole] * 7,
         out_specs=[whole] * 3,
         out_shape=[
             jax.ShapeDtypeStruct((count * 8, HOLD), jnp.float32),
@@ -101,7 +131,7 @@
         compiler_params=pltpu.CompilerParams(vmem_limit_bytes=VMEM_K1),
         cost_estimate=pl.CostEstimate(flops=count * length * freqs * 4, bytes_accessed=count * 8 * HOLD * 4, transcendentals=0),
         name="template_spectra",
-    )(lags, line, waves, head, forward, phase)
+    )(lags, spread, line, waves, head, forward, phase)
 
 
 def join_kernel(*refs):
@@ -256,19 +286,25 @@
     forward, phase, high, low = (jnp.asarray(t) for t in host_tables(time_dev))
     swap = lambda block, change: lax.ppermute(block, "tmpl", route(change))
 
-    apart = (channels // per) ^ lax.axis_index("tmpl")
-    rank_z = (position_bits(Z_ORDER) >> (apart & 6)) & 3
-    rank_x = (position_bits(X_ORDER) >> ((apart >> 2) & 6)) & 3
-    place = ((apart & 1) * 16 + rank_x * 4 + rank_z) * per + channels % per
-    slots = (place * 8).reshape(-1, stations)
-
-    waves, lags = templates.reshape(-1, length), moveouts.reshape(-1, HOLD)
-    own, waves, head, forward, phase, lags, slots, high, low = load(
-        [records, waves, forward[:length], forward, phase, lags, slots, high, low]
+    spread = jnp.asarray(spread_table(stations))
+    own, waves, head, forward, phase, lags, spread, high, low, slots = load(
+        [
+            records,
+            templates.reshape(-1, length),
+            forward[:length],
+            forward,
+            phase,
+            moveouts.reshape(-1, stations),
+            spread,
+            high,
+            low,
+        ],
+        channels.reshape(-1, stations),
+        per,
     )
     line = join([own] + [swap(records, (0, d, 0)) for d in Z_ORDER])
     plane = [swap(line, (d, 0, 0)) for d in X_ORDER]
-    q, line_q, table = template_spectra(lags, line, waves, head, forward, phase, 32 * per, freqs)
+    q, line_q, table = template_spectra(lags, spread, line, waves, head, forward, phase, 32 * per, freqs)
     far = [swap(block, (0, 0, 1)) for block in [line_q] + plane]
     table = record_spectra(plane, forward, table, line.shape[0], freqs)
     parts, early = detect(slots, far, table, q, forward, high, low, batches * count, stations, freqs, time_dev)

time: 40.3 us -> 39.2 us (0.973)
  waiting for transfers between devices: 7.56 us -> 9.66 us
  local copies, waits for them, and re-layouts: 1.43 us -> 0 us
  other arithmetic: 2.09 us -> 0.67 us
    ppermute x10, waiting for transfers between devices: 0.37 us -> 2.25 us  [per_device(): swap = lambda block, change: lax.ppermute(block, 'tmpl', route(change))]
    reshape x1 -> x0, local copies, waits for them, and re-layouts: 1.43 us -> none  [per_device(): waves, lags = (templates.reshape(-1, length), moveouts.reshape(-1, HOLD))]
    mul x1 -> x0, other arithmetic: 1.43 us -> none  [per_device(): slots = (place * 8).reshape(-1, stations)]
  transfers between devices with their start and end apart: 11 -> 11, of which waited for: 2 -> 4; matrix products, arithmetic and copies ran while one was open for 7% -> 0% of each run, Pallas kernels for 19% -> 19%
where the time goes in v7:
time: 39.2 us; the launch traced here: 39.1 us
  starting transfers between devices  16.3 us (42%)
  Pallas kernels  12.4 us (32%)
  waiting for transfers between devices  9.66 us (25%)
  other arithmetic  0.67 us (2%)
    ppermute x10, starting transfers between devices, per_device(): swap = lambda block, change: lax.ppermute(block, 'tmpl', route(change))  15 us
    ppermute x1, waiting for transfers between devices, per_device(): lax.ppermute(early, 'tm', [(i, i - 1) for i in range(1, lax.axis_size('tm...  7.41 us
    pallas_call x1, Pallas kernels, detect(): pl.pallas_call(functools.partial(detect_kernel, len(blocks), count, stati...  4.74 us
    pallas_call x1, Pallas kernels, template_spectra(): pl.pallas_call(functools.partial(template_kernel, 8 * lags.shape[1], freq...  3.88 us
    pallas_call x1, Pallas kernels, load(): pl.pallas_call(functools.partial(load_kernel, len(arrays) + 1, per), in_s...  2.66 us
    ppermute x10, waiting for transfers between devices, per_device(): swap = lambda block, change: lax.ppermute(block, 'tmpl', route(change))  2.25 us
    ppermute x1, starting transfers between devices, per_device(): lax.ppermute(early, 'tm', [(i, i - 1) for i in range(1, lax.axis_size('tm...  1.29 us
  transfers between devices with their start and end apart: 11, of which 4 were waited for; matrix products, arithmetic and copies ran while one was open for 0% of the time, Pallas kernels for 19%

profile of v7, /device:TPU:1, one launch (start us, length us, event | category | flops | bytes accessed | tf_op | source)
XLA Modules:
  0.0 39.1 jit_solution(7232174564656368590)
XLA Ops:
  0.0 5.2 %collective-permute-start = (bf16[48,512]{1,0:T(8,128)(2,1)}, bf16[48,512]{1,0:T(8,128)(2,1)S(1)}, u32[]{:S(2)}, u32[]{:S(2)}) collective-permute-start(bf16[48,512]{1,0:T(8,128)(2,1)} %refs_1_.1), channel_id=1, source_target_pairs={{0,48},{8,56},{16,32},{24,40},{32,16},{40,24},{48,0},{56,8},{64,11... | collective-permute-start | bytes 147464 | tf_op jit(solution)/shard_map/ppermute | solution.py:287
  5.2 0.0 collective-permute-start.1
  5.2 0.3 collective-permute-start.2
  5.5 2.7 %load.1 = (bf16[48,512]{1,0:T(8,128)(2,1)S(1)}, bf16[3072,200]{1,0:T(8,128)(2,1)S(1)}, bf16[200,768]{1,0:T(8,128)(2,1)S(1)}, bf16[512,768]{1,0:T(8,128)(2,1)S(1)...) custom-call(s32[64,48]{1,0:T(8,128)} %bitcast.5, ...), custom_call_target="tpu_custom_call" | custom-call | tf_op jit(solution)/shard_map/load/pallas_call | solution.py:79
  8.1 0.0 collective-permute-done.refs_1_
  8.1 1.7 %collective-permute-done.1.refs_2_ = bf16[48,512]{1,0:T(8,128)(2,1)S(1)} collective-permute-done((bf16[48,512]{1,0:T(8,128)(2,1)}, bf16[48,512]{1,0:T(8,128)(2,1)S(1)}, u32[]{:S(2)}, u32[]{:S(2)}) %collective-permute-start.1) | collective-permute-done | bytes 49184 | tf_op jit(solution)/shard_map/ppermute | solution.py:287
  9.9 0.0 collective-permute-done.2.refs_3_
  9.9 2.8 %collective-permute-start.4 = (bf16[192,512]{1,0:T(8,128)(2,1)S(1)}, bf16[192,512]{1,0:T(8,128)(2,1)S(1)}, u32[]{:S(2)}, u32[]{:S(2)}) collective-permute-start(bf16[192,512]{1,0:T(8,128)(2,1)S(1)} %join.1.line_ref), channel_id=1, source_target_pairs={{0,128},{8,136},{16,144},{24,152},{32,160},{40,168},{48,176},{56,1... | collective-permute-start | bytes 589832 | tf_op jit(solution)/shard_map/ppermute | solution.py:287
  12.7 0.3 collective-permute-start.6
  13.0 0.6 %collective-permute-start.8 = (bf16[192,512]{1,0:T(8,128)(2,1)S(1)}, bf16[192,512]{1,0:T(8,128)(2,1)S(1)}, u32[]{:S(2)}, u32[]{:S(2)}) collective-permute-start(bf16[192,512]{1,0:T(8,128)(2,1)S(1)} %join.1.line_ref), channel_id=1, source_target_pairs={{0,192},{8,200},{16,208},{24,216},{32,224},{40,232},{48,240},{56,2... | collective-permute-start | bytes 589832 | tf_op jit(solution)/shard_map/ppermute | solution.py:287
  13.6 3.9 %template_spectra.1 = (f32[24576,128]{1,0:T(8,128)S(1)}, bf16[192,512]{1,0:T(8,128)(2,1)S(1)}, f32[12288,128]{1,0:T(8,128)S(1)}) custom-call(s32[64,48]{1,0:T(8,128)S(1)} %get-tuple-element.21.lag_ref, bf16[80,384]{1,0:T(8,128)(2,1)S(1)} %get-tuple-element.22.spread_ref, bf16[192,512]{1,0:T(8,128)(2,1)S(1)} %join.1.line_ref, ...), custom_call_target="tpu_custom_call" | custom-call | flops 943718400 | bytes 12582912 | tf_op jit(solution)/shard_map/template_spectra/pallas_call | solution.py:122
  17.5 2.1 %collective-permute-start.3 = (bf16[192,512]{1,0:T(8,128)(2,1)S(1)}, bf16[192,512]{1,0:T(8,128)(2,1)S(1)}, u32[]{:S(2)}, u32[]{:S(2)}) collective-permute-start(bf16[192,512]{1,0:T(8,128)(2,1)S(1)} %get-tuple-element.28), channel_id=1, source_target_pairs={{0,8},{8,0},{16,24},{24,16},{32,40},{40,32},{48,56},{56,48},{64,72... | collective-permute-start | bytes 589832 | tf_op jit(solution)/shard_map/ppermute | solution.py:287
  19.6 0.0 collective-permute-done.4.refs_0_
  19.6 1.3 %collective-permute-start.5 = (bf16[192,512]{1,0:T(8,128)(2,1)S(1)}, bf16[192,512]{1,0:T(8,128)(2,1)S(1)}, u32[]{:S(2)}, u32[]{:S(2)}) collective-permute-start(bf16[192,512]{1,0:T(8,128)(2,1)S(1)} %collective-permute-done.4.refs_0_), channel_id=1, source_target_pairs={{0,8},{8,0},{16,24},{24,16},{32,40},{40,32},{48,56},{56,48},{64,72... | collective-permute-start | bytes 589832 | tf_op jit(solution)/shard_map/ppermute | solution.py:287
  20.9 0.0 collective-permute-done.6.refs_1_
  20.9 2.2 %collective-permute-start.7 = (bf16[192,512]{1,0:T(8,128)(2,1)S(1)}, bf16[192,512]{1,0:T(8,128)(2,1)S(1)}, u32[]{:S(2)}, u32[]{:S(2)}) collective-permute-start(bf16[192,512]{1,0:T(8,128)(2,1)S(1)} %collective-permute-done.6.refs_1_), channel_id=1, source_target_pairs={{0,8},{8,0},{16,24},{24,16},{32,40},{40,32},{48,56},{56,48},{64,72... | collective-permute-start | bytes 589832 | tf_op jit(solution)/shard_map/ppermute | solution.py:287
  23.1 0.0 collective-permute-done.8.refs_2_
  23.1 0.2 collective-permute-start.9
  23.3 0.7 %record_spectra.1.refs_4_ = f32[12288,128]{1,0:T(8,128)S(1)} custom-call(bf16[192,512]{1,0:T(8,128)(2,1)S(1)} %collective-permute-done.4.refs_0_, bf16[192,512]{1,0:T(8,128)(2,1)S(1)} %collective-permute-done.6.refs_1_, bf16[192,512]{1,0:T(8,128)(2,1)S(1)} %collective-permute-done.8.refs_2_, ...), custom_call_target="tpu_custom_call", output_to_operand_aliasing={{}: (4, {})} | custom-call | flops 452984832 | bytes 2359296 | tf_op jit(solution)/shard_map/record_spectra/pallas_call | solution.py:176
  24.0 0.0 collective-permute-done.3.refs_0_
  24.0 0.0 collective-permute-done.5.refs_1_
  24.0 0.1 collective-permute-done.7.refs_2_
  24.2 0.4 collective-permute-done.9.refs_3_
  24.5 4.7 %detect.1 = (bf16[128,768]{1,0:T(8,128)(2,1)S(1)}, bf16[64,256]{1,0:T(8,128)(2,1)S(1)}, f32[12288,128]{1,0:T(8,128)S(1)}) custom-call(s32[64,48]{1,0:T(8,128)S(1)} %get-tuple-element.20.slots, bf16[192,512]{1,0:T(8,128)(2,1)S(1)} %collective-permute-done.3.refs_0_, ...), custom_call_target="tpu_custom_call", output_to_operand_aliasing={{2}: (5, {})} | custom-call | flops 603979776 | bytes 12582912 | tf_op jit(solution)/shard_map/detect/pallas_call | solution.py:251
  29.3 1.3 %collective-permute-start.10 = (bf16[64,256]{1,0:T(8,128)(2,1)S(1)}, bf16[64,256]{1,0:T(8,128)(2,1)S(1)}, u32[]{:S(2)}, u32[]{:S(2)}) collective-permute-start(bf16[64,256]{1,0:T(8,128)(2,1)S(1)} %get-tuple-element.34), channel_id=1, source_target_pairs={{1,0},{2,1},{3,2},{4,3},{5,4},{6,5},{7,6},{9,8},{10,9},{11,10},{12... | collective-permute-start | bytes 98312 | tf_op jit(solution)/shard_map/ppermute | solution.py:312
  30.6 0.4 own_window.1
  31.0 7.4 %collective-permute-done.10 = bf16[64,256]{1,0:T(8,128)(2,1)S(1)} collective-permute-done((bf16[64,256]{1,0:T(8,128)(2,1)S(1)}, bf16[64,256]{1,0:T(8,128)(2,1)S(1)}, u32[]{:S(2)}, u32[]{:S(2)}) %collective-permute-start.10) | collective-permute-done | bytes 32800 | tf_op jit(solution)/shard_map/ppermute | solution.py:312
  38.4 0.7 %convert_add_fusion = f32[64,512]{1,0:T(8,128)} fusion(f32[64,512]{1,0:T(8,128)S(1)} %own_window.1, bf16[64,256]{1,0:T(8,128)(2,1)S(1)} %collective-permute-done.10), kind=kLoop, calls=%fused_computation | loop fusion | flops 65536 | bytes 294912 | tf_op jit(solution)/shard_map/add | solution.py:314
  (1 shorter events, 0.0 us)
Async XLA Ops:
  0.0 8.1 %collective-permute-start = (bf16[48,512]{1,0:T(8,128)(2,1)}, bf16[48,512]{1,0:T(8,128)(2,1)S(1)}, u32[]{:S(2)}, u32[]{:S(2)}) collective-permute-start(bf16[48,512]{1,0:T(8,128)(2,1)} %refs_1_.1), channel_id=1, source_target_pairs={{0,48},{8,56},{16,32},{24,40},{32,16},{40,24},{48,0},{56,8},{64,11... | collective-permute-start | bytes 147464 | tf_op jit(solution)/shard_map/ppermute | solution.py:287
  5.2 4.7 %collective-permute-start.1 = (bf16[48,512]{1,0:T(8,128)(2,1)}, bf16[48,512]{1,0:T(8,128)(2,1)S(1)}, u32[]{:S(2)}, u32[]{:S(2)}) collective-permute-start(bf16[48,512]{1,0:T(8,128)(2,1)} %refs_1_.1), channel_id=1, source_target_pairs={{0,32},{8,40},{16,48},{24,56},{32,0},{40,8},{48,16},{56,24},{64,96... | collective-permute-start | bytes 147464 | tf_op jit(solution)/shard_map/ppermute | solution.py:287
  5.2 4.7 %collective-permute-start.2 = (bf16[48,512]{1,0:T(8,128)(2,1)}, bf16[48,512]{1,0:T(8,128)(2,1)S(1)}, u32[]{:S(2)}, u32[]{:S(2)}) collective-permute-start(bf16[48,512]{1,0:T(8,128)(2,1)} %refs_1_.1), channel_id=1, source_target_pairs={{0,16},{8,24},{16,0},{24,8},{32,48},{40,56},{48,32},{56,40},{64,80... | collective-permute-start | bytes 147464 | tf_op jit(solution)/shard_map/ppermute | solution.py:287
  9.9 9.7 %collective-permute-start.4 = (bf16[192,512]{1,0:T(8,128)(2,1)S(1)}, bf16[192,512]{1,0:T(8,128)(2,1)S(1)}, u32[]{:S(2)}, u32[]{:S(2)}) collective-permute-start(bf16[192,512]{1,0:T(8,128)(2,1)S(1)} %join.1.line_ref), channel_id=1, source_target_pairs={{0,128},{8,136},{16,144},{24,152},{32,160},{40,168},{48,176},{56,1... | collective-permute-start | bytes 589832 | tf_op jit(solution)/shard_map/ppermute | solution.py:287
  12.7 8.2 %collective-permute-start.6 = (bf16[192,512]{1,0:T(8,128)(2,1)S(1)}, bf16[192,512]{1,0:T(8,128)(2,1)S(1)}, u32[]{:S(2)}, u32[]{:S(2)}) collective-permute-start(bf16[192,512]{1,0:T(8,128)(2,1)S(1)} %join.1.line_ref), channel_id=1, source_target_pairs={{0,64},{8,72},{16,80},{24,88},{32,96},{40,104},{48,112},{56,120},{... | collective-permute-start | bytes 589832 | tf_op jit(solution)/shard_map/ppermute | solution.py:287
  13.0 10.1 %collective-permute-start.8 = (bf16[192,512]{1,0:T(8,128)(2,1)S(1)}, bf16[192,512]{1,0:T(8,128)(2,1)S(1)}, u32[]{:S(2)}, u32[]{:S(2)}) collective-permute-start(bf16[192,512]{1,0:T(8,128)(2,1)S(1)} %join.1.line_ref), channel_id=1, source_target_pairs={{0,192},{8,200},{16,208},{24,216},{32,224},{40,232},{48,240},{56,2... | collective-permute-start | bytes 589832 | tf_op jit(solution)/shard_map/ppermute | solution.py:287
  17.5 6.5 %collective-permute-start.3 = (bf16[192,512]{1,0:T(8,128)(2,1)S(1)}, bf16[192,512]{1,0:T(8,128)(2,1)S(1)}, u32[]{:S(2)}, u32[]{:S(2)}) collective-permute-start(bf16[192,512]{1,0:T(8,128)(2,1)S(1)} %get-tuple-element.28), channel_id=1, source_target_pairs={{0,8},{8,0},{16,24},{24,16},{32,40},{40,32},{48,56},{56,48},{64,72... | collective-permute-start | bytes 589832 | tf_op jit(solution)/shard_map/ppermute | solution.py:287
  19.6 4.4 %collective-permute-start.5 = (bf16[192,512]{1,0:T(8,128)(2,1)S(1)}, bf16[192,512]{1,0:T(8,128)(2,1)S(1)}, u32[]{:S(2)}, u32[]{:S(2)}) collective-permute-start(bf16[192,512]{1,0:T(8,128)(2,1)S(1)} %collective-permute-done.4.refs_0_), channel_id=1, source_target_pairs={{0,8},{8,0},{16,24},{24,16},{32,40},{40,32},{48,56},{56,48},{64,72... | collective-permute-start | bytes 589832 | tf_op jit(solution)/shard_map/ppermute | solution.py:287
  20.9 3.3 %collective-permute-start.7 = (bf16[192,512]{1,0:T(8,128)(2,1)S(1)}, bf16[192,512]{1,0:T(8,128)(2,1)S(1)}, u32[]{:S(2)}, u32[]{:S(2)}) collective-permute-start(bf16[192,512]{1,0:T(8,128)(2,1)S(1)} %collective-permute-done.6.refs_1_), channel_id=1, source_target_pairs={{0,8},{8,0},{16,24},{24,16},{32,40},{40,32},{48,56},{56,48},{64,72... | collective-permute-start | bytes 589832 | tf_op jit(solution)/shard_map/ppermute | solution.py:287
  23.1 1.4 %collective-permute-start.9 = (bf16[192,512]{1,0:T(8,128)(2,1)S(1)}, bf16[192,512]{1,0:T(8,128)(2,1)S(1)}, u32[]{:S(2)}, u32[]{:S(2)}) collective-permute-start(bf16[192,512]{1,0:T(8,128)(2,1)S(1)} %collective-permute-done.8.refs_2_), channel_id=1, source_target_pairs={{0,8},{8,0},{16,24},{24,16},{32,40},{40,32},{48,56},{56,48},{64,72... | collective-permute-start | bytes 589832 | tf_op jit(solution)/shard_map/ppermute | solution.py:287
  29.3 9.1 %collective-permute-start.10 = (bf16[64,256]{1,0:T(8,128)(2,1)S(1)}, bf16[64,256]{1,0:T(8,128)(2,1)S(1)}, u32[]{:S(2)}, u32[]{:S(2)}) collective-permute-start(bf16[64,256]{1,0:T(8,128)(2,1)S(1)} %get-tuple-element.34), channel_id=1, source_target_pairs={{1,0},{2,1},{3,2},{4,3},{5,4},{6,5},{7,6},{9,8},{10,9},{11,10},{12... | collective-permute-start | bytes 98312 | tf_op jit(solution)/shard_map/ppermute | solution.py:312

commit v8 on v7

--- a/solution.py
+++ b/solution.py
@@ -15,7 +15,7 @@
 HOLD = 128
 LAG_ROWS = 64
 SPREAD_ROWS = 64
-Z_ORDER = (3, 2, 1)
+Z_ORDER = (3, 1, 2)
 X_ORDER = (2, 1, 3)
 VMEM_K1 = 12 << 20
 VMEM_K2 = 12 << 20

time: 39.2 us -> 38.2 us (0.974)
  waiting for transfers between devices: 9.66 us -> 8.86 us
    ppermute x1, waiting for transfers between devices: 7.41 us -> 6.91 us  [per_device(): lax.ppermute(early, 'tm', [(i, i - 1) for i in range(1, lax.axis_size('tm...]
  transfers between devices with their start and end apart: 11 -> 11, of which waited for: 4 -> 3; matrix products, arithmetic and copies ran while one was open for 0% -> 0% of each run, Pallas kernels for 19% -> 20%
where the time goes in v8:
time: 38.2 us; the launch traced here: 38.1 us
  starting transfers between devices  16.1 us (42%)
  Pallas kernels  12.4 us (32%)
  waiting for transfers between devices  8.86 us (23%)
  other arithmetic  0.67 us (2%)
    ppermute x10, starting transfers between devices, per_device(): swap = lambda block, change: lax.ppermute(block, 'tmpl', route(change))  14.8 us
    ppermute x1, waiting for transfers between devices, per_device(): lax.ppermute(early, 'tm', [(i, i - 1) for i in range(1, lax.axis_size('tm...  6.91 us
    pallas_call x1, Pallas kernels, detect(): pl.pallas_call(functools.partial(detect_kernel, len(blocks), count, stati...  4.74 us
    pallas_call x1, Pallas kernels, template_spectra(): pl.pallas_call(functools.partial(template_kernel, 8 * lags.shape[1], freq...  3.88 us
    pallas_call x1, Pallas kernels, load(): pl.pallas_call(functools.partial(load_kernel, len(arrays) + 1, per), in_s...  2.66 us
    ppermute x10, waiting for transfers between devices, per_device(): swap = lambda block, change: lax.ppermute(block, 'tmpl', route(change))  1.95 us
    ppermute x1, starting transfers between devices, per_device(): lax.ppermute(early, 'tm', [(i, i - 1) for i in range(1, lax.axis_size('tm...  1.29 us
  transfers between devices with their start and end apart: 11, of which 3 were waited for; matrix products, arithmetic and copies ran while one was open for 0% of the time, Pallas kernels for 20%

profile of v8, /device:TPU:1, one launch (start us, length us, event | category | flops | bytes accessed | tf_op | source)
XLA Modules:
  0.0 38.1 jit_solution(16921895872772775687)
XLA Ops:
  0.0 5.2 %collective-permute-start = (bf16[48,512]{1,0:T(8,128)(2,1)}, bf16[48,512]{1,0:T(8,128)(2,1)S(1)}, u32[]{:S(2)}, u32[]{:S(2)}) collective-permute-start(bf16[48,512]{1,0:T(8,128)(2,1)} %refs_1_.1), channel_id=1, source_target_pairs={{0,48},{8,56},{16,32},{24,40},{32,16},{40,24},{48,0},{56,8},{64,11... | collective-permute-start | bytes 147464 | tf_op jit(solution)/shard_map/ppermute | solution.py:287
  5.2 0.0 collective-permute-start.1
  5.2 0.3 collective-permute-start.2
  5.5 2.7 %load.1 = (bf16[48,512]{1,0:T(8,128)(2,1)S(1)}, bf16[3072,200]{1,0:T(8,128)(2,1)S(1)}, bf16[200,768]{1,0:T(8,128)(2,1)S(1)}, bf16[512,768]{1,0:T(8,128)(2,1)S(1)...) custom-call(s32[64,48]{1,0:T(8,128)} %bitcast.5, ...), custom_call_target="tpu_custom_call" | custom-call | tf_op jit(solution)/shard_map/load/pallas_call | solution.py:79
  8.1 0.0 collective-permute-done.refs_1_
  8.1 1.6 %collective-permute-done.1.refs_2_ = bf16[48,512]{1,0:T(8,128)(2,1)S(1)} collective-permute-done((bf16[48,512]{1,0:T(8,128)(2,1)}, bf16[48,512]{1,0:T(8,128)(2,1)S(1)}, u32[]{:S(2)}, u32[]{:S(2)}) %collective-permute-start.1) | collective-permute-done | bytes 49184 | tf_op jit(solution)/shard_map/ppermute | solution.py:287
  9.7 0.0 collective-permute-done.2.refs_3_
  9.7 2.3 %collective-permute-start.4 = (bf16[192,512]{1,0:T(8,128)(2,1)S(1)}, bf16[192,512]{1,0:T(8,128)(2,1)S(1)}, u32[]{:S(2)}, u32[]{:S(2)}) collective-permute-start(bf16[192,512]{1,0:T(8,128)(2,1)S(1)} %join.1.line_ref), channel_id=1, source_target_pairs={{0,128},{8,136},{16,144},{24,152},{32,160},{40,168},{48,176},{56,1... | collective-permute-start | bytes 589832 | tf_op jit(solution)/shard_map/ppermute | solution.py:287
  12.1 0.3 collective-permute-start.6
  12.4 0.7 %collective-permute-start.8 = (bf16[192,512]{1,0:T(8,128)(2,1)S(1)}, bf16[192,512]{1,0:T(8,128)(2,1)S(1)}, u32[]{:S(2)}, u32[]{:S(2)}) collective-permute-start(bf16[192,512]{1,0:T(8,128)(2,1)S(1)} %join.1.line_ref), channel_id=1, source_target_pairs={{0,192},{8,200},{16,208},{24,216},{32,224},{40,232},{48,240},{56,2... | collective-permute-start | bytes 589832 | tf_op jit(solution)/shard_map/ppermute | solution.py:287
  13.1 3.9 %template_spectra.1 = (f32[24576,128]{1,0:T(8,128)S(1)}, bf16[192,512]{1,0:T(8,128)(2,1)S(1)}, f32[12288,128]{1,0:T(8,128)S(1)}) custom-call(s32[64,48]{1,0:T(8,128)S(1)} %get-tuple-element.21.lag_ref, bf16[80,384]{1,0:T(8,128)(2,1)S(1)} %get-tuple-element.22.spread_ref, bf16[192,512]{1,0:T(8,128)(2,1)S(1)} %join.1.line_ref, ...), custom_call_target="tpu_custom_call" | custom-call | flops 943718400 | bytes 12582912 | tf_op jit(solution)/shard_map/template_spectra/pallas_call | solution.py:122
  17.0 2.9 %collective-permute-start.3 = (bf16[192,512]{1,0:T(8,128)(2,1)S(1)}, bf16[192,512]{1,0:T(8,128)(2,1)S(1)}, u32[]{:S(2)}, u32[]{:S(2)}) collective-permute-start(bf16[192,512]{1,0:T(8,128)(2,1)S(1)} %get-tuple-element.28), channel_id=1, source_target_pairs={{0,8},{8,0},{16,24},{24,16},{32,40},{40,32},{48,56},{56,48},{64,72... | collective-permute-start | bytes 589832 | tf_op jit(solution)/shard_map/ppermute | solution.py:287
  19.9 0.0 collective-permute-done.4.refs_0_
  19.9 1.0 %collective-permute-start.5 = (bf16[192,512]{1,0:T(8,128)(2,1)S(1)}, bf16[192,512]{1,0:T(8,128)(2,1)S(1)}, u32[]{:S(2)}, u32[]{:S(2)}) collective-permute-start(bf16[192,512]{1,0:T(8,128)(2,1)S(1)} %collective-permute-done.4.refs_0_), channel_id=1, source_target_pairs={{0,8},{8,0},{16,24},{24,16},{32,40},{40,32},{48,56},{56,48},{64,72... | collective-permute-start | bytes 589832 | tf_op jit(solution)/shard_map/ppermute | solution.py:287
  20.9 0.0 collective-permute-done.6.refs_1_
  20.9 1.6 %collective-permute-start.7 = (bf16[192,512]{1,0:T(8,128)(2,1)S(1)}, bf16[192,512]{1,0:T(8,128)(2,1)S(1)}, u32[]{:S(2)}, u32[]{:S(2)}) collective-permute-start(bf16[192,512]{1,0:T(8,128)(2,1)S(1)} %collective-permute-done.6.refs_1_), channel_id=1, source_target_pairs={{0,8},{8,0},{16,24},{24,16},{32,40},{40,32},{48,56},{56,48},{64,72... | collective-permute-start | bytes 589832 | tf_op jit(solution)/shard_map/ppermute | solution.py:287
  22.5 0.0 collective-permute-done.8.refs_2_
  22.5 0.6 %collective-permute-start.9 = (bf16[192,512]{1,0:T(8,128)(2,1)S(1)}, bf16[192,512]{1,0:T(8,128)(2,1)S(1)}, u32[]{:S(2)}, u32[]{:S(2)}) collective-permute-start(bf16[192,512]{1,0:T(8,128)(2,1)S(1)} %collective-permute-done.8.refs_2_), channel_id=1, source_target_pairs={{0,8},{8,0},{16,24},{24,16},{32,40},{40,32},{48,56},{56,48},{64,72... | collective-permute-start | bytes 589832 | tf_op jit(solution)/shard_map/ppermute | solution.py:287
  23.0 0.7 %record_spectra.1.refs_4_ = f32[12288,128]{1,0:T(8,128)S(1)} custom-call(bf16[192,512]{1,0:T(8,128)(2,1)S(1)} %collective-permute-done.4.refs_0_, bf16[192,512]{1,0:T(8,128)(2,1)S(1)} %collective-permute-done.6.refs_1_, bf16[192,512]{1,0:T(8,128)(2,1)S(1)} %collective-permute-done.8.refs_2_, ...), custom_call_target="tpu_custom_call", output_to_operand_aliasing={{}: (4, {})} | custom-call | flops 452984832 | bytes 2359296 | tf_op jit(solution)/shard_map/record_spectra/pallas_call | solution.py:176
  23.7 0.0 collective-permute-done.3.refs_0_
  23.7 0.0 collective-permute-done.5.refs_1_
  23.7 0.0 collective-permute-done.7.refs_2_
  23.7 0.3 collective-permute-done.9.refs_3_
  24.1 4.7 %detect.1 = (bf16[128,768]{1,0:T(8,128)(2,1)S(1)}, bf16[64,256]{1,0:T(8,128)(2,1)S(1)}, f32[12288,128]{1,0:T(8,128)S(1)}) custom-call(s32[64,48]{1,0:T(8,128)S(1)} %get-tuple-element.20.slots, bf16[192,512]{1,0:T(8,128)(2,1)S(1)} %collective-permute-done.3.refs_0_, ...), custom_call_target="tpu_custom_call", output_to_operand_aliasing={{2}: (5, {})} | custom-call | flops 603979776 | bytes 12582912 | tf_op jit(solution)/shard_map/detect/pallas_call | solution.py:251
  28.8 1.3 %collective-permute-start.10 = (bf16[64,256]{1,0:T(8,128)(2,1)S(1)}, bf16[64,256]{1,0:T(8,128)(2,1)S(1)}, u32[]{:S(2)}, u32[]{:S(2)}) collective-permute-start(bf16[64,256]{1,0:T(8,128)(2,1)S(1)} %get-tuple-element.34), channel_id=1, source_target_pairs={{1,0},{2,1},{3,2},{4,3},{5,4},{6,5},{7,6},{9,8},{10,9},{11,10},{12... | collective-permute-start | bytes 98312 | tf_op jit(solution)/shard_map/ppermute | solution.py:312
  30.1 0.4 %own_window.1 = f32[64,512]{1,0:T(8,128)S(1)} custom-call(bf16[128,768]{1,0:T(8,128)(2,1)S(1)} %get-tuple-element.33.parts_ref, bf16[768,768]{1,0:T(8,128)(2,1)S(1)} %get-tuple-element.31.refs_7_.high_ref, bf16[768,768]{1,0:T(8,128)(2,1)S(1)} %get-tuple-element.32.refs_8_.low_ref), custom_call_target="tpu_custom_call" | custom-call | flops 150994944 | bytes 4194304 | tf_op jit(solution)/shard_map/own_window/pallas_call | solution.py:202
  30.5 6.9 %collective-permute-done.10 = bf16[64,256]{1,0:T(8,128)(2,1)S(1)} collective-permute-done((bf16[64,256]{1,0:T(8,128)(2,1)S(1)}, bf16[64,256]{1,0:T(8,128)(2,1)S(1)}, u32[]{:S(2)}, u32[]{:S(2)}) %collective-permute-start.10) | collective-permute-done | bytes 32800 | tf_op jit(solution)/shard_map/ppermute | solution.py:312
  37.4 0.7 %convert_add_fusion = f32[64,512]{1,0:T(8,128)} fusion(f32[64,512]{1,0:T(8,128)S(1)} %own_window.1, bf16[64,256]{1,0:T(8,128)(2,1)S(1)} %collective-permute-done.10), kind=kLoop, calls=%fused_computation | loop fusion | flops 65536 | bytes 294912 | tf_op jit(solution)/shard_map/add | solution.py:314
  (1 shorter events, 0.0 us)
Async XLA Ops:
  0.0 8.1 %collective-permute-start = (bf16[48,512]{1,0:T(8,128)(2,1)}, bf16[48,512]{1,0:T(8,128)(2,1)S(1)}, u32[]{:S(2)}, u32[]{:S(2)}) collective-permute-start(bf16[48,512]{1,0:T(8,128)(2,1)} %refs_1_.1), channel_id=1, source_target_pairs={{0,48},{8,56},{16,32},{24,40},{32,16},{40,24},{48,0},{56,8},{64,11... | collective-permute-start | bytes 147464 | tf_op jit(solution)/shard_map/ppermute | solution.py:287
  5.2 4.5 %collective-permute-start.1 = (bf16[48,512]{1,0:T(8,128)(2,1)}, bf16[48,512]{1,0:T(8,128)(2,1)S(1)}, u32[]{:S(2)}, u32[]{:S(2)}) collective-permute-start(bf16[48,512]{1,0:T(8,128)(2,1)} %refs_1_.1), channel_id=1, source_target_pairs={{0,16},{8,24},{16,0},{24,8},{32,48},{40,56},{48,32},{56,40},{64,80... | collective-permute-start | bytes 147464 | tf_op jit(solution)/shard_map/ppermute | solution.py:287
  5.2 4.5 %collective-permute-start.2 = (bf16[48,512]{1,0:T(8,128)(2,1)}, bf16[48,512]{1,0:T(8,128)(2,1)S(1)}, u32[]{:S(2)}, u32[]{:S(2)}) collective-permute-start(bf16[48,512]{1,0:T(8,128)(2,1)} %refs_1_.1), channel_id=1, source_target_pairs={{0,32},{8,40},{16,48},{24,56},{32,0},{40,8},{48,16},{56,24},{64,96... | collective-permute-start | bytes 147464 | tf_op jit(solution)/shard_map/ppermute | solution.py:287
  9.7 10.1 %collective-permute-start.4 = (bf16[192,512]{1,0:T(8,128)(2,1)S(1)}, bf16[192,512]{1,0:T(8,128)(2,1)S(1)}, u32[]{:S(2)}, u32[]{:S(2)}) collective-permute-start(bf16[192,512]{1,0:T(8,128)(2,1)S(1)} %join.1.line_ref), channel_id=1, source_target_pairs={{0,128},{8,136},{16,144},{24,152},{32,160},{40,168},{48,176},{56,1... | collective-permute-start | bytes 589832 | tf_op jit(solution)/shard_map/ppermute | solution.py:287
  12.1 8.8 %collective-permute-start.6 = (bf16[192,512]{1,0:T(8,128)(2,1)S(1)}, bf16[192,512]{1,0:T(8,128)(2,1)S(1)}, u32[]{:S(2)}, u32[]{:S(2)}) collective-permute-start(bf16[192,512]{1,0:T(8,128)(2,1)S(1)} %join.1.line_ref), channel_id=1, source_target_pairs={{0,64},{8,72},{16,80},{24,88},{32,96},{40,104},{48,112},{56,120},{... | collective-permute-start | bytes 589832 | tf_op jit(solution)/shard_map/ppermute | solution.py:287
  12.4 10.1 %collective-permute-start.8 = (bf16[192,512]{1,0:T(8,128)(2,1)S(1)}, bf16[192,512]{1,0:T(8,128)(2,1)S(1)}, u32[]{:S(2)}, u32[]{:S(2)}) collective-permute-start(bf16[192,512]{1,0:T(8,128)(2,1)S(1)} %join.1.line_ref), channel_id=1, source_target_pairs={{0,192},{8,200},{16,208},{24,216},{32,224},{40,232},{48,240},{56,2... | collective-permute-start | bytes 589832 | tf_op jit(solution)/shard_map/ppermute | solution.py:287
  17.0 6.7 %collective-permute-start.3 = (bf16[192,512]{1,0:T(8,128)(2,1)S(1)}, bf16[192,512]{1,0:T(8,128)(2,1)S(1)}, u32[]{:S(2)}, u32[]{:S(2)}) collective-permute-start(bf16[192,512]{1,0:T(8,128)(2,1)S(1)} %get-tuple-element.28), channel_id=1, source_target_pairs={{0,8},{8,0},{16,24},{24,16},{32,40},{40,32},{48,56},{56,48},{64,72... | collective-permute-start | bytes 589832 | tf_op jit(solution)/shard_map/ppermute | solution.py:287
  19.9 3.8 %collective-permute-start.5 = (bf16[192,512]{1,0:T(8,128)(2,1)S(1)}, bf16[192,512]{1,0:T(8,128)(2,1)S(1)}, u32[]{:S(2)}, u32[]{:S(2)}) collective-permute-start(bf16[192,512]{1,0:T(8,128)(2,1)S(1)} %collective-permute-done.4.refs_0_), channel_id=1, source_target_pairs={{0,8},{8,0},{16,24},{24,16},{32,40},{40,32},{48,56},{56,48},{64,72... | collective-permute-start | bytes 589832 | tf_op jit(solution)/shard_map/ppermute | solution.py:287
  20.9 2.9 %collective-permute-start.7 = (bf16[192,512]{1,0:T(8,128)(2,1)S(1)}, bf16[192,512]{1,0:T(8,128)(2,1)S(1)}, u32[]{:S(2)}, u32[]{:S(2)}) collective-permute-start(bf16[192,512]{1,0:T(8,128)(2,1)S(1)} %collective-permute-done.6.refs_1_), channel_id=1, source_target_pairs={{0,8},{8,0},{16,24},{24,16},{32,40},{40,32},{48,56},{56,48},{64,72... | collective-permute-start | bytes 589832 | tf_op jit(solution)/shard_map/ppermute | solution.py:287
  22.5 1.6 %collective-permute-start.9 = (bf16[192,512]{1,0:T(8,128)(2,1)S(1)}, bf16[192,512]{1,0:T(8,128)(2,1)S(1)}, u32[]{:S(2)}, u32[]{:S(2)}) collective-permute-start(bf16[192,512]{1,0:T(8,128)(2,1)S(1)} %collective-permute-done.8.refs_2_), channel_id=1, source_target_pairs={{0,8},{8,0},{16,24},{24,16},{32,40},{40,32},{48,56},{56,48},{64,72... | collective-permute-start | bytes 589832 | tf_op jit(solution)/shard_map/ppermute | solution.py:287
  28.8 8.6 %collective-permute-start.10 = (bf16[64,256]{1,0:T(8,128)(2,1)S(1)}, bf16[64,256]{1,0:T(8,128)(2,1)S(1)}, u32[]{:S(2)}, u32[]{:S(2)}) collective-permute-start(bf16[64,256]{1,0:T(8,128)(2,1)S(1)} %get-tuple-element.34), channel_id=1, source_target_pairs={{1,0},{2,1},{3,2},{4,3},{5,4},{6,5},{7,6},{9,8},{10,9},{11,10},{12... | collective-permute-start | bytes 98312 | tf_op jit(solution)/shard_map/ppermute | solution.py:312

commit v9 on v8

--- a/solution.py
+++ b/solution.py
@@ -166,8 +166,9 @@
 
 
 def record_kernel(freqs, first, *refs):
-    *blocks, forward_ref, _, table = refs
+    *blocks, far_line, forward_ref, _, table = refs
     fill_table(blocks, forward_ref, table, first, freqs)
+    fill_table([far_line], forward_ref, table, table.shape[0] // 16, freqs)
 
 
 def record_spectra(blocks, forward, table, first, freqs):
@@ -215,7 +216,7 @@
     load = pltpu.make_async_copy(slots, slot_ref, sem)
     load.start()
     chunks = freqs // HOLD
-    fill_table(blocks, forward_ref, table, table.shape[0] // 16, freqs)
+    fill_table(blocks, forward_ref, table, table.shape[0] // 8 - n_blocks * blocks[0].shape[0], freqs)
     load.wait()
 
     def one(t, carry):
@@ -231,7 +232,7 @@
         acc[pl.ds(pl.multiple_of(t * 16 + 8, 8), 8), :] = second[0] + second[1]
         return carry
 
-    lax.fori_loop(0, count, one, 0, unroll=2)
+    lax.fori_loop(0, count, one, 0, unroll=4)
     joint = jnp.concatenate(
         [acc[pl.ds(j, count, stride=16), :] + acc[pl.ds(4 + j, count, stride=16), :] for j in range(chunks)]
         + [acc[pl.ds(8 + j, count, stride=16), :] - acc[pl.ds(12 + j, count, stride=16), :] for j in range(chunks)],
@@ -306,8 +307,8 @@
     plane = [swap(line, (d, 0, 0)) for d in X_ORDER]
     q, line_q, table = template_spectra(lags, spread, line, waves, head, forward, phase, 32 * per, freqs)
     far = [swap(block, (0, 0, 1)) for block in [line_q] + plane]
-    table = record_spectra(plane, forward, table, line.shape[0], freqs)
-    parts, early = detect(slots, far, table, q, forward, high, low, batches * count, stations, freqs, time_dev)
+    table = record_spectra(plane + far[:1], forward, table, line.shape[0], freqs)
+    parts, early = detect(slots, far[1:], table, q, forward, high, low, batches * count, stations, freqs, time_dev)
     main = own_window(parts, high, low, time_dev)
     earlier = lax.ppermute(early, "tm", [(i, i - 1) for i in range(1, lax.axis_size("tm"))])
     earlier = earlier.astype(jnp.float32)

time: 38.2 us -> 37.7 us (0.987)
  Pallas kernels: 12.4 us -> 12 us
    pallas_call x1, Pallas kernels: 4.74 us -> 4.22 us  [detect(): pl.pallas_call(functools.partial(detect_kernel, len(blocks), count, stati...]
  transfers between devices with their start and end apart: 11 -> 11, of which waited for: 3 -> 3; matrix products, arithmetic and copies ran while one was open for 0% -> 0% of each run, Pallas kernels for 20% -> 21%
where the time goes in v9:
time: 37.7 us; the launch traced here: 37.6 us
  starting transfers between devices  16.2 us (43%)
  Pallas kernels  12 us (32%)
  waiting for transfers between devices  8.69 us (23%)
  other arithmetic  0.67 us (2%)
    ppermute x10, starting transfers between devices, per_device(): swap = lambda block, change: lax.ppermute(block, 'tmpl', route(change))  14.9 us
    ppermute x1, waiting for transfers between devices, per_device(): lax.ppermute(early, 'tm', [(i, i - 1) for i in range(1, lax.axis_size('tm...  6.91 us
    pallas_call x1, Pallas kernels, detect(): pl.pallas_call(functools.partial(detect_kernel, len(blocks), count, stati...  4.22 us
    pallas_call x1, Pallas kernels, template_spectra(): pl.pallas_call(functools.partial(template_kernel, 8 * lags.shape[1], freq...  3.87 us
    pallas_call x1, Pallas kernels, load(): pl.pallas_call(functools.partial(load_kernel, len(arrays) + 1, per), in_s...  2.66 us
    ppermute x10, waiting for transfers between devices, per_device(): swap = lambda block, change: lax.ppermute(block, 'tmpl', route(change))  1.78 us
    ppermute x1, starting transfers between devices, per_device(): lax.ppermute(early, 'tm', [(i, i - 1) for i in range(1, lax.axis_size('tm...  1.29 us
    pallas_call x1, Pallas kernels, record_spectra(): pl.pallas_call(functools.partial(record_kernel, freqs, first), in_specs=[...  0.86 us
  transfers between devices with their start and end apart: 11, of which 3 were waited for; matrix products, arithmetic and copies ran while one was open for 0% of the time, Pallas kernels for 21%

profile of v9, /device:TPU:1, one launch (start us, length us, event | category | flops | bytes accessed | tf_op | source)
XLA Modules:
  0.0 37.6 jit_solution(10468337349923674053)
XLA Ops:
  0.0 5.2 %collective-permute-start = (bf16[48,512]{1,0:T(8,128)(2,1)}, bf16[48,512]{1,0:T(8,128)(2,1)S(1)}, u32[]{:S(2)}, u32[]{:S(2)}) collective-permute-start(bf16[48,512]{1,0:T(8,128)(2,1)} %refs_1_.1), channel_id=1, source_target_pairs={{0,48},{8,56},{16,32},{24,40},{32,16},{40,24},{48,0},{56,8},{64,11... | collective-permute-start | bytes 147464 | tf_op jit(solution)/shard_map/ppermute | solution.py:288
  5.2 0.0 collective-permute-start.1
  5.2 0.3 collective-permute-start.2
  5.5 2.7 %load.1 = (bf16[48,512]{1,0:T(8,128)(2,1)S(1)}, bf16[3072,200]{1,0:T(8,128)(2,1)S(1)}, bf16[200,768]{1,0:T(8,128)(2,1)S(1)}, bf16[512,768]{1,0:T(8,128)(2,1)S(1)...) custom-call(s32[64,48]{1,0:T(8,128)} %bitcast.5, ...), custom_call_target="tpu_custom_call" | custom-call | tf_op jit(solution)/shard_map/load/pallas_call | solution.py:79
  8.1 0.0 collective-permute-done.refs_1_
  8.1 1.6 %collective-permute-done.1.refs_2_ = bf16[48,512]{1,0:T(8,128)(2,1)S(1)} collective-permute-done((bf16[48,512]{1,0:T(8,128)(2,1)}, bf16[48,512]{1,0:T(8,128)(2,1)S(1)}, u32[]{:S(2)}, u32[]{:S(2)}) %collective-permute-start.1) | collective-permute-done | bytes 49184 | tf_op jit(solution)/shard_map/ppermute | solution.py:288
  9.7 0.0 collective-permute-done.2.refs_3_
  9.7 2.3 %collective-permute-start.3 = (bf16[192,512]{1,0:T(8,128)(2,1)S(1)}, bf16[192,512]{1,0:T(8,128)(2,1)S(1)}, u32[]{:S(2)}, u32[]{:S(2)}) collective-permute-start(bf16[192,512]{1,0:T(8,128)(2,1)S(1)} %join.1.line_ref), channel_id=1, source_target_pairs={{0,128},{8,136},{16,144},{24,152},{32,160},{40,168},{48,176},{56,1... | collective-permute-start | bytes 589832 | tf_op jit(solution)/shard_map/ppermute | solution.py:288
  12.1 0.3 collective-permute-start.5
  12.4 0.7 %collective-permute-start.7 = (bf16[192,512]{1,0:T(8,128)(2,1)S(1)}, bf16[192,512]{1,0:T(8,128)(2,1)S(1)}, u32[]{:S(2)}, u32[]{:S(2)}) collective-permute-start(bf16[192,512]{1,0:T(8,128)(2,1)S(1)} %join.1.line_ref), channel_id=1, source_target_pairs={{0,192},{8,200},{16,208},{24,216},{32,224},{40,232},{48,240},{56,2... | collective-permute-start | bytes 589832 | tf_op jit(solution)/shard_map/ppermute | solution.py:288
  13.1 3.9 %template_spectra.1 = (f32[24576,128]{1,0:T(8,128)S(1)}, bf16[192,512]{1,0:T(8,128)(2,1)S(1)}, f32[12288,128]{1,0:T(8,128)S(1)}) custom-call(s32[64,48]{1,0:T(8,128)S(1)} %get-tuple-element.22.lag_ref, bf16[80,384]{1,0:T(8,128)(2,1)S(1)} %get-tuple-element.23.spread_ref, bf16[192,512]{1,0:T(8,128)(2,1)S(1)} %join.1.line_ref, ...), custom_call_target="tpu_custom_call" | custom-call | flops 943718400 | bytes 12582912 | tf_op jit(solution)/shard_map/template_spectra/pallas_call | solution.py:122
  17.0 2.9 %collective-permute-start.9 = (bf16[192,512]{1,0:T(8,128)(2,1)S(1)}, bf16[192,512]{1,0:T(8,128)(2,1)S(1)}, u32[]{:S(2)}, u32[]{:S(2)}) collective-permute-start(bf16[192,512]{1,0:T(8,128)(2,1)S(1)} %get-tuple-element.28), channel_id=1, source_target_pairs={{0,8},{8,0},{16,24},{24,16},{32,40},{40,32},{48,56},{56,48},{64,72... | collective-permute-start | bytes 589832 | tf_op jit(solution)/shard_map/ppermute | solution.py:288
  19.9 0.0 collective-permute-done.3.refs_0_
  19.9 1.0 %collective-permute-start.4 = (bf16[192,512]{1,0:T(8,128)(2,1)S(1)}, bf16[192,512]{1,0:T(8,128)(2,1)S(1)}, u32[]{:S(2)}, u32[]{:S(2)}) collective-permute-start(bf16[192,512]{1,0:T(8,128)(2,1)S(1)} %collective-permute-done.3.refs_0_), channel_id=1, source_target_pairs={{0,8},{8,0},{16,24},{24,16},{32,40},{40,32},{48,56},{56,48},{64,72... | collective-permute-start | bytes 589832 | tf_op jit(solution)/shard_map/ppermute | solution.py:288
  20.9 0.0 collective-permute-done.5.refs_1_
  20.9 1.6 %collective-permute-start.6 = (bf16[192,512]{1,0:T(8,128)(2,1)S(1)}, bf16[192,512]{1,0:T(8,128)(2,1)S(1)}, u32[]{:S(2)}, u32[]{:S(2)}) collective-permute-start(bf16[192,512]{1,0:T(8,128)(2,1)S(1)} %collective-permute-done.5.refs_1_), channel_id=1, source_target_pairs={{0,8},{8,0},{16,24},{24,16},{32,40},{40,32},{48,56},{56,48},{64,72... | collective-permute-start | bytes 589832 | tf_op jit(solution)/shard_map/ppermute | solution.py:288
  22.5 0.0 collective-permute-done.7.refs_2_
  22.5 0.6 %collective-permute-start.8 = (bf16[192,512]{1,0:T(8,128)(2,1)S(1)}, bf16[192,512]{1,0:T(8,128)(2,1)S(1)}, u32[]{:S(2)}, u32[]{:S(2)}) collective-permute-start(bf16[192,512]{1,0:T(8,128)(2,1)S(1)} %collective-permute-done.7.refs_2_), channel_id=1, source_target_pairs={{0,8},{8,0},{16,24},{24,16},{32,40},{40,32},{48,56},{56,48},{64,72... | collective-permute-start | bytes 589832 | tf_op jit(solution)/shard_map/ppermute | solution.py:288
  23.0 0.0 collective-permute-done.9.refs_3_
  23.0 0.9 %record_spectra.1.refs_3_ = f32[12288,128]{1,0:T(8,128)S(1)} custom-call(bf16[192,512]{1,0:T(8,128)(2,1)S(1)} %collective-permute-done.3.refs_0_, bf16[192,512]{1,0:T(8,128)(2,1)S(1)} %collective-permute-done.5.refs_1_, bf16[192,512]{1,0:T(8,128)(2,1)S(1)} %collective-permute-done.7.refs_2_, ...), custom_call_target="tpu_custom_call", output_to_operand_aliasing={{}: (5, {})} | custom-call | flops 603979776 | bytes 3145728 | tf_op jit(solution)/shard_map/record_spectra/pallas_call | solution.py:177
  23.9 0.0 collective-permute-done.4.refs_0_
  23.9 0.0 collective-permute-done.6.refs_1_
  23.9 0.2 collective-permute-done.8.refs_2_
  24.1 4.2 %detect.1 = (bf16[128,768]{1,0:T(8,128)(2,1)S(1)}, bf16[64,256]{1,0:T(8,128)(2,1)S(1)}, f32[12288,128]{1,0:T(8,128)S(1)}) custom-call(s32[64,48]{1,0:T(8,128)S(1)} %get-tuple-element.20.slots, bf16[192,512]{1,0:T(8,128)(2,1)S(1)} %collective-permute-done.4.refs_0_, ...), custom_call_target="tpu_custom_call", output_to_operand_aliasing={{2}: (4, {})} | custom-call | flops 452984832 | bytes 12582912 | tf_op jit(solution)/shard_map/detect/pallas_call | solution.py:252
  28.3 1.3 %collective-permute-start.10 = (bf16[64,256]{1,0:T(8,128)(2,1)S(1)}, bf16[64,256]{1,0:T(8,128)(2,1)S(1)}, u32[]{:S(2)}, u32[]{:S(2)}) collective-permute-start(bf16[64,256]{1,0:T(8,128)(2,1)S(1)} %get-tuple-element.34), channel_id=1, source_target_pairs={{1,0},{2,1},{3,2},{4,3},{5,4},{6,5},{7,6},{9,8},{10,9},{11,10},{12... | collective-permute-start | bytes 98312 | tf_op jit(solution)/shard_map/ppermute | solution.py:313
  29.6 0.4 %own_window.1 = f32[64,512]{1,0:T(8,128)S(1)} custom-call(bf16[128,768]{1,0:T(8,128)(2,1)S(1)} %get-tuple-element.33.parts_ref, bf16[768,768]{1,0:T(8,128)(2,1)S(1)} %get-tuple-element.31.refs_6_.high_ref, bf16[768,768]{1,0:T(8,128)(2,1)S(1)} %get-tuple-element.32.refs_7_.low_ref), custom_call_target="tpu_custom_call" | custom-call | flops 150994944 | bytes 4194304 | tf_op jit(solution)/shard_map/own_window/pallas_call | solution.py:203
  30.0 6.9 %collective-permute-done.10 = bf16[64,256]{1,0:T(8,128)(2,1)S(1)} collective-permute-done((bf16[64,256]{1,0:T(8,128)(2,1)S(1)}, bf16[64,256]{1,0:T(8,128)(2,1)S(1)}, u32[]{:S(2)}, u32[]{:S(2)}) %collective-permute-start.10) | collective-permute-done | bytes 32800 | tf_op jit(solution)/shard_map/ppermute | solution.py:313
  36.9 0.7 %convert_add_fusion = f32[64,512]{1,0:T(8,128)} fusion(f32[64,512]{1,0:T(8,128)S(1)} %own_window.1, bf16[64,256]{1,0:T(8,128)(2,1)S(1)} %collective-permute-done.10), kind=kLoop, calls=%fused_computation | loop fusion | flops 65536 | bytes 294912 | tf_op jit(solution)/shard_map/add | solution.py:315
  (1 shorter events, 0.0 us)
Async XLA Ops:
  0.0 8.1 %collective-permute-start = (bf16[48,512]{1,0:T(8,128)(2,1)}, bf16[48,512]{1,0:T(8,128)(2,1)S(1)}, u32[]{:S(2)}, u32[]{:S(2)}) collective-permute-start(bf16[48,512]{1,0:T(8,128)(2,1)} %refs_1_.1), channel_id=1, source_target_pairs={{0,48},{8,56},{16,32},{24,40},{32,16},{40,24},{48,0},{56,8},{64,11... | collective-permute-start | bytes 147464 | tf_op jit(solution)/shard_map/ppermute | solution.py:288
  5.2 4.5 %collective-permute-start.1 = (bf16[48,512]{1,0:T(8,128)(2,1)}, bf16[48,512]{1,0:T(8,128)(2,1)S(1)}, u32[]{:S(2)}, u32[]{:S(2)}) collective-permute-start(bf16[48,512]{1,0:T(8,128)(2,1)} %refs_1_.1), channel_id=1, source_target_pairs={{0,16},{8,24},{16,0},{24,8},{32,48},{40,56},{48,32},{56,40},{64,80... | collective-permute-start | bytes 147464 | tf_op jit(solution)/shard_map/ppermute | solution.py:288
  5.2 4.5 %collective-permute-start.2 = (bf16[48,512]{1,0:T(8,128)(2,1)}, bf16[48,512]{1,0:T(8,128)(2,1)S(1)}, u32[]{:S(2)}, u32[]{:S(2)}) collective-permute-start(bf16[48,512]{1,0:T(8,128)(2,1)} %refs_1_.1), channel_id=1, source_target_pairs={{0,32},{8,40},{16,48},{24,56},{32,0},{40,8},{48,16},{56,24},{64,96... | collective-permute-start | bytes 147464 | tf_op jit(solution)/shard_map/ppermute | solution.py:288
  9.7 10.1 %collective-permute-start.3 = (bf16[192,512]{1,0:T(8,128)(2,1)S(1)}, bf16[192,512]{1,0:T(8,128)(2,1)S(1)}, u32[]{:S(2)}, u32[]{:S(2)}) collective-permute-start(bf16[192,512]{1,0:T(8,128)(2,1)S(1)} %join.1.line_ref), channel_id=1, source_target_pairs={{0,128},{8,136},{16,144},{24,152},{32,160},{40,168},{48,176},{56,1... | collective-permute-start | bytes 589832 | tf_op jit(solution)/shard_map/ppermute | solution.py:288
  12.1 8.8 %collective-permute-start.5 = (bf16[192,512]{1,0:T(8,128)(2,1)S(1)}, bf16[192,512]{1,0:T(8,128)(2,1)S(1)}, u32[]{:S(2)}, u32[]{:S(2)}) collective-permute-start(bf16[192,512]{1,0:T(8,128)(2,1)S(1)} %join.1.line_ref), channel_id=1, source_target_pairs={{0,64},{8,72},{16,80},{24,88},{32,96},{40,104},{48,112},{56,120},{... | collective-permute-start | bytes 589832 | tf_op jit(solution)/shard_map/ppermute | solution.py:288
  12.4 10.1 %collective-permute-start.7 = (bf16[192,512]{1,0:T(8,128)(2,1)S(1)}, bf16[192,512]{1,0:T(8,128)(2,1)S(1)}, u32[]{:S(2)}, u32[]{:S(2)}) collective-permute-start(bf16[192,512]{1,0:T(8,128)(2,1)S(1)} %join.1.line_ref), channel_id=1, source_target_pairs={{0,192},{8,200},{16,208},{24,216},{32,224},{40,232},{48,240},{56,2... | collective-permute-start | bytes 589832 | tf_op jit(solution)/shard_map/ppermute | solution.py:288
  17.0 6.1 %collective-permute-start.9 = (bf16[192,512]{1,0:T(8,128)(2,1)S(1)}, bf16[192,512]{1,0:T(8,128)(2,1)S(1)}, u32[]{:S(2)}, u32[]{:S(2)}) collective-permute-start(bf16[192,512]{1,0:T(8,128)(2,1)S(1)} %get-tuple-element.28), channel_id=1, source_target_pairs={{0,8},{8,0},{16,24},{24,16},{32,40},{40,32},{48,56},{56,48},{64,72... | collective-permute-start | bytes 589832 | tf_op jit(solution)/shard_map/ppermute | solution.py:288
  19.9 4.0 %collective-permute-start.4 = (bf16[192,512]{1,0:T(8,128)(2,1)S(1)}, bf16[192,512]{1,0:T(8,128)(2,1)S(1)}, u32[]{:S(2)}, u32[]{:S(2)}) collective-permute-start(bf16[192,512]{1,0:T(8,128)(2,1)S(1)} %collective-permute-done.3.refs_0_), channel_id=1, source_target_pairs={{0,8},{8,0},{16,24},{24,16},{32,40},{40,32},{48,56},{56,48},{64,72... | collective-permute-start | bytes 589832 | tf_op jit(solution)/shard_map/ppermute | solution.py:288
  20.9 3.0 %collective-permute-start.6 = (bf16[192,512]{1,0:T(8,128)(2,1)S(1)}, bf16[192,512]{1,0:T(8,128)(2,1)S(1)}, u32[]{:S(2)}, u32[]{:S(2)}) collective-permute-start(bf16[192,512]{1,0:T(8,128)(2,1)S(1)} %collective-permute-done.5.refs_1_), channel_id=1, source_target_pairs={{0,8},{8,0},{16,24},{24,16},{32,40},{40,32},{48,56},{56,48},{64,72... | collective-permute-start | bytes 589832 | tf_op jit(solution)/shard_map/ppermute | solution.py:288
  22.5 1.6 %collective-permute-start.8 = (bf16[192,512]{1,0:T(8,128)(2,1)S(1)}, bf16[192,512]{1,0:T(8,128)(2,1)S(1)}, u32[]{:S(2)}, u32[]{:S(2)}) collective-permute-start(bf16[192,512]{1,0:T(8,128)(2,1)S(1)} %collective-permute-done.7.refs_2_), channel_id=1, source_target_pairs={{0,8},{8,0},{16,24},{24,16},{32,40},{40,32},{48,56},{56,48},{64,72... | collective-permute-start | bytes 589832 | tf_op jit(solution)/shard_map/ppermute | solution.py:288
  28.3 8.6 %collective-permute-start.10 = (bf16[64,256]{1,0:T(8,128)(2,1)S(1)}, bf16[64,256]{1,0:T(8,128)(2,1)S(1)}, u32[]{:S(2)}, u32[]{:S(2)}) collective-permute-start(bf16[64,256]{1,0:T(8,128)(2,1)S(1)} %get-tuple-element.34), channel_id=1, source_target_pairs={{1,0},{2,1},{3,2},{4,3},{5,4},{6,5},{7,6},{9,8},{10,9},{11,10},{12... | collective-permute-start | bytes 98312 | tf_op jit(solution)/shard_map/ppermute | solution.py:313

commit v10 on v9

--- a/solution.py
+++ b/solution.py
@@ -166,9 +166,9 @@
 
 
 def record_kernel(freqs, first, *refs):
-    *blocks, far_line, forward_ref, _, table = refs
+    *blocks, far_line, far_next, forward_ref, _, table = refs
     fill_table(blocks, forward_ref, table, first, freqs)
-    fill_table([far_line], forward_ref, table, table.shape[0] // 16, freqs)
+    fill_table([far_line, far_next], forward_ref, table, table.shape[0] // 16, freqs)
 
 
 def record_spectra(blocks, forward, table, first, freqs):
@@ -307,8 +307,8 @@
     plane = [swap(line, (d, 0, 0)) for d in X_ORDER]
     q, line_q, table = template_spectra(lags, spread, line, waves, head, forward, phase, 32 * per, freqs)
     far = [swap(block, (0, 0, 1)) for block in [line_q] + plane]
-    table = record_spectra(plane + far[:1], forward, table, line.shape[0], freqs)
-    parts, early = detect(slots, far[1:], table, q, forward, high, low, batches * count, stations, freqs, time_dev)
+    table = record_spectra(plane + far[:2], forward, table, line.shape[0], freqs)
+    parts, early = detect(slots, far[2:], table, q, forward, high, low, batches * count, stations, freqs, time_dev)
     main = own_window(parts, high, low, time_dev)
     earlier = lax.ppermute(early, "tm", [(i, i - 1) for i in range(1, lax.axis_size("tm"))])
     earlier = earlier.astype(jnp.float32)

time: 37.7 us -> 37.7 us (level)
  transfers between devices with their start and end apart: 11 -> 11, of which waited for: 3 -> 2; matrix products, arithmetic and copies ran while one was open for 0% -> 0% of each run, Pallas kernels for 21% -> 21%
where the time goes in v10:
time: 37.7 us; the launch traced here: 37.6 us
  starting transfers between devices  16.2 us (43%)
  Pallas kernels  12.2 us (32%)
  waiting for transfers between devices  8.54 us (23%)
  other arithmetic  0.67 us (2%)
    ppermute x10, starting transfers between devices, per_device(): swap = lambda block, change: lax.ppermute(block, 'tmpl', route(change))  14.9 us
    ppermute x1, waiting for transfers between devices, per_device(): lax.ppermute(early, 'tm', [(i, i - 1) for i in range(1, lax.axis_size('tm...  6.91 us
    pallas_call x1, Pallas kernels, detect(): pl.pallas_call(functools.partial(detect_kernel, len(blocks), count, stati...  4.22 us
    pallas_call x1, Pallas kernels, template_spectra(): pl.pallas_call(functools.partial(template_kernel, 8 * lags.shape[1], freq...  3.87 us
    pallas_call x1, Pallas kernels, load(): pl.pallas_call(functools.partial(load_kernel, len(arrays) + 1, per), in_s...  2.66 us
    ppermute x10, waiting for transfers between devices, per_device(): swap = lambda block, change: lax.ppermute(block, 'tmpl', route(change))  1.63 us
    ppermute x1, starting transfers between devices, per_device(): lax.ppermute(early, 'tm', [(i, i - 1) for i in range(1, lax.axis_size('tm...  1.29 us
    pallas_call x1, Pallas kernels, record_spectra(): pl.pallas_call(functools.partial(record_kernel, freqs, first), in_specs=[...  1.02 us
  transfers between devices with their start and end apart: 11, of which 2 were waited for; matrix products, arithmetic and copies ran while one was open for 0% of the time, Pallas kernels for 21%

profile of v10, /device:TPU:1, one launch (start us, length us, event | category | flops | bytes accessed | tf_op | source)
XLA Modules:
  0.0 37.6 jit_solution(1364630781430467766)
XLA Ops:
  0.0 5.2 %collective-permute-start = (bf16[48,512]{1,0:T(8,128)(2,1)}, bf16[48,512]{1,0:T(8,128)(2,1)S(1)}, u32[]{:S(2)}, u32[]{:S(2)}) collective-permute-start(bf16[48,512]{1,0:T(8,128)(2,1)} %refs_1_.1), channel_id=1, source_target_pairs={{0,48},{8,56},{16,32},{24,40},{32,16},{40,24},{48,0},{56,8},{64,11... | collective-permute-start | bytes 147464 | tf_op jit(solution)/shard_map/ppermute | solution.py:288
  5.2 0.0 collective-permute-start.1
  5.2 0.3 collective-permute-start.2
  5.5 2.7 %load.1 = (bf16[48,512]{1,0:T(8,128)(2,1)S(1)}, bf16[3072,200]{1,0:T(8,128)(2,1)S(1)}, bf16[200,768]{1,0:T(8,128)(2,1)S(1)}, bf16[512,768]{1,0:T(8,128)(2,1)S(1)...) custom-call(s32[64,48]{1,0:T(8,128)} %bitcast.5, ...), custom_call_target="tpu_custom_call" | custom-call | tf_op jit(solution)/shard_map/load/pallas_call | solution.py:79
  8.1 0.0 collective-permute-done.refs_1_
  8.1 1.6 %collective-permute-done.1.refs_2_ = bf16[48,512]{1,0:T(8,128)(2,1)S(1)} collective-permute-done((bf16[48,512]{1,0:T(8,128)(2,1)}, bf16[48,512]{1,0:T(8,128)(2,1)S(1)}, u32[]{:S(2)}, u32[]{:S(2)}) %collective-permute-start.1) | collective-permute-done | bytes 49184 | tf_op jit(solution)/shard_map/ppermute | solution.py:288
  9.7 0.0 collective-permute-done.2.refs_3_
  9.7 2.3 %collective-permute-start.7 = (bf16[192,512]{1,0:T(8,128)(2,1)S(1)}, bf16[192,512]{1,0:T(8,128)(2,1)S(1)}, u32[]{:S(2)}, u32[]{:S(2)}) collective-permute-start(bf16[192,512]{1,0:T(8,128)(2,1)S(1)} %join.1.line_ref), channel_id=1, source_target_pairs={{0,128},{8,136},{16,144},{24,152},{32,160},{40,168},{48,176},{56,1... | collective-permute-start | bytes 589832 | tf_op jit(solution)/shard_map/ppermute | solution.py:288
  12.1 0.3 collective-permute-start.3
  12.4 0.7 %collective-permute-start.5 = (bf16[192,512]{1,0:T(8,128)(2,1)S(1)}, bf16[192,512]{1,0:T(8,128)(2,1)S(1)}, u32[]{:S(2)}, u32[]{:S(2)}) collective-permute-start(bf16[192,512]{1,0:T(8,128)(2,1)S(1)} %join.1.line_ref), channel_id=1, source_target_pairs={{0,192},{8,200},{16,208},{24,216},{32,224},{40,232},{48,240},{56,2... | collective-permute-start | bytes 589832 | tf_op jit(solution)/shard_map/ppermute | solution.py:288
  13.1 3.9 %template_spectra.1 = (f32[24576,128]{1,0:T(8,128)S(1)}, bf16[192,512]{1,0:T(8,128)(2,1)S(1)}, f32[12288,128]{1,0:T(8,128)S(1)}) custom-call(s32[64,48]{1,0:T(8,128)S(1)} %get-tuple-element.22.lag_ref, bf16[80,384]{1,0:T(8,128)(2,1)S(1)} %get-tuple-element.23.spread_ref, bf16[192,512]{1,0:T(8,128)(2,1)S(1)} %join.1.line_ref, ...), custom_call_target="tpu_custom_call" | custom-call | flops 943718400 | bytes 12582912 | tf_op jit(solution)/shard_map/template_spectra/pallas_call | solution.py:122
  17.0 2.9 %collective-permute-start.8 = (bf16[192,512]{1,0:T(8,128)(2,1)S(1)}, bf16[192,512]{1,0:T(8,128)(2,1)S(1)}, u32[]{:S(2)}, u32[]{:S(2)}) collective-permute-start(bf16[192,512]{1,0:T(8,128)(2,1)S(1)} %get-tuple-element.28), channel_id=1, source_target_pairs={{0,8},{8,0},{16,24},{24,16},{32,40},{40,32},{48,56},{56,48},{64,72... | collective-permute-start | bytes 589832 | tf_op jit(solution)/shard_map/ppermute | solution.py:288
  19.9 0.0 collective-permute-done.7.refs_0_
  19.9 1.0 %collective-permute-start.9 = (bf16[192,512]{1,0:T(8,128)(2,1)S(1)}, bf16[192,512]{1,0:T(8,128)(2,1)S(1)}, u32[]{:S(2)}, u32[]{:S(2)}) collective-permute-start(bf16[192,512]{1,0:T(8,128)(2,1)S(1)} %collective-permute-done.7.refs_0_), channel_id=1, source_target_pairs={{0,8},{8,0},{16,24},{24,16},{32,40},{40,32},{48,56},{56,48},{64,72... | collective-permute-start | bytes 589832 | tf_op jit(solution)/shard_map/ppermute | solution.py:288
  20.9 0.0 collective-permute-done.3.refs_1_
  20.9 1.6 %collective-permute-start.4 = (bf16[192,512]{1,0:T(8,128)(2,1)S(1)}, bf16[192,512]{1,0:T(8,128)(2,1)S(1)}, u32[]{:S(2)}, u32[]{:S(2)}) collective-permute-start(bf16[192,512]{1,0:T(8,128)(2,1)S(1)} %collective-permute-done.3.refs_1_), channel_id=1, source_target_pairs={{0,8},{8,0},{16,24},{24,16},{32,40},{40,32},{48,56},{56,48},{64,72... | collective-permute-start | bytes 589832 | tf_op jit(solution)/shard_map/ppermute | solution.py:288
  22.5 0.0 collective-permute-done.5.refs_2_
  22.5 0.6 %collective-permute-start.6 = (bf16[192,512]{1,0:T(8,128)(2,1)S(1)}, bf16[192,512]{1,0:T(8,128)(2,1)S(1)}, u32[]{:S(2)}, u32[]{:S(2)}) collective-permute-start(bf16[192,512]{1,0:T(8,128)(2,1)S(1)} %collective-permute-done.5.refs_2_), channel_id=1, source_target_pairs={{0,8},{8,0},{16,24},{24,16},{32,40},{40,32},{48,56},{56,48},{64,72... | collective-permute-start | bytes 589832 | tf_op jit(solution)/shard_map/ppermute | solution.py:288
  23.0 0.0 collective-permute-done.8.refs_3_
  23.0 0.0 collective-permute-done.9.refs_4_
  23.0 1.0 %record_spectra.1.refs_2_ = f32[12288,128]{1,0:T(8,128)S(1)} custom-call(bf16[192,512]{1,0:T(8,128)(2,1)S(1)} %collective-permute-done.7.refs_0_, bf16[192,512]{1,0:T(8,128)(2,1)S(1)} %collective-permute-done.3.refs_1_, bf16[192,512]{1,0:T(8,128)(2,1)S(1)} %collective-permute-done.5.refs_2_, ...), custom_call_target="tpu_custom_call", output_to_operand_aliasing={{}: (6, {})} | custom-call | flops 754974720 | bytes 3932160 | tf_op jit(solution)/shard_map/record_spectra/pallas_call | solution.py:177
  24.1 0.0 collective-permute-done.4.refs_0_
  24.1 0.0 collective-permute-done.6.refs_1_
  24.1 4.2 %detect.1 = (bf16[128,768]{1,0:T(8,128)(2,1)S(1)}, bf16[64,256]{1,0:T(8,128)(2,1)S(1)}, f32[12288,128]{1,0:T(8,128)S(1)}) custom-call(s32[64,48]{1,0:T(8,128)S(1)} %get-tuple-element.20.slots, bf16[192,512]{1,0:T(8,128)(2,1)S(1)} %collective-permute-done.4.refs_0_, ...), custom_call_target="tpu_custom_call", output_to_operand_aliasing={{2}: (3, {})} | custom-call | flops 301989888 | bytes 12582912 | tf_op jit(solution)/shard_map/detect/pallas_call | solution.py:252
  28.3 1.3 %collective-permute-start.10 = (bf16[64,256]{1,0:T(8,128)(2,1)S(1)}, bf16[64,256]{1,0:T(8,128)(2,1)S(1)}, u32[]{:S(2)}, u32[]{:S(2)}) collective-permute-start(bf16[64,256]{1,0:T(8,128)(2,1)S(1)} %get-tuple-element.34), channel_id=1, source_target_pairs={{1,0},{2,1},{3,2},{4,3},{5,4},{6,5},{7,6},{9,8},{10,9},{11,10},{12... | collective-permute-start | bytes 98312 | tf_op jit(solution)/shard_map/ppermute | solution.py:313
  29.6 0.4 %own_window.1 = f32[64,512]{1,0:T(8,128)S(1)} custom-call(bf16[128,768]{1,0:T(8,128)(2,1)S(1)} %get-tuple-element.33.parts_ref, bf16[768,768]{1,0:T(8,128)(2,1)S(1)} %get-tuple-element.31.refs_5_.high_ref, bf16[768,768]{1,0:T(8,128)(2,1)S(1)} %get-tuple-element.32.refs_6_.low_ref), custom_call_target="tpu_custom_call" | custom-call | flops 150994944 | bytes 4194304 | tf_op jit(solution)/shard_map/own_window/pallas_call | solution.py:203
  30.0 6.9 %collective-permute-done.10 = bf16[64,256]{1,0:T(8,128)(2,1)S(1)} collective-permute-done((bf16[64,256]{1,0:T(8,128)(2,1)S(1)}, bf16[64,256]{1,0:T(8,128)(2,1)S(1)}, u32[]{:S(2)}, u32[]{:S(2)}) %collective-permute-start.10) | collective-permute-done | bytes 32800 | tf_op jit(solution)/shard_map/ppermute | solution.py:313
  36.9 0.7 %convert_add_fusion = f32[64,512]{1,0:T(8,128)} fusion(f32[64,512]{1,0:T(8,128)S(1)} %own_window.1, bf16[64,256]{1,0:T(8,128)(2,1)S(1)} %collective-permute-done.10), kind=kLoop, calls=%fused_computation | loop fusion | flops 65536 | bytes 294912 | tf_op jit(solution)/shard_map/add | solution.py:315
  (1 shorter events, 0.0 us)
Async XLA Ops:
  0.0 8.1 %collective-permute-start = (bf16[48,512]{1,0:T(8,128)(2,1)}, bf16[48,512]{1,0:T(8,128)(2,1)S(1)}, u32[]{:S(2)}, u32[]{:S(2)}) collective-permute-start(bf16[48,512]{1,0:T(8,128)(2,1)} %refs_1_.1), channel_id=1, source_target_pairs={{0,48},{8,56},{16,32},{24,40},{32,16},{40,24},{48,0},{56,8},{64,11... | collective-permute-start | bytes 147464 | tf_op jit(solution)/shard_map/ppermute | solution.py:288
  5.2 4.5 %collective-permute-start.1 = (bf16[48,512]{1,0:T(8,128)(2,1)}, bf16[48,512]{1,0:T(8,128)(2,1)S(1)}, u32[]{:S(2)}, u32[]{:S(2)}) collective-permute-start(bf16[48,512]{1,0:T(8,128)(2,1)} %refs_1_.1), channel_id=1, source_target_pairs={{0,16},{8,24},{16,0},{24,8},{32,48},{40,56},{48,32},{56,40},{64,80... | collective-permute-start | bytes 147464 | tf_op jit(solution)/shard_map/ppermute | solution.py:288
  5.2 4.5 %collective-permute-start.2 = (bf16[48,512]{1,0:T(8,128)(2,1)}, bf16[48,512]{1,0:T(8,128)(2,1)S(1)}, u32[]{:S(2)}, u32[]{:S(2)}) collective-permute-start(bf16[48,512]{1,0:T(8,128)(2,1)} %refs_1_.1), channel_id=1, source_target_pairs={{0,32},{8,40},{16,48},{24,56},{32,0},{40,8},{48,16},{56,24},{64,96... | collective-permute-start | bytes 147464 | tf_op jit(solution)/shard_map/ppermute | solution.py:288
  9.7 10.1 %collective-permute-start.7 = (bf16[192,512]{1,0:T(8,128)(2,1)S(1)}, bf16[192,512]{1,0:T(8,128)(2,1)S(1)}, u32[]{:S(2)}, u32[]{:S(2)}) collective-permute-start(bf16[192,512]{1,0:T(8,128)(2,1)S(1)} %join.1.line_ref), channel_id=1, source_target_pairs={{0,128},{8,136},{16,144},{24,152},{32,160},{40,168},{48,176},{56,1... | collective-permute-start | bytes 589832 | tf_op jit(solution)/shard_map/ppermute | solution.py:288
  12.1 8.8 %collective-permute-start.3 = (bf16[192,512]{1,0:T(8,128)(2,1)S(1)}, bf16[192,512]{1,0:T(8,128)(2,1)S(1)}, u32[]{:S(2)}, u32[]{:S(2)}) collective-permute-start(bf16[192,512]{1,0:T(8,128)(2,1)S(1)} %join.1.line_ref), channel_id=1, source_target_pairs={{0,64},{8,72},{16,80},{24,88},{32,96},{40,104},{48,112},{56,120},{... | collective-permute-start | bytes 589832 | tf_op jit(solution)/shard_map/ppermute | solution.py:288
  12.4 10.1 %collective-permute-start.5 = (bf16[192,512]{1,0:T(8,128)(2,1)S(1)}, bf16[192,512]{1,0:T(8,128)(2,1)S(1)}, u32[]{:S(2)}, u32[]{:S(2)}) collective-permute-start(bf16[192,512]{1,0:T(8,128)(2,1)S(1)} %join.1.line_ref), channel_id=1, source_target_pairs={{0,192},{8,200},{16,208},{24,216},{32,224},{40,232},{48,240},{56,2... | collective-permute-start | bytes 589832 | tf_op jit(solution)/shard_map/ppermute | solution.py:288
  17.0 6.1 %collective-permute-start.8 = (bf16[192,512]{1,0:T(8,128)(2,1)S(1)}, bf16[192,512]{1,0:T(8,128)(2,1)S(1)}, u32[]{:S(2)}, u32[]{:S(2)}) collective-permute-start(bf16[192,512]{1,0:T(8,128)(2,1)S(1)} %get-tuple-element.28), channel_id=1, source_target_pairs={{0,8},{8,0},{16,24},{24,16},{32,40},{40,32},{48,56},{56,48},{64,72... | collective-permute-start | bytes 589832 | tf_op jit(solution)/shard_map/ppermute | solution.py:288
  19.9 3.2 %collective-permute-start.9 = (bf16[192,512]{1,0:T(8,128)(2,1)S(1)}, bf16[192,512]{1,0:T(8,128)(2,1)S(1)}, u32[]{:S(2)}, u32[]{:S(2)}) collective-permute-start(bf16[192,512]{1,0:T(8,128)(2,1)S(1)} %collective-permute-done.7.refs_0_), channel_id=1, source_target_pairs={{0,8},{8,0},{16,24},{24,16},{32,40},{40,32},{48,56},{56,48},{64,72... | collective-permute-start | bytes 589832 | tf_op jit(solution)/shard_map/ppermute | solution.py:288
  20.9 3.2 %collective-permute-start.4 = (bf16[192,512]{1,0:T(8,128)(2,1)S(1)}, bf16[192,512]{1,0:T(8,128)(2,1)S(1)}, u32[]{:S(2)}, u32[]{:S(2)}) collective-permute-start(bf16[192,512]{1,0:T(8,128)(2,1)S(1)} %collective-permute-done.3.refs_1_), channel_id=1, source_target_pairs={{0,8},{8,0},{16,24},{24,16},{32,40},{40,32},{48,56},{56,48},{64,72... | collective-permute-start | bytes 589832 | tf_op jit(solution)/shard_map/ppermute | solution.py:288
  22.5 1.6 %collective-permute-start.6 = (bf16[192,512]{1,0:T(8,128)(2,1)S(1)}, bf16[192,512]{1,0:T(8,128)(2,1)S(1)}, u32[]{:S(2)}, u32[]{:S(2)}) collective-permute-start(bf16[192,512]{1,0:T(8,128)(2,1)S(1)} %collective-permute-done.5.refs_2_), channel_id=1, source_target_pairs={{0,8},{8,0},{16,24},{24,16},{32,40},{40,32},{48,56},{56,48},{64,72... | collective-permute-start | bytes 589832 | tf_op jit(solution)/shard_map/ppermute | solution.py:288
  28.3 8.6 %collective-permute-start.10 = (bf16[64,256]{1,0:T(8,128)(2,1)S(1)}, bf16[64,256]{1,0:T(8,128)(2,1)S(1)}, u32[]{:S(2)}, u32[]{:S(2)}) collective-permute-start(bf16[64,256]{1,0:T(8,128)(2,1)S(1)} %get-tuple-element.34), channel_id=1, source_target_pairs={{1,0},{2,1},{3,2},{4,3},{5,4},{6,5},{7,6},{9,8},{10,9},{11,10},{12... | collective-permute-start | bytes 98312 | tf_op jit(solution)/shard_map/ppermute | solution.py:313
